TPU v7x, 256 devices: a whole 4x4x8 slice. The times are simulated.
256 devices in a mesh: tiles: 64 (over z, x, core), rep: 4 (over y).
Axes of the slice: x: 4, y: 4, z: 8, core: 2. Of those that a mesh axis runs over, the one named last changes fastest.
Arguments:
- affinity: bfloat16 [1024, 512, 512], P(('tiles', 'rep')), may hold values from -0.25 to 0.25
- tile_pairs: int32 [1024, 2], P(('tiles', 'rep')), may hold values from 0 to 255, as said below
- factors: float32 [256, 512, 256], P('tiles'), may hold values from -6 to 6
Outputs:
- polar_factors: float32 [256, 512, 256], P('tiles')
Inputs may be any that keep to these rules, and one draw needn't show every extreme that they name: `tile_pairs`: column 0 of a row is an image owned by the index of tiles that holds the row (images o * 4 to (o + 1) * 4 - 1 belong to index o); column 1 differs from column 0 by 1 to 4, and by exactly 4 in the first row held by every index of tiles.
All inputs are finite; a program needn't handle non-finite values.
Results may differ from a plain program's by a relative error of at most 0.0022.
Values may be sent and summed in bfloat16 or wider, within the bound.
No kernel may reach another device: no remote copies, remote signals or barrier semaphores. Data moves between devices by JAX's collectives and lax.ppermute only.
A program may use at most 64 MiB of HBM per device.

v0:
```python
import functools
import math

import jax
import jax.numpy as jnp
from jax import lax
from jax.experimental import pallas as pl
from jax.experimental.pallas import tpu as pltpu
from jax.sharding import PartitionSpec as P


P_SIZE = 512
NS_STEPS = 6
WIDE_STEPS = 1

epsilon = 1e-06
start_scale = 0.25
ascent_step = 0.25


SMEM = pl.BlockSpec(memory_space=pltpu.SMEM)
VMEM = pl.BlockSpec(memory_space=pltpu.VMEM)
MIB = 1 << 20


def mate(x):
    n = lax.axis_size("tiles")
    return lax.ppermute(x, "tiles", [(i, i ^ 1) for i in range(n)])


def across(x):
    n = lax.axis_size("tiles")
    pairs = [(i, i + 1) for i in range(1, n - 1, 2)]
    return lax.ppermute(x, "tiles", pairs + [(b, a) for a, b in pairs])


def turned(x, by):
    n = lax.axis_size("rep")
    return lax.ppermute(x, "rep", [(i, (i + by) % n) for i in range(n)])


def dot(a, b, dims=((1,), (0,))):
    return lax.dot_general(a, b, (dims, ((), ())), preferred_element_type=jnp.float32)


TN = ((0,), (0,))
NT = ((1,), (1,))


def accumulate(acc, slot, fresh, term):
    acc[slot] = jnp.where(fresh, jnp.zeros_like(term), acc[slot]) + term


def backward_kernel(meta, affinity, rounded, own, to_mate, c0, c1, c2, c3, acc):
    tiles = affinity.shape[0]
    images = rounded.shape[0]
    slots = [meta[tiles + t] for t in range(tiles)]
    for t in range(tiles):
        fresh = slots[t] >= 0
        for u in range(t):
            fresh = jnp.logical_and(fresh, slots[u] != slots[t])
        accumulate(acc, slots[t], fresh, dot(affinity[t], rounded[meta[t]], TN))

    def total(slot):
        hit = slots[0] == slot
        for t in range(1, tiles):
            hit = jnp.logical_or(hit, slots[t] == slot)
        value = acc[slot]
        return jnp.where(hit, value, jnp.zeros_like(value))

    for k, ref in enumerate((c0, c1, c2, c3)):
        ref[...] = total(meta[2 * tiles + k]).astype(ref.dtype)
    for j in range(images):
        to_mate[j] = total(2 * images + j).astype(to_mate.dtype)
    for j in range(images):
        own[j] = total(images + j)


def forward_kernel(meta, affinity, rounded, from_mate, from_across, own, terms, p0, p1, p2, p3, rhs, acc):
    tiles = affinity.shape[0]
    images = rounded.shape[0]
    for j in range(images):
        acc[j] = own[j] + terms[j].astype(jnp.float32)
    for t in range(tiles):
        slot = meta[tiles + t]

        @pl.when(slot < images)
        def _():
            rhs[...] = from_across[slot]

        @pl.when(jnp.logical_and(slot >= images, slot < 2 * images))
        def _():
            rhs[...] = rounded[slot - images]

        @pl.when(slot >= 2 * images)
        def _():
            rhs[...] = from_mate[slot - 2 * images]

        first = meta[t]
        acc[first] = acc[first] + dot(affinity[t], rhs[...])
    for k, ref in enumerate((p0, p1, p2, p3)):
        ref[...] = acc[meta[2 * tiles + k]].astype(ref.dtype)


def split(x):
    high = x.astype(jnp.bfloat16)
    return high, (x - high.astype(jnp.float32)).astype(jnp.bfloat16)


def project_kernel(places, meta, factors, *rest):
    count = len(places)
    gradients = rest[:count]
    out, held, sems = rest[-3:]
    ys = []
    for place, gradient in zip(places, gradients):
        x = factors[meta[place]] + ascent_step * gradient[...].astype(jnp.float32)
        squares = jnp.sum(jnp.sum(x * x, axis=0, keepdims=True), axis=1, keepdims=True)
        x = x * (start_scale * math.sqrt(x.shape[1]) * lax.rsqrt(squares + epsilon))
        ys.append(x.T)
    for step in range(NS_STEPS):
        if step < NS_STEPS - WIDE_STEPS:
            highs = [y.astype(jnp.bfloat16) for y in ys]
            grams = [dot(h, h, NT).astype(jnp.bfloat16) for h in highs]
            changes = [dot(g, h) for g, h in zip(grams, highs)]
        else:
            halves = [split(y) for y in ys]
            mixed = [dot(high, low, NT) for high, low in halves]
            grams = [split(dot(high, high, NT) + (m + m.T)) for (high, low), m in zip(halves, mixed)]
            changes = [
                dot(gh, high) + (dot(gl, high) + dot(gh, low))
                for (gh, gl), (high, low) in zip(grams, halves)
            ]
        ys = [1.5 * y - 0.5 * c for y, c in zip(ys, changes)]
    copies = []
    for k, (place, y) in enumerate(zip(places, ys)):
        held[k] = (y * math.sqrt(P_SIZE)).T
        copies.append(pltpu.make_async_copy(held.at[k], out.at[meta[place]], sems.at[k]))
        copies[-1].start()
    for copy in copies:
        copy.wait()


def project(places, meta, factors, gradients, result=None):
    _, keypoints, universe = factors.shape
    count = len(places)
    in_specs = [SMEM, VMEM] + [VMEM] * count
    operands = [meta, factors, *gradients]
    aliases = {}
    if result is not None:
        aliases = {len(operands): 0}
        in_specs.append(pl.BlockSpec(memory_space=pl.ANY))
        operands.append(result)
    return pl.pallas_call(
        functools.partial(project_kernel, places),
        out_shape=jax.ShapeDtypeStruct(factors.shape, jnp.float32),
        in_specs=in_specs,
        out_specs=pl.BlockSpec(memory_space=pl.ANY),
        scratch_shapes=[
            pltpu.VMEM((count, keypoints, universe), jnp.float32),
            pltpu.SemaphoreType.DMA((count,)),
        ],
        input_output_aliases=aliases,
        compiler_params=pltpu.CompilerParams(vmem_limit_bytes=16 * MIB),
        cost_estimate=pl.CostEstimate(flops=count * 2000000000, bytes_accessed=count * 2000000, transcendentals=0),
        name="project",
    )(*operands)


def shards(affinity, tile_pairs, factors):
    images, keypoints, universe = factors.shape
    tiles = affinity.shape[0]
    owner = lax.axis_index("tiles")
    turn = lax.axis_index("rep")
    first = tile_pairs[:, 0] - owner * images
    slot = tile_pairs[:, 1] - (owner - 1) * images
    swapped = jnp.where(slot < images, slot + 2 * images, jnp.where(slot < 2 * images, slot, slot - 2 * images))
    slot = jnp.where(owner % 2 == 0, slot, swapped)
    order = (turn + jnp.arange(images, dtype=jnp.int32)) % images
    meta = jnp.concatenate([first, slot, order]).astype(jnp.int32)

    rounded = factors.astype(jnp.bfloat16)
    rounded, meta = lax.optimization_barrier((rounded, meta))
    from_across = across(rounded)

    wide = jax.ShapeDtypeStruct((images, keypoints, universe), jnp.float32)
    narrow = jax.ShapeDtypeStruct((images, keypoints, universe), jnp.bfloat16)
    one_wide = jax.ShapeDtypeStruct((keypoints, universe), jnp.float32)
    one = jax.ShapeDtypeStruct((keypoints, universe), jnp.bfloat16)

    own, to_mate, c0, c1, c2, c3 = pl.pallas_call(
        backward_kernel,
        out_shape=(wide, narrow, one_wide, one, one, one),
        in_specs=[SMEM, VMEM, VMEM],
        out_specs=(VMEM,) * 6,
        scratch_shapes=[pltpu.VMEM((3 * images, keypoints, universe), jnp.float32)],
        compiler_params=pltpu.CompilerParams(vmem_limit_bytes=12 * MIB),
        cost_estimate=pl.CostEstimate(flops=600000000, bytes_accessed=8000000, transcendentals=0),
        name="backward",
    )(meta, affinity, rounded)
    x1 = turned(c1, 1)
    x3 = turned(c3, -1)
    x2 = turned(c2, 2)
    from_mate = mate(rounded)
    terms = mate(to_mate)
    p0, p1, p2, p3 = pl.pallas_call(
        forward_kernel,
        out_shape=(one_wide, one, one, one),
        in_specs=[SMEM] + [VMEM] * 6,
        out_specs=(VMEM,) * 4,
        scratch_shapes=[
            pltpu.VMEM((keypoints, universe), jnp.bfloat16),
            pltpu.VMEM((images, keypoints, universe), jnp.float32),
        ],
        compiler_params=pltpu.CompilerParams(vmem_limit_bytes=12 * MIB),
        cost_estimate=pl.CostEstimate(flops=600000000, bytes_accessed=8000000, transcendentals=0),
        name="forward",
    )(meta, affinity, rounded, from_mate, from_across, own, terms)
    crossing = c0 + x1.astype(jnp.float32) + x2.astype(jnp.float32) + x3.astype(jnp.float32)
    crossed = across(crossing.astype(jnp.bfloat16))
    y1 = turned(p1, 1)
    y3 = turned(p3, -1)
    y2 = turned(p2, 2)
    gradient = p0 + y1.astype(jnp.float32) + y2.astype(jnp.float32) + y3.astype(jnp.float32) + crossed.astype(jnp.float32)
    gradient = gradient.astype(jnp.bfloat16)
    z1 = turned(gradient, 1)
    z3 = turned(gradient, -1)
    z2 = turned(gradient, 2)
    own_place = 2 * tiles
    result = project((own_place,), meta, factors, (gradient,))
    result = project((own_place + 3, own_place + 1), meta, factors, (z1, z3), result)
    result = project((own_place + 2,), meta, factors, (z2,), result)
    return result


def solution(mesh):
    in_specs = (P(("tiles", "rep"), None, None), P(("tiles", "rep"), None), P("tiles", None, None))
    out_specs = P("tiles", None, None)

    def step(*arguments):
        return shards(*arguments)

    step = jax.shard_map(step, mesh=mesh, in_specs=in_specs, out_specs=out_specs, check_vma=False)
    return step
```

profile of v0, /device:TPU:103, one launch (start us, length us, event | category | flops | bytes accessed | tf_op | source)
XLA Modules:
  0.0 79.3 jit_solution(10363367732952800515)
XLA Ops:
  0.0 0.0 copy-start.2
  0.0 0.0 copy-start
  0.0 1.8 %convert_element_type.30.rounded = bf16[4,512,256]{2,1,0:T(8,128)(2,1)S(1)} convert(f32[4,512,256]{2,1,0:T(8,128)} %factors.5) | non-fusion elementwise | flops 524288 | bytes 3145728 | tf_op jit(solution)/shard_map/convert_element_type | solution.py:181
  1.9 0.0 copy-done.2
  1.9 0.1 pad_add_fusion.meta
  2.0 0.7 collective-permute-start
  2.7 4.6 %collective-permute-start.1 = (bf16[4,512,256]{2,1,0:T(8,128)(2,1)S(1)}, bf16[4,512,256]{2,1,0:T(8,128)(2,1)S(1)}, u32[]{:S(2)}, u32[]{:S(2)}) collective-permute-start(bf16[4,512,256]{2,1,0:T(8,128)(2,1)S(1)} %convert_element_type.30.rounded), channel_id=1, source_target_pairs={{4,8},{12,16},{20,24},{28,32},{36,40},{44,48},{52,56},{60,64},{68,... | collective-permute-start | bytes 3145736 | tf_op jit(solution)/shard_map/ppermute | solution.py:34
  7.3 0.0 copy-done
  7.3 1.8 %backward.1 = (f32[4,512,256]{2,1,0:T(8,128)S(1)}, bf16[4,512,256]{2,1,0:T(8,128)(2,1)S(1)}, f32[512,256]{1,0:T(8,128)S(1)}, bf16[512,256]{1,0:T(8,128)(2,1)S(1)...) custom-call(s32[12]{0:T(128)S(1)} %pad_add_fusion.meta, bf16[4,512,512]{2,1,0:T(8,128)(2,1)S(1)} %copy-done, ...), custom_call_target="tpu_custom_call" | custom-call | flops 600000000 | bytes 8000000 | tf_op jit(solution)/shard_map/backward/pallas_call | solution.py:190
  9.1 0.1 collective-permute-start.2
  9.2 2.8 %collective-permute-start.8 = (bf16[512,256]{1,0:T(8,128)(2,1)S(1)}, bf16[512,256]{1,0:T(8,128)(2,1)S(1)}, u32[]{:S(2)}, u32[]{:S(2)}) collective-permute-start(bf16[512,256]{1,0:T(8,128)(2,1)S(1)} %get-tuple-element.28), channel_id=1, source_target_pairs={{0,3},{1,0},{2,1},{3,2},{4,7},{5,4},{6,5},{7,6},{8,11},{9,8},{10,9... | collective-permute-start | bytes 786440 | tf_op jit(solution)/shard_map/ppermute | solution.py:39
  12.0 0.4 collective-permute-start.7
  12.3 10.4 %collective-permute-done.8 = bf16[512,256]{1,0:T(8,128)(2,1)S(1)} collective-permute-done((bf16[512,256]{1,0:T(8,128)(2,1)S(1)}, bf16[512,256]{1,0:T(8,128)(2,1)S(1)}, u32[]{:S(2)}, u32[]{:S(2)}) %collective-permute-start.8) | collective-permute-done | bytes 262176 | tf_op jit(solution)/shard_map/ppermute | solution.py:39
  22.7 0.0 collective-permute-start.6
  22.7 0.0 collective-permute-done.7
  22.7 9.0 %collective-permute-done.6 = bf16[512,256]{1,0:T(8,128)(2,1)S(1)} collective-permute-done((bf16[512,256]{1,0:T(8,128)(2,1)S(1)}, bf16[512,256]{1,0:T(8,128)(2,1)S(1)}, u32[]{:S(2)}, u32[]{:S(2)}) %collective-permute-start.6) | collective-permute-done | bytes 262176 | tf_op jit(solution)/shard_map/ppermute | solution.py:39
  31.7 0.1 add_convert_fusion.1
  31.8 6.4 %collective-permute-start.9 = (bf16[512,256]{1,0:T(8,128)(2,1)S(1)}, bf16[512,256]{1,0:T(8,128)(2,1)S(1)}, u32[]{:S(2)}, u32[]{:S(2)}) collective-permute-start(bf16[512,256]{1,0:T(8,128)(2,1)S(1)} %add_convert_fusion.1), channel_id=1, source_target_pairs={{4,8},{12,16},{20,24},{28,32},{36,40},{44,48},{52,56},{60,64},{68,... | collective-permute-start | bytes 786440 | tf_op jit(solution)/shard_map/ppermute | solution.py:34
  38.2 0.0 collective-permute-done.from_mate
  38.2 0.0 collective-permute-done.1.from_across
  38.2 0.0 collective-permute-done.2.terms
  38.2 0.0 copy-start.1
  38.2 2.6 %forward.1 = (f32[512,256]{1,0:T(8,128)S(1)}, bf16[512,256]{1,0:T(8,128)(2,1)S(1)}, bf16[512,256]{1,0:T(8,128)(2,1)S(1)}, bf16[512,256]{1,0:T(8,128)(2,1)S(1)}) custom-call(s32[12]{0:T(128)S(1)} %pad_add_fusion.meta, bf16[4,512,512]{2,1,0:T(8,128)(2,1)S(1)} %copy-done, bf16[4,512,256]{2,1,0:T(8,128)(2,1)S(1)} %convert_element_type.30.rounded, ...), custom_call_target="tpu_custom_call" | custom-call | flops 600000000 | bytes 8000000 | tf_op jit(solution)/shard_map/forward/pallas_call | solution.py:205
  40.9 1.5 %collective-permute-start.5 = (bf16[512,256]{1,0:T(8,128)(2,1)S(1)}, bf16[512,256]{1,0:T(8,128)(2,1)S(1)}, u32[]{:S(2)}, u32[]{:S(2)}) collective-permute-start(bf16[512,256]{1,0:T(8,128)(2,1)S(1)} %get-tuple-element.24), channel_id=1, source_target_pairs={{0,3},{1,0},{2,1},{3,2},{4,7},{5,4},{6,5},{7,6},{8,11},{9,8},{10,9... | collective-permute-start | bytes 786440 | tf_op jit(solution)/shard_map/ppermute | solution.py:39
  42.4 0.0 collective-permute-start.4
  42.4 0.7 collective-permute-start.3
  43.1 0.0 collective-permute-done.9
  43.1 6.2 %collective-permute-done.5 = bf16[512,256]{1,0:T(8,128)(2,1)S(1)} collective-permute-done((bf16[512,256]{1,0:T(8,128)(2,1)S(1)}, bf16[512,256]{1,0:T(8,128)(2,1)S(1)}, u32[]{:S(2)}, u32[]{:S(2)}) %collective-permute-start.5) | collective-permute-done | bytes 262176 | tf_op jit(solution)/shard_map/ppermute | solution.py:39
  49.3 2.7 %collective-permute-done.4 = bf16[512,256]{1,0:T(8,128)(2,1)S(1)} collective-permute-done((bf16[512,256]{1,0:T(8,128)(2,1)S(1)}, bf16[512,256]{1,0:T(8,128)(2,1)S(1)}, u32[]{:S(2)}, u32[]{:S(2)}) %collective-permute-start.4) | collective-permute-done | bytes 262176 | tf_op jit(solution)/shard_map/ppermute | solution.py:39
  52.0 3.4 %collective-permute-done.3 = bf16[512,256]{1,0:T(8,128)(2,1)S(1)} collective-permute-done((bf16[512,256]{1,0:T(8,128)(2,1)S(1)}, bf16[512,256]{1,0:T(8,128)(2,1)S(1)}, u32[]{:S(2)}, u32[]{:S(2)}) %collective-permute-start.3) | collective-permute-done | bytes 262176 | tf_op jit(solution)/shard_map/ppermute | solution.py:39
  55.4 0.2 add_convert_fusion.rest_0_
  55.6 0.1 collective-permute-start.11
  55.7 2.7 %collective-permute-start.12 = (bf16[512,256]{1,0:T(8,128)(2,1)S(1)}, bf16[512,256]{1,0:T(8,128)(2,1)S(1)}, u32[]{:S(2)}, u32[]{:S(2)}) collective-permute-start(bf16[512,256]{1,0:T(8,128)(2,1)S(1)} %add_convert_fusion.rest_0_), channel_id=1, source_target_pairs={{0,3},{1,0},{2,1},{3,2},{4,7},{5,4},{6,5},{7,6},{8,11},{9,8},{10,9... | collective-permute-start | bytes 786440 | tf_op jit(solution)/shard_map/ppermute | solution.py:39
  58.3 0.0 collective-permute-start.10
  58.3 0.0 copy-done.1
  58.3 4.4 %project.3.rest_2_ = f32[4,512,256]{2,1,0:T(8,128)} custom-call(s32[12]{0:T(128)S(1)} %pad_add_fusion.meta, f32[4,512,256]{2,1,0:T(8,128)S(1)} %copy-done.1, bf16[512,256]{1,0:T(8,128)(2,1)S(1)} %add_convert_fusion.rest_0_), custom_call_target="tpu_custom_call" | custom-call | flops 2000000000 | bytes 2000000 | tf_op jit(solution)/shard_map/project/pallas_call | solution.py:153
  62.7 7.3 %collective-permute-done.11.rest_0_ = bf16[512,256]{1,0:T(8,128)(2,1)S(1)} collective-permute-done((bf16[512,256]{1,0:T(8,128)(2,1)S(1)}, bf16[512,256]{1,0:T(8,128)(2,1)S(1)}, u32[]{:S(2)}, u32[]{:S(2)}) %collective-permute-start.11) | collective-permute-done | bytes 262176 | tf_op jit(solution)/shard_map/ppermute | solution.py:39
  70.0 0.0 collective-permute-done.12.rest_1_
  70.0 4.7 %project.4.rest_1_ = f32[4,512,256]{2,1,0:T(8,128)} custom-call(s32[12]{0:T(128)S(1)} %pad_add_fusion.meta, f32[4,512,256]{2,1,0:T(8,128)S(1)} %copy-done.1, bf16[512,256]{1,0:T(8,128)(2,1)S(1)} %collective-permute-done.11.rest_0_, bf16[512,256]{1,0:T(8,128)(2,1)S(1)} %collective-permute-done.12.rest_1_, ...), custom_call_target="tpu_custom_call", output_to_operand_aliasing={{}: (4, {})} | custom-call | flops 4000000000 | bytes 4000000 | tf_op jit(solution)/shard_map/project/pallas_call | solution.py:153
  74.8 0.0 collective-permute-done.10.rest_0_
  74.8 4.4 %project.5 = f32[4,512,256]{2,1,0:T(8,128)} custom-call(s32[12]{0:T(128)S(1)} %pad_add_fusion.meta, f32[4,512,256]{2,1,0:T(8,128)S(1)} %copy-done.1, bf16[512,256]{1,0:T(8,128)(2,1)S(1)} %collective-permute-done.10.rest_0_, f32[4,512,256]{2,1,0:T(8,128)} %project.4.rest_1_), custom_call_target="tpu_custom_call", output_to_operand_aliasing={{}: (3, {})} | custom-call | flops 2000000000 | bytes 2000000 | tf_op jit(solution)/shard_map/project/pallas_call | solution.py:153
  (2 shorter events, 0.0 us)
Async XLA Ops:
  0.0 1.9 %copy-start.2 = (s32[4,2]{0,1:T(2,128)S(1)}, s32[4,2]{0,1:T(2,128)}, u32[]{:S(2)}) copy-start(s32[4,2]{0,1:T(2,128)} %param.4) | copy-start | bytes 100
  0.0 7.3 %copy-start = (bf16[4,512,512]{2,1,0:T(8,128)(2,1)S(1)}, bf16[4,512,512]{2,1,0:T(8,128)(2,1)}, u32[]{:S(2)}) copy-start(bf16[4,512,512]{2,1,0:T(8,128)(2,1)} %affinity.3) | copy-start | bytes 6291460
  2.0 36.2 %collective-permute-start = (bf16[4,512,256]{2,1,0:T(8,128)(2,1)S(1)}, bf16[4,512,256]{2,1,0:T(8,128)(2,1)S(1)}, u32[]{:S(2)}, u32[]{:S(2)}) collective-permute-start(bf16[4,512,256]{2,1,0:T(8,128)(2,1)S(1)} %convert_element_type.30.rounded), channel_id=1, source_target_pairs={{0,4},{4,0},{8,12},{12,8},{16,20},{20,16},{24,28},{28,24},{32,36},... | collective-permute-start | bytes 3145736 | tf_op jit(solution)/shard_map/ppermute | solution.py:28
  2.7 35.5 %collective-permute-start.1 = (bf16[4,512,256]{2,1,0:T(8,128)(2,1)S(1)}, bf16[4,512,256]{2,1,0:T(8,128)(2,1)S(1)}, u32[]{:S(2)}, u32[]{:S(2)}) collective-permute-start(bf16[4,512,256]{2,1,0:T(8,128)(2,1)S(1)} %convert_element_type.30.rounded), channel_id=1, source_target_pairs={{4,8},{12,16},{20,24},{28,32},{36,40},{44,48},{52,56},{60,64},{68,... | collective-permute-start | bytes 3145736 | tf_op jit(solution)/shard_map/ppermute | solution.py:34
  9.1 29.1 %collective-permute-start.2 = (bf16[4,512,256]{2,1,0:T(8,128)(2,1)S(1)}, bf16[4,512,256]{2,1,0:T(8,128)(2,1)S(1)}, u32[]{:S(2)}, u32[]{:S(2)}) collective-permute-start(bf16[4,512,256]{2,1,0:T(8,128)(2,1)S(1)} %get-tuple-element.20), channel_id=1, source_target_pairs={{0,4},{4,0},{8,12},{12,8},{16,20},{20,16},{24,28},{28,24},{32,36},... | collective-permute-start | bytes 3145736 | tf_op jit(solution)/shard_map/ppermute | solution.py:28
  9.2 13.5 %collective-permute-start.8 = (bf16[512,256]{1,0:T(8,128)(2,1)S(1)}, bf16[512,256]{1,0:T(8,128)(2,1)S(1)}, u32[]{:S(2)}, u32[]{:S(2)}) collective-permute-start(bf16[512,256]{1,0:T(8,128)(2,1)S(1)} %get-tuple-element.28), channel_id=1, source_target_pairs={{0,3},{1,0},{2,1},{3,2},{4,7},{5,4},{6,5},{7,6},{8,11},{9,8},{10,9... | collective-permute-start | bytes 786440 | tf_op jit(solution)/shard_map/ppermute | solution.py:39
  12.0 10.7 %collective-permute-start.7 = (bf16[512,256]{1,0:T(8,128)(2,1)S(1)}, bf16[512,256]{1,0:T(8,128)(2,1)S(1)}, u32[]{:S(2)}, u32[]{:S(2)}) collective-permute-start(bf16[512,256]{1,0:T(8,128)(2,1)S(1)} %get-tuple-element.27), channel_id=1, source_target_pairs={{0,2},{1,3},{2,0},{3,1},{4,6},{5,7},{6,4},{7,5},{8,10},{9,11},{10,... | collective-permute-start | bytes 786440 | tf_op jit(solution)/shard_map/ppermute | solution.py:39
  22.7 9.0 %collective-permute-start.6 = (bf16[512,256]{1,0:T(8,128)(2,1)S(1)}, bf16[512,256]{1,0:T(8,128)(2,1)S(1)}, u32[]{:S(2)}, u32[]{:S(2)}) collective-permute-start(bf16[512,256]{1,0:T(8,128)(2,1)S(1)} %get-tuple-element.26), channel_id=1, source_target_pairs={{0,1},{1,2},{2,3},{3,0},{4,5},{5,6},{6,7},{7,4},{8,9},{9,10},{10,1... | collective-permute-start | bytes 786440 | tf_op jit(solution)/shard_map/ppermute | solution.py:39
  31.8 11.3 %collective-permute-start.9 = (bf16[512,256]{1,0:T(8,128)(2,1)S(1)}, bf16[512,256]{1,0:T(8,128)(2,1)S(1)}, u32[]{:S(2)}, u32[]{:S(2)}) collective-permute-start(bf16[512,256]{1,0:T(8,128)(2,1)S(1)} %add_convert_fusion.1), channel_id=1, source_target_pairs={{4,8},{12,16},{20,24},{28,32},{36,40},{44,48},{52,56},{60,64},{68,... | collective-permute-start | bytes 786440 | tf_op jit(solution)/shard_map/ppermute | solution.py:34
  38.2 20.1 %copy-start.1 = (f32[4,512,256]{2,1,0:T(8,128)S(1)}, f32[4,512,256]{2,1,0:T(8,128)}, u32[]{:S(2)}) copy-start(f32[4,512,256]{2,1,0:T(8,128)} %factors.5) | copy-start | bytes 6291460
  40.9 8.4 %collective-permute-start.5 = (bf16[512,256]{1,0:T(8,128)(2,1)S(1)}, bf16[512,256]{1,0:T(8,128)(2,1)S(1)}, u32[]{:S(2)}, u32[]{:S(2)}) collective-permute-start(bf16[512,256]{1,0:T(8,128)(2,1)S(1)} %get-tuple-element.24), channel_id=1, source_target_pairs={{0,3},{1,0},{2,1},{3,2},{4,7},{5,4},{6,5},{7,6},{8,11},{9,8},{10,9... | collective-permute-start | bytes 786440 | tf_op jit(solution)/shard_map/ppermute | solution.py:39
  42.4 9.5 %collective-permute-start.4 = (bf16[512,256]{1,0:T(8,128)(2,1)S(1)}, bf16[512,256]{1,0:T(8,128)(2,1)S(1)}, u32[]{:S(2)}, u32[]{:S(2)}) collective-permute-start(bf16[512,256]{1,0:T(8,128)(2,1)S(1)} %get-tuple-element.23), channel_id=1, source_target_pairs={{0,2},{1,3},{2,0},{3,1},{4,6},{5,7},{6,4},{7,5},{8,10},{9,11},{10,... | collective-permute-start | bytes 786440 | tf_op jit(solution)/shard_map/ppermute | solution.py:39
  42.4 13.0 %collective-permute-start.3 = (bf16[512,256]{1,0:T(8,128)(2,1)S(1)}, bf16[512,256]{1,0:T(8,128)(2,1)S(1)}, u32[]{:S(2)}, u32[]{:S(2)}) collective-permute-start(bf16[512,256]{1,0:T(8,128)(2,1)S(1)} %get-tuple-element.22), channel_id=1, source_target_pairs={{0,1},{1,2},{2,3},{3,0},{4,5},{5,6},{6,7},{7,4},{8,9},{9,10},{10,1... | collective-permute-start | bytes 786440 | tf_op jit(solution)/shard_map/ppermute | solution.py:39
  55.6 14.5 %collective-permute-start.11 = (bf16[512,256]{1,0:T(8,128)(2,1)S(1)}, bf16[512,256]{1,0:T(8,128)(2,1)S(1)}, u32[]{:S(2)}, u32[]{:S(2)}) collective-permute-start(bf16[512,256]{1,0:T(8,128)(2,1)S(1)} %add_convert_fusion.rest_0_), channel_id=1, source_target_pairs={{0,1},{1,2},{2,3},{3,0},{4,5},{5,6},{6,7},{7,4},{8,9},{9,10},{10,1... | collective-permute-start | bytes 786440 | tf_op jit(solution)/shard_map/ppermute | solution.py:39
  55.7 14.4 %collective-permute-start.12 = (bf16[512,256]{1,0:T(8,128)(2,1)S(1)}, bf16[512,256]{1,0:T(8,128)(2,1)S(1)}, u32[]{:S(2)}, u32[]{:S(2)}) collective-permute-start(bf16[512,256]{1,0:T(8,128)(2,1)S(1)} %add_convert_fusion.rest_0_), channel_id=1, source_target_pairs={{0,3},{1,0},{2,1},{3,2},{4,7},{5,4},{6,5},{7,6},{8,11},{9,8},{10,9... | collective-permute-start | bytes 786440 | tf_op jit(solution)/shard_map/ppermute | solution.py:39
  58.3 16.4 %collective-permute-start.10 = (bf16[512,256]{1,0:T(8,128)(2,1)S(1)}, bf16[512,256]{1,0:T(8,128)(2,1)S(1)}, u32[]{:S(2)}, u32[]{:S(2)}) collective-permute-start(bf16[512,256]{1,0:T(8,128)(2,1)S(1)} %add_convert_fusion.rest_0_), channel_id=1, source_target_pairs={{0,2},{1,3},{2,0},{3,1},{4,6},{5,7},{6,4},{7,5},{8,10},{9,11},{10,... | collective-permute-start | bytes 786440 | tf_op jit(solution)/shard_map/ppermute | solution.py:39
where the time goes:
time: 79.9 us; the launch traced here: 79.3 us
  waiting for transfers between devices  39 us (49%)
  starting transfers between devices  19.9 us (25%)
  Pallas kernels  17.9 us (22%)
  other arithmetic  2.23 us (3%)
    ppermute x9, waiting for transfers between devices, turned(): return lax.ppermute(x, 'rep', [(i, (i + by) % n) for i in range(n)])  39 us
    pallas_call x3, Pallas kernels, project(): pl.pallas_call(functools.partial(project_kernel, places), out_shape=jax.S...  13.4 us
    ppermute x2, starting transfers between devices, across(): return lax.ppermute(x, 'tiles', pairs + [(b, a) for a, b in pairs])  11 us
    ppermute x9, starting transfers between devices, turned(): return lax.ppermute(x, 'rep', [(i, (i + by) % n) for i in range(n)])  8.13 us
    pallas_call x1, Pallas kernels, shards(): pl.pallas_call(forward_kernel, out_shape=(one_wide, one, one, one), in_sp...  2.64 us
    convert_element_type x1, other arithmetic, shards(): rounded = factors.astype(jnp.bfloat16)  1.84 us
    pallas_call x1, Pallas kernels, shards(): pl.pallas_call(backward_kernel, out_shape=(wide, narrow, one_wide, one, o...  1.79 us
  transfers between devices with their start and end apart: 13, of which 6 were waited for; matrix products, arithmetic and copies ran while one was open for 0% of the time, Pallas kernels for 17%

commit v1 on v0

--- a/solution.py
+++ b/solution.py
@@ -47,19 +47,18 @@
 NT = ((1,), (1,))
 
 
-def accumulate(acc, slot, fresh, term):
-    acc[slot] = jnp.where(fresh, jnp.zeros_like(term), acc[slot]) + term
-
-
-def backward_kernel(meta, affinity, rounded, own, to_mate, c0, c1, c2, c3, acc):
+def backward_kernel(meta, affinity, left, right, own_left, own_right, to_mate, c0, c1, c2, c3, acc):
     tiles = affinity.shape[0]
-    images = rounded.shape[0]
+    images = left.shape[0]
+    half = left.shape[2]
     slots = [meta[tiles + t] for t in range(tiles)]
     for t in range(tiles):
         fresh = slots[t] >= 0
         for u in range(t):
             fresh = jnp.logical_and(fresh, slots[u] != slots[t])
-        accumulate(acc, slots[t], fresh, dot(affinity[t], rounded[meta[t]], TN))
+        first = jnp.concatenate([left[meta[t]], right[meta[t]]], axis=1)
+        term = dot(affinity[t], first, TN)
+        acc[slots[t]] = jnp.where(fresh, jnp.zeros_like(term), acc[slots[t]]) + term
 
     def total(slot):
         hit = slots[0] == slot
@@ -73,33 +72,50 @@
     for j in range(images):
         to_mate[j] = total(2 * images + j).astype(to_mate.dtype)
     for j in range(images):
-        own[j] = total(images + j)
-
-
-def forward_kernel(meta, affinity, rounded, from_mate, from_across, own, terms, p0, p1, p2, p3, rhs, acc):
+        value = total(images + j)
+        own_left[j] = value[:, :half]
+        own_right[j] = value[:, half:]
+
+
+def forward_kernel(start, meta, affinity, rounded, from_mate, from_across, own, terms, p0, p1, p2, p3, rhs, acc):
     tiles = affinity.shape[0]
-    images = rounded.shape[0]
+    images, _, half = rounded.shape
     for j in range(images):
-        acc[j] = own[j] + terms[j].astype(jnp.float32)
+        acc[j] = own[j] + terms[j, :, start : start + half].astype(jnp.float32)
     for t in range(tiles):
         slot = meta[tiles + t]
 
         @pl.when(slot < images)
         def _():
-            rhs[...] = from_across[slot]
+            rhs[t] = from_across[slot]
 
         @pl.when(jnp.logical_and(slot >= images, slot < 2 * images))
         def _():
-            rhs[...] = rounded[slot - images]
+            rhs[t] = rounded[slot - images]
 
         @pl.when(slot >= 2 * images)
         def _():
-            rhs[...] = from_mate[slot - 2 * images]
-
-        first = meta[t]
-        acc[first] = acc[first] + dot(affinity[t], rhs[...])
+            rhs[t] = from_mate[slot - 2 * images]
+
+    for t in range(tiles):
+        acc[meta[t]] = acc[meta[t]] + dot(affinity[t], rhs[t])
     for k, ref in enumerate((p0, p1, p2, p3)):
         ref[...] = acc[meta[2 * tiles + k]].astype(ref.dtype)
+
+
+def round_kernel(wide, left, right):
+    half = left.shape[2]
+    left[...] = wide[:, :, :half].astype(left.dtype)
+    right[...] = wide[:, :, half:].astype(right.dtype)
+
+
+def sum_kernel(start, *refs):
+    total = refs[0][...]
+    width = total.shape[1]
+    for ref in refs[1:-1]:
+        part = ref[...] if ref.shape[1] == width else ref[:, start : start + width]
+        total = total + part.astype(jnp.float32)
+    refs[-1][...] = total.astype(refs[-1].dtype)
 
 
 def split(x):
@@ -109,11 +125,11 @@
 
 def project_kernel(places, meta, factors, *rest):
     count = len(places)
-    gradients = rest[:count]
+    gradients = [jnp.concatenate([rest[2 * k][...], rest[2 * k + 1][...]], axis=1) for k in range(count)]
     out, held, sems = rest[-3:]
     ys = []
     for place, gradient in zip(places, gradients):
-        x = factors[meta[place]] + ascent_step * gradient[...].astype(jnp.float32)
+        x = factors[meta[place]] + ascent_step * gradient.astype(jnp.float32)
         squares = jnp.sum(jnp.sum(x * x, axis=0, keepdims=True), axis=1, keepdims=True)
         x = x * (start_scale * math.sqrt(x.shape[1]) * lax.rsqrt(squares + epsilon))
         ys.append(x.T)
@@ -143,8 +159,10 @@
 def project(places, meta, factors, gradients, result=None):
     _, keypoints, universe = factors.shape
     count = len(places)
-    in_specs = [SMEM, VMEM] + [VMEM] * count
-    operands = [meta, factors, *gradients]
+    operands = [meta, factors]
+    for pair in gradients:
+        operands += pair
+    in_specs = [SMEM] + [VMEM] * (len(operands) - 1)
     aliases = {}
     if result is not None:
         aliases = {len(operands): 0}
@@ -178,57 +196,92 @@
     order = (turn + jnp.arange(images, dtype=jnp.int32)) % images
     meta = jnp.concatenate([first, slot, order]).astype(jnp.int32)
 
-    rounded = factors.astype(jnp.bfloat16)
-    rounded, meta = lax.optimization_barrier((rounded, meta))
-    from_across = across(rounded)
-
-    wide = jax.ShapeDtypeStruct((images, keypoints, universe), jnp.float32)
-    narrow = jax.ShapeDtypeStruct((images, keypoints, universe), jnp.bfloat16)
-    one_wide = jax.ShapeDtypeStruct((keypoints, universe), jnp.float32)
-    one = jax.ShapeDtypeStruct((keypoints, universe), jnp.bfloat16)
-
-    own, to_mate, c0, c1, c2, c3 = pl.pallas_call(
+    half = universe // 2
+
+    left, right = pl.pallas_call(
+        round_kernel,
+        out_shape=(jax.ShapeDtypeStruct((images, keypoints, half), jnp.bfloat16),) * 2,
+        in_specs=[VMEM],
+        out_specs=(VMEM, VMEM),
+        compiler_params=pltpu.CompilerParams(vmem_limit_bytes=8 * MIB),
+        name="rounded",
+    )(factors)
+    left, right, meta = lax.optimization_barrier((left, right, meta))
+    across_left = across(left)
+    across_right = across(right)
+
+    def shape(*dims, dtype=jnp.bfloat16):
+        return jax.ShapeDtypeStruct(dims, dtype)
+
+    own_half = shape(images, keypoints, half, dtype=jnp.float32)
+    own_left, own_right, to_mate, c0, c1, c2, c3 = pl.pallas_call(
         backward_kernel,
-        out_shape=(wide, narrow, one_wide, one, one, one),
-        in_specs=[SMEM, VMEM, VMEM],
-        out_specs=(VMEM,) * 6,
+        out_shape=(
+            own_half,
+            own_half,
+            shape(images, keypoints, universe),
+            shape(keypoints, universe, dtype=jnp.float32),
+        )
+        + (shape(keypoints, universe),) * 3,
+        in_specs=[SMEM, VMEM, VMEM, VMEM],
+        out_specs=(VMEM,) * 7,
         scratch_shapes=[pltpu.VMEM((3 * images, keypoints, universe), jnp.float32)],
         compiler_params=pltpu.CompilerParams(vmem_limit_bytes=12 * MIB),
         cost_estimate=pl.CostEstimate(flops=600000000, bytes_accessed=8000000, transcendentals=0),
         name="backward",
-    )(meta, affinity, rounded)
+    )(meta, affinity, left, right)
     x1 = turned(c1, 1)
     x3 = turned(c3, -1)
     x2 = turned(c2, 2)
-    from_mate = mate(rounded)
+    mate_left = mate(left)
+    mate_right = mate(right)
     terms = mate(to_mate)
-    p0, p1, p2, p3 = pl.pallas_call(
-        forward_kernel,
-        out_shape=(one_wide, one, one, one),
-        in_specs=[SMEM] + [VMEM] * 6,
-        out_specs=(VMEM,) * 4,
-        scratch_shapes=[
-            pltpu.VMEM((keypoints, universe), jnp.bfloat16),
-            pltpu.VMEM((images, keypoints, universe), jnp.float32),
-        ],
-        compiler_params=pltpu.CompilerParams(vmem_limit_bytes=12 * MIB),
-        cost_estimate=pl.CostEstimate(flops=600000000, bytes_accessed=8000000, transcendentals=0),
-        name="forward",
-    )(meta, affinity, rounded, from_mate, from_across, own, terms)
-    crossing = c0 + x1.astype(jnp.float32) + x2.astype(jnp.float32) + x3.astype(jnp.float32)
-    crossed = across(crossing.astype(jnp.bfloat16))
-    y1 = turned(p1, 1)
-    y3 = turned(p3, -1)
-    y2 = turned(p2, 2)
-    gradient = p0 + y1.astype(jnp.float32) + y2.astype(jnp.float32) + y3.astype(jnp.float32) + crossed.astype(jnp.float32)
-    gradient = gradient.astype(jnp.bfloat16)
-    z1 = turned(gradient, 1)
-    z3 = turned(gradient, -1)
-    z2 = turned(gradient, 2)
-    own_place = 2 * tiles
-    result = project((own_place,), meta, factors, (gradient,))
-    result = project((own_place + 3, own_place + 1), meta, factors, (z1, z3), result)
-    result = project((own_place + 2,), meta, factors, (z2,), result)
+
+    def added(start, *operands):
+        return pl.pallas_call(
+            functools.partial(sum_kernel, start),
+            out_shape=shape(*operands[0].shape),
+            in_specs=[VMEM] * len(operands),
+            out_specs=VMEM,
+            compiler_params=pltpu.CompilerParams(vmem_limit_bytes=4 * MIB),
+            cost_estimate=pl.CostEstimate(flops=1000000, bytes_accessed=1000000, transcendentals=0),
+            name="added",
+        )(*operands)
+
+    crossed = across(added(0, c0, x1, x2, x3))
+
+    def forward(start, *operands):
+        return pl.pallas_call(
+            functools.partial(forward_kernel, start),
+            out_shape=(shape(keypoints, half, dtype=jnp.float32),) + (shape(keypoints, half),) * 3,
+            in_specs=[SMEM] + [VMEM] * 6,
+            out_specs=(VMEM,) * 4,
+            scratch_shapes=[
+                pltpu.VMEM((tiles, keypoints, half), jnp.bfloat16),
+                pltpu.VMEM((images, keypoints, half), jnp.float32),
+            ],
+            compiler_params=pltpu.CompilerParams(vmem_limit_bytes=8 * MIB),
+            cost_estimate=pl.CostEstimate(flops=600000000, bytes_accessed=4000000, transcendentals=0),
+            name="forward",
+        )(meta, affinity, *operands, terms)
+
+    def scattered(parts):
+        return parts[0], turned(parts[1], 1), turned(parts[3], -1), turned(parts[2], 2)
+
+    def gathered(gradient):
+        return [turned(gradient, 1), turned(gradient, -1), turned(gradient, 2)]
+
+    left_parts = forward(0, left, mate_left, across_left, own_left)
+    left_parts = scattered(left_parts)
+    right_parts = forward(half, right, mate_right, across_right, own_right)
+    right_parts = scattered(right_parts)
+    left_sum = added(0, *left_parts[:1], crossed, *left_parts[1:])
+    right_sum = added(half, *right_parts[:1], crossed, *right_parts[1:])
+    zl = gathered(left_sum)
+    zr = gathered(right_sum)
+    own = 2 * tiles
+    result = project((own,), meta, factors, [(left_sum, right_sum)])
+    result = project((own + 3, own + 1, own + 2), meta, factors, list(zip(zl, zr)), result)
     return result
 
 

time: 79.9 us -> 68.9 us (0.86)
  the two profiles are of different devices: /device:TPU:103 before, /device:TPU:128 now
where the time goes in v1:
time: 68.9 us; the launch traced here: 68.7 us
  starting transfers between devices  36.8 us (53%)
  Pallas kernels  14.9 us (22%)
  waiting for transfers between devices  14.2 us (21%)
  local copies, waits for them, and re-layouts  2.29 us (3%)
    ppermute x15, starting transfers between devices, turned(): return lax.ppermute(x, 'rep', [(i, (i + by) % n) for i in range(n)])  24.5 us
    ppermute x15, waiting for transfers between devices, turned(): return lax.ppermute(x, 'rep', [(i, (i + by) % n) for i in range(n)])  14.2 us
    ppermute x3, starting transfers between devices, across(): return lax.ppermute(x, 'tiles', pairs + [(b, a) for a, b in pairs])  12.3 us
    pallas_call x2, Pallas kernels, project(): pl.pallas_call(functools.partial(project_kernel, places), out_shape=jax.S...  9.75 us
    pallas_call x2, Pallas kernels, forward(): pl.pallas_call(functools.partial(forward_kernel, start), out_shape=(shape...  2.97 us
    unnamed x8, local copies, waits for them, and re-layouts  2.29 us
    pallas_call x1, Pallas kernels, shards(): pl.pallas_call(backward_kernel, out_shape=(own_half, own_half, shape(imag...  1.8 us
  transfers between devices with their start and end apart: 21, of which 7 were waited for; matrix products, arithmetic and copies ran while one was open for 0% of the time, Pallas kernels for 11%

profile of v1, /device:TPU:128, one launch (start us, length us, event | category | flops | bytes accessed | tf_op | source)
XLA Modules:
  0.0 68.7 jit_solution(18412714238696756307)
XLA Ops:
  0.0 1.7 %copy-done.1 = f32[4,512,256]{2,1,0:T(8,128)S(1)} copy-done((f32[4,512,256]{2,1,0:T(8,128)S(1)}, f32[4,512,256]{2,1,0:T(8,128)}, u32[]{:S(2)}) %copy-start.1) | copy-done | bytes 2097176
  1.7 0.1 rounded.1
  1.9 0.5 copy-done.3
  2.4 0.1 pad_add_fusion.meta
  2.5 1.8 %backward.1 = (f32[4,512,128]{2,1,0:T(8,128)S(1)}, f32[4,512,128]{2,1,0:T(8,128)S(1)}, bf16[4,512,256]{2,1,0:T(8,128)(2,1)S(1)}, f32[512,256]{1,0:T(8,128)S(1)},...) custom-call(s32[12]{0:T(128)S(1)} %pad_add_fusion.meta, ...), custom_call_target="tpu_custom_call" | custom-call | flops 600000000 | bytes 8000000 | tf_op jit(solution)/shard_map/backward/pallas_call | solution.py:217
  4.3 0.1 collective-permute-start.2
  4.4 1.7 %collective-permute-start.3 = (bf16[512,256]{1,0:T(8,128)(2,1)S(1)}, bf16[512,256]{1,0:T(8,128)(2,1)S(1)}, u32[]{:S(2)}, u32[]{:S(2)}) collective-permute-start(bf16[512,256]{1,0:T(8,128)(2,1)S(1)} %get-tuple-element.34), channel_id=1, source_target_pairs={{0,1},{1,2},{2,3},{3,0},{4,5},{5,6},{6,7},{7,4},{8,9},{9,10},{10,1... | collective-permute-start | bytes 786440 | tf_op jit(solution)/shard_map/ppermute | solution.py:39
  6.1 2.9 %collective-permute-start.4 = (bf16[512,256]{1,0:T(8,128)(2,1)S(1)}, bf16[512,256]{1,0:T(8,128)(2,1)S(1)}, u32[]{:S(2)}, u32[]{:S(2)}) collective-permute-start(bf16[512,256]{1,0:T(8,128)(2,1)S(1)} %get-tuple-element.35), channel_id=1, source_target_pairs={{0,2},{1,3},{2,0},{3,1},{4,6},{5,7},{6,4},{7,5},{8,10},{9,11},{10,... | collective-permute-start | bytes 786440 | tf_op jit(solution)/shard_map/ppermute | solution.py:39
  9.0 1.3 %collective-permute-start.5 = (bf16[512,256]{1,0:T(8,128)(2,1)S(1)}, bf16[512,256]{1,0:T(8,128)(2,1)S(1)}, u32[]{:S(2)}, u32[]{:S(2)}) collective-permute-start(bf16[512,256]{1,0:T(8,128)(2,1)S(1)} %get-tuple-element.36), channel_id=1, source_target_pairs={{0,3},{1,0},{2,1},{3,2},{4,7},{5,4},{6,5},{7,6},{8,11},{9,8},{10,9... | collective-permute-start | bytes 786440 | tf_op jit(solution)/shard_map/ppermute | solution.py:39
  10.3 4.1 %collective-permute-done.3.refs_1_ = bf16[512,256]{1,0:T(8,128)(2,1)S(1)} collective-permute-done((bf16[512,256]{1,0:T(8,128)(2,1)S(1)}, bf16[512,256]{1,0:T(8,128)(2,1)S(1)}, u32[]{:S(2)}, u32[]{:S(2)}) %collective-permute-start.3) | collective-permute-done | bytes 262176 | tf_op jit(solution)/shard_map/ppermute | solution.py:39
  14.4 3.4 %collective-permute-start.12 = (bf16[4,512,128]{2,1,0:T(8,128)(2,1)S(1)}, bf16[4,512,128]{2,1,0:T(8,128)(2,1)S(1)}, u32[]{:S(2)}, u32[]{:S(2)}) collective-permute-start(bf16[4,512,128]{2,1,0:T(8,128)(2,1)S(1)} %get-tuple-element.29.right.rounded), channel_id=1, source_target_pairs={{4,8},{12,16},{20,24},{28,32},{36,40},{44,48},{52,56},{60,64},{68,... | collective-permute-start | bytes 1572872 | tf_op jit(solution)/shard_map/ppermute | solution.py:34
  17.8 3.4 %collective-permute-done.4.refs_2_ = bf16[512,256]{1,0:T(8,128)(2,1)S(1)} collective-permute-done((bf16[512,256]{1,0:T(8,128)(2,1)S(1)}, bf16[512,256]{1,0:T(8,128)(2,1)S(1)}, u32[]{:S(2)}, u32[]{:S(2)}) %collective-permute-start.4) | collective-permute-done | bytes 262176 | tf_op jit(solution)/shard_map/ppermute | solution.py:39
  21.2 4.3 %collective-permute-start.1 = (bf16[4,512,128]{2,1,0:T(8,128)(2,1)S(1)}, bf16[4,512,128]{2,1,0:T(8,128)(2,1)S(1)}, u32[]{:S(2)}, u32[]{:S(2)}) collective-permute-start(bf16[4,512,128]{2,1,0:T(8,128)(2,1)S(1)} %get-tuple-element.28.left.rounded), channel_id=1, source_target_pairs={{4,8},{12,16},{20,24},{28,32},{36,40},{44,48},{52,56},{60,64},{68,... | collective-permute-start | bytes 1572872 | tf_op jit(solution)/shard_map/ppermute | solution.py:34
  25.5 0.1 added.3
  25.7 0.0 collective-permute-done.11.from_mate
  25.7 4.6 %collective-permute-start.6 = (bf16[512,256]{1,0:T(8,128)(2,1)S(1)}, bf16[512,256]{1,0:T(8,128)(2,1)S(1)}, u32[]{:S(2)}, u32[]{:S(2)}) collective-permute-start(bf16[512,256]{1,0:T(8,128)(2,1)S(1)} %added.3), channel_id=1, source_target_pairs={{4,8},{12,16},{20,24},{28,32},{36,40},{44,48},{52,56},{60,64},{68,... | collective-permute-start | bytes 786440 | tf_op jit(solution)/shard_map/ppermute | solution.py:34
  30.3 0.0 collective-permute-done.2.terms
  30.3 1.5 %forward.3 = (f32[512,128]{1,0:T(8,128)S(1)}, bf16[512,128]{1,0:T(8,128)(2,1)S(1)}, bf16[512,128]{1,0:T(8,128)(2,1)S(1)}, bf16[512,128]{1,0:T(8,128)(2,1)S(1)}) custom-call(s32[12]{0:T(128)S(1)} %pad_add_fusion.meta, bf16[4,512,512]{2,1,0:T(8,128)(2,1)S(1)} %copy-done, bf16[4,512,128]{2,1,0:T(8,128)(2,1)S(1)} %get-tuple-element.29.right.rounded, ...), custom_call_target="tpu_custom_call" | custom-call | flops 600000000 | bytes 4000000 | tf_op jit(solution)/shard_map/forward/pallas_call | solution.py:254
  31.8 1.2 %collective-permute-start.13 = (bf16[512,128]{1,0:T(8,128)(2,1)S(1)}, bf16[512,128]{1,0:T(8,128)(2,1)S(1)}, u32[]{:S(2)}, u32[]{:S(2)}) collective-permute-start(bf16[512,128]{1,0:T(8,128)(2,1)S(1)} %get-tuple-element.42), channel_id=1, source_target_pairs={{0,1},{1,2},{2,3},{3,0},{4,5},{5,6},{6,7},{7,4},{8,9},{9,10},{10,1... | collective-permute-start | bytes 393224 | tf_op jit(solution)/shard_map/ppermute | solution.py:39
  33.0 2.1 %collective-permute-start.14 = (bf16[512,128]{1,0:T(8,128)(2,1)S(1)}, bf16[512,128]{1,0:T(8,128)(2,1)S(1)}, u32[]{:S(2)}, u32[]{:S(2)}) collective-permute-start(bf16[512,128]{1,0:T(8,128)(2,1)S(1)} %get-tuple-element.43), channel_id=1, source_target_pairs={{0,3},{1,0},{2,1},{3,2},{4,7},{5,4},{6,5},{7,6},{8,11},{9,8},{10,9... | collective-permute-start | bytes 393224 | tf_op jit(solution)/shard_map/ppermute | solution.py:39
  35.1 0.0 collective-permute-done.from_mate
  35.1 4.3 %collective-permute-start.15 = (bf16[512,128]{1,0:T(8,128)(2,1)S(1)}, bf16[512,128]{1,0:T(8,128)(2,1)S(1)}, u32[]{:S(2)}, u32[]{:S(2)}) collective-permute-start(bf16[512,128]{1,0:T(8,128)(2,1)S(1)} %get-tuple-element.44), channel_id=1, source_target_pairs={{0,2},{1,3},{2,0},{3,1},{4,6},{5,7},{6,4},{7,5},{8,10},{9,11},{10,... | collective-permute-start | bytes 393224 | tf_op jit(solution)/shard_map/ppermute | solution.py:39
  39.4 1.5 %forward.2 = (f32[512,128]{1,0:T(8,128)S(1)}, bf16[512,128]{1,0:T(8,128)(2,1)S(1)}, bf16[512,128]{1,0:T(8,128)(2,1)S(1)}, bf16[512,128]{1,0:T(8,128)(2,1)S(1)}) custom-call(s32[12]{0:T(128)S(1)} %pad_add_fusion.meta, bf16[4,512,512]{2,1,0:T(8,128)(2,1)S(1)} %copy-done, bf16[4,512,128]{2,1,0:T(8,128)(2,1)S(1)} %get-tuple-element.28.left.rounded, ...), custom_call_target="tpu_custom_call" | custom-call | flops 600000000 | bytes 4000000 | tf_op jit(solution)/shard_map/forward/pallas_call | solution.py:254
  40.9 0.0 copy-start.2
  40.9 0.1 collective-permute-start.7
  41.0 3.2 %collective-permute-start.8 = (bf16[512,128]{1,0:T(8,128)(2,1)S(1)}, bf16[512,128]{1,0:T(8,128)(2,1)S(1)}, u32[]{:S(2)}, u32[]{:S(2)}) collective-permute-start(bf16[512,128]{1,0:T(8,128)(2,1)S(1)} %get-tuple-element.38), channel_id=1, source_target_pairs={{0,3},{1,0},{2,1},{3,2},{4,7},{5,4},{6,5},{7,6},{8,11},{9,8},{10,9... | collective-permute-start | bytes 393224 | tf_op jit(solution)/shard_map/ppermute | solution.py:39
  44.2 0.0 collective-permute-done.13.refs_2_
  44.2 0.8 %collective-permute-start.9 = (bf16[512,128]{1,0:T(8,128)(2,1)S(1)}, bf16[512,128]{1,0:T(8,128)(2,1)S(1)}, u32[]{:S(2)}, u32[]{:S(2)}) collective-permute-start(bf16[512,128]{1,0:T(8,128)(2,1)S(1)} %get-tuple-element.39), channel_id=1, source_target_pairs={{0,2},{1,3},{2,0},{3,1},{4,6},{5,7},{6,4},{7,5},{8,10},{9,11},{10,... | collective-permute-start | bytes 393224 | tf_op jit(solution)/shard_map/ppermute | solution.py:39
  45.0 0.0 collective-permute-done.14.refs_3_
  45.0 0.0 collective-permute-done.15.refs_4_
  45.0 0.1 added.5.rest_1_
  45.1 0.9 %collective-permute-start.16 = (bf16[512,128]{1,0:T(8,128)(2,1)S(1)}, bf16[512,128]{1,0:T(8,128)(2,1)S(1)}, u32[]{:S(2)}, u32[]{:S(2)}) collective-permute-start(bf16[512,128]{1,0:T(8,128)(2,1)S(1)} %added.5.rest_1_), channel_id=1, source_target_pairs={{0,1},{1,2},{2,3},{3,0},{4,5},{5,6},{6,7},{7,4},{8,9},{9,10},{10,1... | collective-permute-start | bytes 393224 | tf_op jit(solution)/shard_map/ppermute | solution.py:39
  46.0 2.6 %collective-permute-start.18 = (bf16[512,128]{1,0:T(8,128)(2,1)S(1)}, bf16[512,128]{1,0:T(8,128)(2,1)S(1)}, u32[]{:S(2)}, u32[]{:S(2)}) collective-permute-start(bf16[512,128]{1,0:T(8,128)(2,1)S(1)} %added.5.rest_1_), channel_id=1, source_target_pairs={{0,3},{1,0},{2,1},{3,2},{4,7},{5,4},{6,5},{7,6},{8,11},{9,8},{10,9... | collective-permute-start | bytes 393224 | tf_op jit(solution)/shard_map/ppermute | solution.py:39
  48.6 1.5 %collective-permute-done.7.refs_2_ = bf16[512,128]{1,0:T(8,128)(2,1)S(1)} collective-permute-done((bf16[512,128]{1,0:T(8,128)(2,1)S(1)}, bf16[512,128]{1,0:T(8,128)(2,1)S(1)}, u32[]{:S(2)}, u32[]{:S(2)}) %collective-permute-start.7) | collective-permute-done | bytes 131104 | tf_op jit(solution)/shard_map/ppermute | solution.py:39
  50.1 0.0 collective-permute-start.20
  50.1 0.7 collective-permute-done.8.refs_3_
  50.8 1.3 %collective-permute-done.9.refs_4_ = bf16[512,128]{1,0:T(8,128)(2,1)S(1)} collective-permute-done((bf16[512,128]{1,0:T(8,128)(2,1)S(1)}, bf16[512,128]{1,0:T(8,128)(2,1)S(1)}, u32[]{:S(2)}, u32[]{:S(2)}) %collective-permute-start.9) | collective-permute-done | bytes 131104 | tf_op jit(solution)/shard_map/ppermute | solution.py:39
  52.1 0.1 added.4.rest_0_
  52.2 0.8 %collective-permute-start.10 = (bf16[512,128]{1,0:T(8,128)(2,1)S(1)}, bf16[512,128]{1,0:T(8,128)(2,1)S(1)}, u32[]{:S(2)}, u32[]{:S(2)}) collective-permute-start(bf16[512,128]{1,0:T(8,128)(2,1)S(1)} %added.4.rest_0_), channel_id=1, source_target_pairs={{0,1},{1,2},{2,3},{3,0},{4,5},{5,6},{6,7},{7,4},{8,9},{9,10},{10,1... | collective-permute-start | bytes 393224 | tf_op jit(solution)/shard_map/ppermute | solution.py:39
  52.9 2.5 %collective-permute-start.17 = (bf16[512,128]{1,0:T(8,128)(2,1)S(1)}, bf16[512,128]{1,0:T(8,128)(2,1)S(1)}, u32[]{:S(2)}, u32[]{:S(2)}) collective-permute-start(bf16[512,128]{1,0:T(8,128)(2,1)S(1)} %added.4.rest_0_), channel_id=1, source_target_pairs={{0,3},{1,0},{2,1},{3,2},{4,7},{5,4},{6,5},{7,6},{8,11},{9,8},{10,9... | collective-permute-start | bytes 393224 | tf_op jit(solution)/shard_map/ppermute | solution.py:39
  55.5 1.2 %collective-permute-done.16.rest_1_ = bf16[512,128]{1,0:T(8,128)(2,1)S(1)} collective-permute-done((bf16[512,128]{1,0:T(8,128)(2,1)S(1)}, bf16[512,128]{1,0:T(8,128)(2,1)S(1)}, u32[]{:S(2)}, u32[]{:S(2)}) %collective-permute-start.16) | collective-permute-done | bytes 131104 | tf_op jit(solution)/shard_map/ppermute | solution.py:39
  56.7 0.0 collective-permute-start.19
  56.7 4.4 %project.2.rest_6_ = f32[4,512,256]{2,1,0:T(8,128)} custom-call(s32[12]{0:T(128)S(1)} %pad_add_fusion.meta, f32[4,512,256]{2,1,0:T(8,128)S(1)} %copy-done.2, bf16[512,128]{1,0:T(8,128)(2,1)S(1)} %added.4.rest_0_, bf16[512,128]{1,0:T(8,128)(2,1)S(1)} %added.5.rest_1_), custom_call_target="tpu_custom_call" | custom-call | flops 2000000000 | bytes 2000000 | tf_op jit(solution)/shard_map/project/pallas_call | solution.py:171
  61.1 0.0 collective-permute-done.18.rest_3_
  61.1 0.0 collective-permute-done.10.rest_0_
  61.1 0.0 collective-permute-done.17.rest_2_
  61.1 2.1 %collective-permute-done.19.rest_4_ = bf16[512,128]{1,0:T(8,128)(2,1)S(1)} collective-permute-done((bf16[512,128]{1,0:T(8,128)(2,1)S(1)}, bf16[512,128]{1,0:T(8,128)(2,1)S(1)}, u32[]{:S(2)}, u32[]{:S(2)}) %collective-permute-start.19) | collective-permute-done | bytes 131104 | tf_op jit(solution)/shard_map/ppermute | solution.py:39
  63.2 5.4 %project.3 = f32[4,512,256]{2,1,0:T(8,128)} custom-call(s32[12]{0:T(128)S(1)} %pad_add_fusion.meta, f32[4,512,256]{2,1,0:T(8,128)S(1)} %copy-done.2, bf16[512,128]{1,0:T(8,128)(2,1)S(1)} %collective-permute-done.10.rest_0_, bf16[512,128]{1,0:T(8,128)(2,1)S(1)} %collective-permute-done.16.rest_1_, ...), custom_call_target="tpu_custom_call", output_to_operand_aliasing={{}: (8, {})} | custom-call | flops 6000000000 | bytes 6000000 | tf_op jit(solution)/shard_map/project/pallas_call | solution.py:171
  (14 shorter events, 0.0 us)
Async XLA Ops:
  0.0 2.5 %copy-start = (bf16[4,512,512]{2,1,0:T(8,128)(2,1)S(1)}, bf16[4,512,512]{2,1,0:T(8,128)(2,1)}, u32[]{:S(2)}) copy-start(bf16[4,512,512]{2,1,0:T(8,128)(2,1)} %affinity.5) | copy-start | bytes 6291460
  0.0 1.7 %copy-start.1 = (f32[4,512,256]{2,1,0:T(8,128)S(1)}, f32[4,512,256]{2,1,0:T(8,128)}, u32[]{:S(2)}) copy-start(f32[4,512,256]{2,1,0:T(8,128)} %factors.3) | copy-start | bytes 6291460
  1.7 0.7 copy-start.3
  4.3 25.9 %collective-permute-start.2 = (bf16[4,512,256]{2,1,0:T(8,128)(2,1)S(1)}, bf16[4,512,256]{2,1,0:T(8,128)(2,1)S(1)}, u32[]{:S(2)}, u32[]{:S(2)}) collective-permute-start(bf16[4,512,256]{2,1,0:T(8,128)(2,1)S(1)} %get-tuple-element.31), channel_id=1, source_target_pairs={{0,4},{4,0},{8,12},{12,8},{16,20},{20,16},{24,28},{28,24},{32,36},... | collective-permute-start | bytes 3145736 | tf_op jit(solution)/shard_map/ppermute | solution.py:28
  4.4 10.0 %collective-permute-start.3 = (bf16[512,256]{1,0:T(8,128)(2,1)S(1)}, bf16[512,256]{1,0:T(8,128)(2,1)S(1)}, u32[]{:S(2)}, u32[]{:S(2)}) collective-permute-start(bf16[512,256]{1,0:T(8,128)(2,1)S(1)} %get-tuple-element.34), channel_id=1, source_target_pairs={{0,1},{1,2},{2,3},{3,0},{4,5},{5,6},{6,7},{7,4},{8,9},{9,10},{10,1... | collective-permute-start | bytes 786440 | tf_op jit(solution)/shard_map/ppermute | solution.py:39
  6.1 15.1 %collective-permute-start.4 = (bf16[512,256]{1,0:T(8,128)(2,1)S(1)}, bf16[512,256]{1,0:T(8,128)(2,1)S(1)}, u32[]{:S(2)}, u32[]{:S(2)}) collective-permute-start(bf16[512,256]{1,0:T(8,128)(2,1)S(1)} %get-tuple-element.35), channel_id=1, source_target_pairs={{0,2},{1,3},{2,0},{3,1},{4,6},{5,7},{6,4},{7,5},{8,10},{9,11},{10,... | collective-permute-start | bytes 786440 | tf_op jit(solution)/shard_map/ppermute | solution.py:39
  9.0 12.2 %collective-permute-start.5 = (bf16[512,256]{1,0:T(8,128)(2,1)S(1)}, bf16[512,256]{1,0:T(8,128)(2,1)S(1)}, u32[]{:S(2)}, u32[]{:S(2)}) collective-permute-start(bf16[512,256]{1,0:T(8,128)(2,1)S(1)} %get-tuple-element.36), channel_id=1, source_target_pairs={{0,3},{1,0},{2,1},{3,2},{4,7},{5,4},{6,5},{7,6},{8,11},{9,8},{10,9... | collective-permute-start | bytes 786440 | tf_op jit(solution)/shard_map/ppermute | solution.py:39
  10.3 15.3 %collective-permute-start.11 = (bf16[4,512,128]{2,1,0:T(8,128)(2,1)S(1)}, bf16[4,512,128]{2,1,0:T(8,128)(2,1)S(1)}, u32[]{:S(2)}, u32[]{:S(2)}) collective-permute-start(bf16[4,512,128]{2,1,0:T(8,128)(2,1)S(1)} %get-tuple-element.29.right.rounded), channel_id=1, source_target_pairs={{0,4},{4,0},{8,12},{12,8},{16,20},{20,16},{24,28},{28,24},{32,36},... | collective-permute-start | bytes 1572872 | tf_op jit(solution)/shard_map/ppermute | solution.py:28
  14.4 15.8 %collective-permute-start.12 = (bf16[4,512,128]{2,1,0:T(8,128)(2,1)S(1)}, bf16[4,512,128]{2,1,0:T(8,128)(2,1)S(1)}, u32[]{:S(2)}, u32[]{:S(2)}) collective-permute-start(bf16[4,512,128]{2,1,0:T(8,128)(2,1)S(1)} %get-tuple-element.29.right.rounded), channel_id=1, source_target_pairs={{4,8},{12,16},{20,24},{28,32},{36,40},{44,48},{52,56},{60,64},{68,... | collective-permute-start | bytes 1572872 | tf_op jit(solution)/shard_map/ppermute | solution.py:34
  21.2 13.9 %collective-permute-start = (bf16[4,512,128]{2,1,0:T(8,128)(2,1)S(1)}, bf16[4,512,128]{2,1,0:T(8,128)(2,1)S(1)}, u32[]{:S(2)}, u32[]{:S(2)}) collective-permute-start(bf16[4,512,128]{2,1,0:T(8,128)(2,1)S(1)} %get-tuple-element.28.left.rounded), channel_id=1, source_target_pairs={{0,4},{4,0},{8,12},{12,8},{16,20},{20,16},{24,28},{28,24},{32,36},... | collective-permute-start | bytes 1572872 | tf_op jit(solution)/shard_map/ppermute | solution.py:28
  21.2 18.2 %collective-permute-start.1 = (bf16[4,512,128]{2,1,0:T(8,128)(2,1)S(1)}, bf16[4,512,128]{2,1,0:T(8,128)(2,1)S(1)}, u32[]{:S(2)}, u32[]{:S(2)}) collective-permute-start(bf16[4,512,128]{2,1,0:T(8,128)(2,1)S(1)} %get-tuple-element.28.left.rounded), channel_id=1, source_target_pairs={{4,8},{12,16},{20,24},{28,32},{36,40},{44,48},{52,56},{60,64},{68,... | collective-permute-start | bytes 1572872 | tf_op jit(solution)/shard_map/ppermute | solution.py:34
  25.7 15.3 %collective-permute-start.6 = (bf16[512,256]{1,0:T(8,128)(2,1)S(1)}, bf16[512,256]{1,0:T(8,128)(2,1)S(1)}, u32[]{:S(2)}, u32[]{:S(2)}) collective-permute-start(bf16[512,256]{1,0:T(8,128)(2,1)S(1)} %added.3), channel_id=1, source_target_pairs={{4,8},{12,16},{20,24},{28,32},{36,40},{44,48},{52,56},{60,64},{68,... | collective-permute-start | bytes 786440 | tf_op jit(solution)/shard_map/ppermute | solution.py:34
  31.8 12.4 %collective-permute-start.13 = (bf16[512,128]{1,0:T(8,128)(2,1)S(1)}, bf16[512,128]{1,0:T(8,128)(2,1)S(1)}, u32[]{:S(2)}, u32[]{:S(2)}) collective-permute-start(bf16[512,128]{1,0:T(8,128)(2,1)S(1)} %get-tuple-element.42), channel_id=1, source_target_pairs={{0,1},{1,2},{2,3},{3,0},{4,5},{5,6},{6,7},{7,4},{8,9},{9,10},{10,1... | collective-permute-start | bytes 393224 | tf_op jit(solution)/shard_map/ppermute | solution.py:39
  33.0 12.0 %collective-permute-start.14 = (bf16[512,128]{1,0:T(8,128)(2,1)S(1)}, bf16[512,128]{1,0:T(8,128)(2,1)S(1)}, u32[]{:S(2)}, u32[]{:S(2)}) collective-permute-start(bf16[512,128]{1,0:T(8,128)(2,1)S(1)} %get-tuple-element.43), channel_id=1, source_target_pairs={{0,3},{1,0},{2,1},{3,2},{4,7},{5,4},{6,5},{7,6},{8,11},{9,8},{10,9... | collective-permute-start | bytes 393224 | tf_op jit(solution)/shard_map/ppermute | solution.py:39
  35.1 9.9 %collective-permute-start.15 = (bf16[512,128]{1,0:T(8,128)(2,1)S(1)}, bf16[512,128]{1,0:T(8,128)(2,1)S(1)}, u32[]{:S(2)}, u32[]{:S(2)}) collective-permute-start(bf16[512,128]{1,0:T(8,128)(2,1)S(1)} %get-tuple-element.44), channel_id=1, source_target_pairs={{0,2},{1,3},{2,0},{3,1},{4,6},{5,7},{6,4},{7,5},{8,10},{9,11},{10,... | collective-permute-start | bytes 393224 | tf_op jit(solution)/shard_map/ppermute | solution.py:39
  40.9 15.8 %copy-start.2 = (f32[4,512,256]{2,1,0:T(8,128)S(1)}, f32[4,512,256]{2,1,0:T(8,128)}, u32[]{:S(2)}) copy-start(f32[4,512,256]{2,1,0:T(8,128)} %factors.3) | copy-start | bytes 6291460
  40.9 9.2 %collective-permute-start.7 = (bf16[512,128]{1,0:T(8,128)(2,1)S(1)}, bf16[512,128]{1,0:T(8,128)(2,1)S(1)}, u32[]{:S(2)}, u32[]{:S(2)}) collective-permute-start(bf16[512,128]{1,0:T(8,128)(2,1)S(1)} %get-tuple-element.37), channel_id=1, source_target_pairs={{0,1},{1,2},{2,3},{3,0},{4,5},{5,6},{6,7},{7,4},{8,9},{9,10},{10,1... | collective-permute-start | bytes 393224 | tf_op jit(solution)/shard_map/ppermute | solution.py:39
  41.0 9.8 %collective-permute-start.8 = (bf16[512,128]{1,0:T(8,128)(2,1)S(1)}, bf16[512,128]{1,0:T(8,128)(2,1)S(1)}, u32[]{:S(2)}, u32[]{:S(2)}) collective-permute-start(bf16[512,128]{1,0:T(8,128)(2,1)S(1)} %get-tuple-element.38), channel_id=1, source_target_pairs={{0,3},{1,0},{2,1},{3,2},{4,7},{5,4},{6,5},{7,6},{8,11},{9,8},{10,9... | collective-permute-start | bytes 393224 | tf_op jit(solution)/shard_map/ppermute | solution.py:39
  44.2 7.9 %collective-permute-start.9 = (bf16[512,128]{1,0:T(8,128)(2,1)S(1)}, bf16[512,128]{1,0:T(8,128)(2,1)S(1)}, u32[]{:S(2)}, u32[]{:S(2)}) collective-permute-start(bf16[512,128]{1,0:T(8,128)(2,1)S(1)} %get-tuple-element.39), channel_id=1, source_target_pairs={{0,2},{1,3},{2,0},{3,1},{4,6},{5,7},{6,4},{7,5},{8,10},{9,11},{10,... | collective-permute-start | bytes 393224 | tf_op jit(solution)/shard_map/ppermute | solution.py:39
  45.1 11.6 %collective-permute-start.16 = (bf16[512,128]{1,0:T(8,128)(2,1)S(1)}, bf16[512,128]{1,0:T(8,128)(2,1)S(1)}, u32[]{:S(2)}, u32[]{:S(2)}) collective-permute-start(bf16[512,128]{1,0:T(8,128)(2,1)S(1)} %added.5.rest_1_), channel_id=1, source_target_pairs={{0,1},{1,2},{2,3},{3,0},{4,5},{5,6},{6,7},{7,4},{8,9},{9,10},{10,1... | collective-permute-start | bytes 393224 | tf_op jit(solution)/shard_map/ppermute | solution.py:39
  46.0 15.1 %collective-permute-start.18 = (bf16[512,128]{1,0:T(8,128)(2,1)S(1)}, bf16[512,128]{1,0:T(8,128)(2,1)S(1)}, u32[]{:S(2)}, u32[]{:S(2)}) collective-permute-start(bf16[512,128]{1,0:T(8,128)(2,1)S(1)} %added.5.rest_1_), channel_id=1, source_target_pairs={{0,3},{1,0},{2,1},{3,2},{4,7},{5,4},{6,5},{7,6},{8,11},{9,8},{10,9... | collective-permute-start | bytes 393224 | tf_op jit(solution)/shard_map/ppermute | solution.py:39
  50.1 11.0 %collective-permute-start.20 = (bf16[512,128]{1,0:T(8,128)(2,1)S(1)}, bf16[512,128]{1,0:T(8,128)(2,1)S(1)}, u32[]{:S(2)}, u32[]{:S(2)}) collective-permute-start(bf16[512,128]{1,0:T(8,128)(2,1)S(1)} %added.5.rest_1_), channel_id=1, source_target_pairs={{0,2},{1,3},{2,0},{3,1},{4,6},{5,7},{6,4},{7,5},{8,10},{9,11},{10,... | collective-permute-start | bytes 393224 | tf_op jit(solution)/shard_map/ppermute | solution.py:39
  52.2 8.9 %collective-permute-start.10 = (bf16[512,128]{1,0:T(8,128)(2,1)S(1)}, bf16[512,128]{1,0:T(8,128)(2,1)S(1)}, u32[]{:S(2)}, u32[]{:S(2)}) collective-permute-start(bf16[512,128]{1,0:T(8,128)(2,1)S(1)} %added.4.rest_0_), channel_id=1, source_target_pairs={{0,1},{1,2},{2,3},{3,0},{4,5},{5,6},{6,7},{7,4},{8,9},{9,10},{10,1... | collective-permute-start | bytes 393224 | tf_op jit(solution)/shard_map/ppermute | solution.py:39
  52.9 8.2 %collective-permute-start.17 = (bf16[512,128]{1,0:T(8,128)(2,1)S(1)}, bf16[512,128]{1,0:T(8,128)(2,1)S(1)}, u32[]{:S(2)}, u32[]{:S(2)}) collective-permute-start(bf16[512,128]{1,0:T(8,128)(2,1)S(1)} %added.4.rest_0_), channel_id=1, source_target_pairs={{0,3},{1,0},{2,1},{3,2},{4,7},{5,4},{6,5},{7,6},{8,11},{9,8},{10,9... | collective-permute-start | bytes 393224 | tf_op jit(solution)/shard_map/ppermute | solution.py:39
  56.7 6.5 %collective-permute-start.19 = (bf16[512,128]{1,0:T(8,128)(2,1)S(1)}, bf16[512,128]{1,0:T(8,128)(2,1)S(1)}, u32[]{:S(2)}, u32[]{:S(2)}) collective-permute-start(bf16[512,128]{1,0:T(8,128)(2,1)S(1)} %added.4.rest_0_), channel_id=1, source_target_pairs={{0,2},{1,3},{2,0},{3,1},{4,6},{5,7},{6,4},{7,5},{8,10},{9,11},{10,... | collective-permute-start | bytes 393224 | tf_op jit(solution)/shard_map/ppermute | solution.py:39

commit v2 on v1

--- a/solution.py
+++ b/solution.py
@@ -43,20 +43,37 @@
     return lax.dot_general(a, b, (dims, ((), ())), preferred_element_type=jnp.float32)
 
 
+def places(pairs, images):
+    owner = lax.axis_index("tiles")
+    tiles = pairs.shape[1]
+    even = lax.rem(owner, 2) == 0
+    firsts, slots = [], []
+    for t in range(tiles):
+        firsts.append(pairs[0, t] - owner * images)
+        slot = pairs[1, t] - (owner - 1) * images
+        shift = jnp.where(slot < images, 2 * images, jnp.where(slot < 2 * images, 0, -2 * images))
+        slots.append(slot + jnp.where(even, 0, shift))
+    return firsts, slots, order(images)
+
+
+def order(images):
+    turn = lax.axis_index("rep")
+    return [lax.rem(turn + k, images) for k in range(images)]
+
+
 TN = ((0,), (0,))
 NT = ((1,), (1,))
 
 
-def backward_kernel(meta, affinity, left, right, own_left, own_right, to_mate, c0, c1, c2, c3, acc):
+def backward_kernel(pairs, affinity, left, right, own_left, own_right, to_mate, c0, c1, c2, c3, acc):
     tiles = affinity.shape[0]
-    images = left.shape[0]
-    half = left.shape[2]
-    slots = [meta[tiles + t] for t in range(tiles)]
+    images, _, half = left.shape
+    firsts, slots, turns = places(pairs, images)
     for t in range(tiles):
         fresh = slots[t] >= 0
         for u in range(t):
             fresh = jnp.logical_and(fresh, slots[u] != slots[t])
-        first = jnp.concatenate([left[meta[t]], right[meta[t]]], axis=1)
+        first = jnp.concatenate([left[firsts[t]], right[firsts[t]]], axis=1)
         term = dot(affinity[t], first, TN)
         acc[slots[t]] = jnp.where(fresh, jnp.zeros_like(term), acc[slots[t]]) + term
 
@@ -67,8 +84,8 @@
         value = acc[slot]
         return jnp.where(hit, value, jnp.zeros_like(value))
 
-    for k, ref in enumerate((c0, c1, c2, c3)):
-        ref[...] = total(meta[2 * tiles + k]).astype(ref.dtype)
+    for turn, ref in zip(turns, (c0, c1, c2, c3)):
+        ref[...] = total(turn).astype(ref.dtype)
     for j in range(images):
         to_mate[j] = total(2 * images + j).astype(to_mate.dtype)
     for j in range(images):
@@ -77,13 +94,19 @@
         own_right[j] = value[:, half:]
 
 
-def forward_kernel(start, meta, affinity, rounded, from_mate, from_across, own, terms, p0, p1, p2, p3, rhs, acc):
+def forward_kernel(
+    start, pairs, affinity, rounded, from_mate, from_across, own, terms, p0, p1, p2, p3, rhs, acc, held, sem
+):
     tiles = affinity.shape[0]
     images, _, half = rounded.shape
+    copy = pltpu.make_async_copy(pairs, held, sem)
+    copy.start()
     for j in range(images):
         acc[j] = own[j] + terms[j, :, start : start + half].astype(jnp.float32)
+    copy.wait()
+    firsts, slots, turns = places(held, images)
     for t in range(tiles):
-        slot = meta[tiles + t]
+        slot = slots[t]
 
         @pl.when(slot < images)
         def _():
@@ -98,9 +121,9 @@
             rhs[t] = from_mate[slot - 2 * images]
 
     for t in range(tiles):
-        acc[meta[t]] = acc[meta[t]] + dot(affinity[t], rhs[t])
-    for k, ref in enumerate((p0, p1, p2, p3)):
-        ref[...] = acc[meta[2 * tiles + k]].astype(ref.dtype)
+        acc[firsts[t]] = acc[firsts[t]] + dot(affinity[t], rhs[t])
+    for turn, ref in zip(turns, (p0, p1, p2, p3)):
+        ref[...] = acc[turn].astype(ref.dtype)
 
 
 def round_kernel(wide, left, right):
@@ -123,13 +146,14 @@
     return high, (x - high.astype(jnp.float32)).astype(jnp.bfloat16)
 
 
-def project_kernel(places, meta, factors, *rest):
-    count = len(places)
+def project_kernel(ahead, factors, *rest):
+    count = len(ahead)
+    turns = order(factors.shape[0])
     gradients = [jnp.concatenate([rest[2 * k][...], rest[2 * k + 1][...]], axis=1) for k in range(count)]
     out, held, sems = rest[-3:]
     ys = []
-    for place, gradient in zip(places, gradients):
-        x = factors[meta[place]] + ascent_step * gradient.astype(jnp.float32)
+    for k, gradient in zip(ahead, gradients):
+        x = factors[turns[k]] + ascent_step * gradient.astype(jnp.float32)
         squares = jnp.sum(jnp.sum(x * x, axis=0, keepdims=True), axis=1, keepdims=True)
         x = x * (start_scale * math.sqrt(x.shape[1]) * lax.rsqrt(squares + epsilon))
         ys.append(x.T)
@@ -148,28 +172,28 @@
             ]
         ys = [1.5 * y - 0.5 * c for y, c in zip(ys, changes)]
     copies = []
-    for k, (place, y) in enumerate(zip(places, ys)):
+    for k, y in enumerate(ys):
         held[k] = (y * math.sqrt(P_SIZE)).T
-        copies.append(pltpu.make_async_copy(held.at[k], out.at[meta[place]], sems.at[k]))
+        copies.append(pltpu.make_async_copy(held.at[k], out.at[turns[ahead[k]]], sems.at[k]))
         copies[-1].start()
     for copy in copies:
         copy.wait()
 
 
-def project(places, meta, factors, gradients, result=None):
+def project(ahead, factors, gradients, result=None):
     _, keypoints, universe = factors.shape
-    count = len(places)
-    operands = [meta, factors]
+    count = len(ahead)
+    operands = [factors]
     for pair in gradients:
         operands += pair
-    in_specs = [SMEM] + [VMEM] * (len(operands) - 1)
+    in_specs = [VMEM] * len(operands)
     aliases = {}
     if result is not None:
         aliases = {len(operands): 0}
         in_specs.append(pl.BlockSpec(memory_space=pl.ANY))
         operands.append(result)
     return pl.pallas_call(
-        functools.partial(project_kernel, places),
+        functools.partial(project_kernel, ahead),
         out_shape=jax.ShapeDtypeStruct(factors.shape, jnp.float32),
         in_specs=in_specs,
         out_specs=pl.BlockSpec(memory_space=pl.ANY),
@@ -186,39 +210,28 @@
 
 def shards(affinity, tile_pairs, factors):
     images, keypoints, universe = factors.shape
-    tiles = affinity.shape[0]
-    owner = lax.axis_index("tiles")
-    turn = lax.axis_index("rep")
-    first = tile_pairs[:, 0] - owner * images
-    slot = tile_pairs[:, 1] - (owner - 1) * images
-    swapped = jnp.where(slot < images, slot + 2 * images, jnp.where(slot < 2 * images, slot, slot - 2 * images))
-    slot = jnp.where(owner % 2 == 0, slot, swapped)
-    order = (turn + jnp.arange(images, dtype=jnp.int32)) % images
-    meta = jnp.concatenate([first, slot, order]).astype(jnp.int32)
-
     half = universe // 2
-
+    pairs = tile_pairs.T
     left, right = pl.pallas_call(
         round_kernel,
         out_shape=(jax.ShapeDtypeStruct((images, keypoints, half), jnp.bfloat16),) * 2,
         in_specs=[VMEM],
         out_specs=(VMEM, VMEM),
         compiler_params=pltpu.CompilerParams(vmem_limit_bytes=8 * MIB),
+        cost_estimate=pl.CostEstimate(flops=1000000, bytes_accessed=3000000, transcendentals=0),
         name="rounded",
     )(factors)
-    left, right, meta = lax.optimization_barrier((left, right, meta))
     across_left = across(left)
     across_right = across(right)
 
     def shape(*dims, dtype=jnp.bfloat16):
         return jax.ShapeDtypeStruct(dims, dtype)
 
-    own_half = shape(images, keypoints, half, dtype=jnp.float32)
     own_left, own_right, to_mate, c0, c1, c2, c3 = pl.pallas_call(
         backward_kernel,
         out_shape=(
-            own_half,
-            own_half,
+            shape(images, keypoints, half, dtype=jnp.float32),
+            shape(images, keypoints, half, dtype=jnp.float32),
             shape(images, keypoints, universe),
             shape(keypoints, universe, dtype=jnp.float32),
         )
@@ -229,7 +242,7 @@
         compiler_params=pltpu.CompilerParams(vmem_limit_bytes=12 * MIB),
         cost_estimate=pl.CostEstimate(flops=600000000, bytes_accessed=8000000, transcendentals=0),
         name="backward",
-    )(meta, affinity, left, right)
+    )(pairs, affinity, left, right)
     x1 = turned(c1, 1)
     x3 = turned(c3, -1)
     x2 = turned(c2, 2)
@@ -254,16 +267,18 @@
         return pl.pallas_call(
             functools.partial(forward_kernel, start),
             out_shape=(shape(keypoints, half, dtype=jnp.float32),) + (shape(keypoints, half),) * 3,
-            in_specs=[SMEM] + [VMEM] * 6,
+            in_specs=[pl.BlockSpec(memory_space=pl.ANY)] + [VMEM] * 6,
             out_specs=(VMEM,) * 4,
             scratch_shapes=[
-                pltpu.VMEM((tiles, keypoints, half), jnp.bfloat16),
+                pltpu.VMEM((affinity.shape[0], keypoints, half), jnp.bfloat16),
                 pltpu.VMEM((images, keypoints, half), jnp.float32),
+                pltpu.SMEM(pairs.shape, jnp.int32),
+                pltpu.SemaphoreType.DMA(()),
             ],
             compiler_params=pltpu.CompilerParams(vmem_limit_bytes=8 * MIB),
             cost_estimate=pl.CostEstimate(flops=600000000, bytes_accessed=4000000, transcendentals=0),
             name="forward",
-        )(meta, affinity, *operands, terms)
+        )(pairs, affinity, *operands, terms)
 
     def scattered(parts):
         return parts[0], turned(parts[1], 1), turned(parts[3], -1), turned(parts[2], 2)
@@ -279,9 +294,8 @@
     right_sum = added(half, *right_parts[:1], crossed, *right_parts[1:])
     zl = gathered(left_sum)
     zr = gathered(right_sum)
-    own = 2 * tiles
-    result = project((own,), meta, factors, [(left_sum, right_sum)])
-    result = project((own + 3, own + 1, own + 2), meta, factors, list(zip(zl, zr)), result)
+    result = project((0,), factors, [(left_sum, right_sum)])
+    result = project((3, 1, 2), factors, list(zip(zl, zr)), result)
     return result
 
 

time: 68.9 us -> 69 us (level)
  Pallas kernels: 14.9 us -> 13.9 us
  local copies, waits for them, and re-layouts: 2.29 us -> 3.05 us
    pallas_call x3, Pallas kernels: 11.6 us -> 10.5 us  [the longest x2 8.7 us: project(): pl.pallas_call(functools.partial(project_kernel, ahead), out_shape=jax.Sh...]
    unnamed x8, local copies, waits for them, and re-layouts: 2.29 us -> 3.05 us
  transfers between devices with their start and end apart: 21 -> 21, of which waited for: 7 -> 7; matrix products, arithmetic and copies ran while one was open for 0% -> 0% of each run, Pallas kernels for 11% -> 10%
where the time goes in v2:
time: 69 us; the launch traced here: 68.8 us
  starting transfers between devices  36.9 us (53%)
  waiting for transfers between devices  14.7 us (21%)
  Pallas kernels  13.9 us (20%)
  local copies, waits for them, and re-layouts  3.05 us (4%)
    ppermute x15, starting transfers between devices, turned(): return lax.ppermute(x, 'rep', [(i, (i + by) % n) for i in range(n)])  24.5 us
    ppermute x15, waiting for transfers between devices, turned(): return lax.ppermute(x, 'rep', [(i, (i + by) % n) for i in range(n)])  14.7 us
    ppermute x3, starting transfers between devices, across(): return lax.ppermute(x, 'tiles', pairs + [(b, a) for a, b in pairs])  12.3 us
    pallas_call x2, Pallas kernels, project(): pl.pallas_call(functools.partial(project_kernel, ahead), out_shape=jax.Sh...  8.7 us
    unnamed x8, local copies, waits for them, and re-layouts  3.05 us
    pallas_call x2, Pallas kernels, forward(): pl.pallas_call(functools.partial(forward_kernel, start), out_shape=(shape...  2.92 us
    pallas_call x1, Pallas kernels, shards(): pl.pallas_call(backward_kernel, out_shape=(shape(images, keypoints, half,...  1.83 us
  transfers between devices with their start and end apart: 21, of which 7 were waited for; matrix products, arithmetic and copies ran while one was open for 0% of the time, Pallas kernels for 10%

profile of v2, /device:TPU:128, one launch (start us, length us, event | category | flops | bytes accessed | tf_op | source)
XLA Modules:
  0.0 68.8 jit_solution(506679829825175622)
XLA Ops:
  0.0 1.6 %copy-done.1 = f32[4,512,256]{2,1,0:T(8,128)S(1)} copy-done((f32[4,512,256]{2,1,0:T(8,128)S(1)}, f32[4,512,256]{2,1,0:T(8,128)}, u32[]{:S(2)}) %copy-start.1) | copy-done | bytes 2097176
  1.6 0.1 rounded.1
  1.7 1.5 %copy-done = bf16[4,512,512]{2,1,0:T(8,128)(2,1)S(1)} copy-done((bf16[4,512,512]{2,1,0:T(8,128)(2,1)S(1)}, bf16[4,512,512]{2,1,0:T(8,128)(2,1)}, u32[]{:S(2)}) %copy-start) | copy-done | bytes 2097176
  3.2 1.8 %backward.1 = (f32[4,512,128]{2,1,0:T(8,128)S(1)}, f32[4,512,128]{2,1,0:T(8,128)S(1)}, bf16[4,512,256]{2,1,0:T(8,128)(2,1)S(1)}, f32[512,256]{1,0:T(8,128)S(1)},...) custom-call(s32[2,4]{1,0:T(2,128)S(1)} %bitcast.1, ...), custom_call_target="tpu_custom_call" | custom-call | flops 600000000 | bytes 8000000 | tf_op jit(solution)/shard_map/backward/pallas_call | solution.py:230
  5.0 0.1 collective-permute-start.2
  5.1 1.7 %collective-permute-start.3 = (bf16[512,256]{1,0:T(8,128)(2,1)S(1)}, bf16[512,256]{1,0:T(8,128)(2,1)S(1)}, u32[]{:S(2)}, u32[]{:S(2)}) collective-permute-start(bf16[512,256]{1,0:T(8,128)(2,1)S(1)} %get-tuple-element.28), channel_id=1, source_target_pairs={{0,1},{1,2},{2,3},{3,0},{4,5},{5,6},{6,7},{7,4},{8,9},{9,10},{10,1... | collective-permute-start | bytes 786440 | tf_op jit(solution)/shard_map/ppermute | solution.py:39
  6.8 2.9 %collective-permute-start.4 = (bf16[512,256]{1,0:T(8,128)(2,1)S(1)}, bf16[512,256]{1,0:T(8,128)(2,1)S(1)}, u32[]{:S(2)}, u32[]{:S(2)}) collective-permute-start(bf16[512,256]{1,0:T(8,128)(2,1)S(1)} %get-tuple-element.29), channel_id=1, source_target_pairs={{0,2},{1,3},{2,0},{3,1},{4,6},{5,7},{6,4},{7,5},{8,10},{9,11},{10,... | collective-permute-start | bytes 786440 | tf_op jit(solution)/shard_map/ppermute | solution.py:39
  9.7 1.3 %collective-permute-start.5 = (bf16[512,256]{1,0:T(8,128)(2,1)S(1)}, bf16[512,256]{1,0:T(8,128)(2,1)S(1)}, u32[]{:S(2)}, u32[]{:S(2)}) collective-permute-start(bf16[512,256]{1,0:T(8,128)(2,1)S(1)} %get-tuple-element.30), channel_id=1, source_target_pairs={{0,3},{1,0},{2,1},{3,2},{4,7},{5,4},{6,5},{7,6},{8,11},{9,8},{10,9... | collective-permute-start | bytes 786440 | tf_op jit(solution)/shard_map/ppermute | solution.py:39
  11.0 0.0 collective-permute-start.11
  11.0 4.1 %collective-permute-done.3.refs_1_ = bf16[512,256]{1,0:T(8,128)(2,1)S(1)} collective-permute-done((bf16[512,256]{1,0:T(8,128)(2,1)S(1)}, bf16[512,256]{1,0:T(8,128)(2,1)S(1)}, u32[]{:S(2)}, u32[]{:S(2)}) %collective-permute-start.3) | collective-permute-done | bytes 262176 | tf_op jit(solution)/shard_map/ppermute | solution.py:39
  15.1 3.4 %collective-permute-start.12 = (bf16[4,512,128]{2,1,0:T(8,128)(2,1)S(1)}, bf16[4,512,128]{2,1,0:T(8,128)(2,1)S(1)}, u32[]{:S(2)}, u32[]{:S(2)}) collective-permute-start(bf16[4,512,128]{2,1,0:T(8,128)(2,1)S(1)} %get-tuple-element.23.right.rounded), channel_id=1, source_target_pairs={{4,8},{12,16},{20,24},{28,32},{36,40},{44,48},{52,56},{60,64},{68,... | collective-permute-start | bytes 1572872 | tf_op jit(solution)/shard_map/ppermute | solution.py:34
  18.5 3.4 %collective-permute-done.4.refs_2_ = bf16[512,256]{1,0:T(8,128)(2,1)S(1)} collective-permute-done((bf16[512,256]{1,0:T(8,128)(2,1)S(1)}, bf16[512,256]{1,0:T(8,128)(2,1)S(1)}, u32[]{:S(2)}, u32[]{:S(2)}) %collective-permute-start.4) | collective-permute-done | bytes 262176 | tf_op jit(solution)/shard_map/ppermute | solution.py:39
  21.9 0.0 collective-permute-start
  21.9 4.3 %collective-permute-start.1 = (bf16[4,512,128]{2,1,0:T(8,128)(2,1)S(1)}, bf16[4,512,128]{2,1,0:T(8,128)(2,1)S(1)}, u32[]{:S(2)}, u32[]{:S(2)}) collective-permute-start(bf16[4,512,128]{2,1,0:T(8,128)(2,1)S(1)} %get-tuple-element.22.left.rounded), channel_id=1, source_target_pairs={{4,8},{12,16},{20,24},{28,32},{36,40},{44,48},{52,56},{60,64},{68,... | collective-permute-start | bytes 1572872 | tf_op jit(solution)/shard_map/ppermute | solution.py:34
  26.2 0.1 added.3
  26.4 0.0 collective-permute-done.11.from_mate
  26.4 4.6 %collective-permute-start.6 = (bf16[512,256]{1,0:T(8,128)(2,1)S(1)}, bf16[512,256]{1,0:T(8,128)(2,1)S(1)}, u32[]{:S(2)}, u32[]{:S(2)}) collective-permute-start(bf16[512,256]{1,0:T(8,128)(2,1)S(1)} %added.3), channel_id=1, source_target_pairs={{4,8},{12,16},{20,24},{28,32},{36,40},{44,48},{52,56},{60,64},{68,... | collective-permute-start | bytes 786440 | tf_op jit(solution)/shard_map/ppermute | solution.py:34
  30.9 0.0 collective-permute-done.12.from_across
  30.9 0.0 collective-permute-done.2.terms
  31.0 1.5 %forward.3 = (f32[512,128]{1,0:T(8,128)S(1)}, bf16[512,128]{1,0:T(8,128)(2,1)S(1)}, bf16[512,128]{1,0:T(8,128)(2,1)S(1)}, bf16[512,128]{1,0:T(8,128)(2,1)S(1)}) custom-call(s32[2,4]{1,0:T(2,128)S(1)} %bitcast.2, bf16[4,512,512]{2,1,0:T(8,128)(2,1)S(1)} %copy-done, bf16[4,512,128]{2,1,0:T(8,128)(2,1)S(1)} %get-tuple-element.23.right.rounded, ...), custom_call_target="tpu_custom_call" | custom-call | flops 600000000 | bytes 4000000 | tf_op jit(solution)/shard_map/forward/pallas_call | solution.py:267
  32.4 1.2 %collective-permute-start.13 = (bf16[512,128]{1,0:T(8,128)(2,1)S(1)}, bf16[512,128]{1,0:T(8,128)(2,1)S(1)}, u32[]{:S(2)}, u32[]{:S(2)}) collective-permute-start(bf16[512,128]{1,0:T(8,128)(2,1)S(1)} %get-tuple-element.36), channel_id=1, source_target_pairs={{0,1},{1,2},{2,3},{3,0},{4,5},{5,6},{6,7},{7,4},{8,9},{9,10},{10,1... | collective-permute-start | bytes 393224 | tf_op jit(solution)/shard_map/ppermute | solution.py:39
  33.6 2.1 %collective-permute-start.14 = (bf16[512,128]{1,0:T(8,128)(2,1)S(1)}, bf16[512,128]{1,0:T(8,128)(2,1)S(1)}, u32[]{:S(2)}, u32[]{:S(2)}) collective-permute-start(bf16[512,128]{1,0:T(8,128)(2,1)S(1)} %get-tuple-element.37), channel_id=1, source_target_pairs={{0,3},{1,0},{2,1},{3,2},{4,7},{5,4},{6,5},{7,6},{8,11},{9,8},{10,9... | collective-permute-start | bytes 393224 | tf_op jit(solution)/shard_map/ppermute | solution.py:39
  35.8 4.3 %collective-permute-start.15 = (bf16[512,128]{1,0:T(8,128)(2,1)S(1)}, bf16[512,128]{1,0:T(8,128)(2,1)S(1)}, u32[]{:S(2)}, u32[]{:S(2)}) collective-permute-start(bf16[512,128]{1,0:T(8,128)(2,1)S(1)} %get-tuple-element.38), channel_id=1, source_target_pairs={{0,2},{1,3},{2,0},{3,1},{4,6},{5,7},{6,4},{7,5},{8,10},{9,11},{10,... | collective-permute-start | bytes 393224 | tf_op jit(solution)/shard_map/ppermute | solution.py:39
  40.0 0.0 collective-permute-done.1.from_across
  40.0 1.5 %forward.2 = (f32[512,128]{1,0:T(8,128)S(1)}, bf16[512,128]{1,0:T(8,128)(2,1)S(1)}, bf16[512,128]{1,0:T(8,128)(2,1)S(1)}, bf16[512,128]{1,0:T(8,128)(2,1)S(1)}) custom-call(s32[2,4]{1,0:T(2,128)S(1)} %bitcast.3, bf16[4,512,512]{2,1,0:T(8,128)(2,1)S(1)} %copy-done, bf16[4,512,128]{2,1,0:T(8,128)(2,1)S(1)} %get-tuple-element.22.left.rounded, ...), custom_call_target="tpu_custom_call" | custom-call | flops 600000000 | bytes 4000000 | tf_op jit(solution)/shard_map/forward/pallas_call | solution.py:267
  41.5 0.0 copy-start.2
  41.5 0.1 collective-permute-start.7
  41.6 0.0 collective-permute-done.6.refs_1_
  41.6 3.2 %collective-permute-start.8 = (bf16[512,128]{1,0:T(8,128)(2,1)S(1)}, bf16[512,128]{1,0:T(8,128)(2,1)S(1)}, u32[]{:S(2)}, u32[]{:S(2)}) collective-permute-start(bf16[512,128]{1,0:T(8,128)(2,1)S(1)} %get-tuple-element.32), channel_id=1, source_target_pairs={{0,3},{1,0},{2,1},{3,2},{4,7},{5,4},{6,5},{7,6},{8,11},{9,8},{10,9... | collective-permute-start | bytes 393224 | tf_op jit(solution)/shard_map/ppermute | solution.py:39
  44.8 0.8 %collective-permute-start.9 = (bf16[512,128]{1,0:T(8,128)(2,1)S(1)}, bf16[512,128]{1,0:T(8,128)(2,1)S(1)}, u32[]{:S(2)}, u32[]{:S(2)}) collective-permute-start(bf16[512,128]{1,0:T(8,128)(2,1)S(1)} %get-tuple-element.33), channel_id=1, source_target_pairs={{0,2},{1,3},{2,0},{3,1},{4,6},{5,7},{6,4},{7,5},{8,10},{9,11},{10,... | collective-permute-start | bytes 393224 | tf_op jit(solution)/shard_map/ppermute | solution.py:39
  45.7 0.0 collective-permute-done.14.refs_3_
  45.7 0.0 collective-permute-done.15.refs_4_
  45.7 0.1 added.5.rest_1_
  45.8 0.9 %collective-permute-start.16 = (bf16[512,128]{1,0:T(8,128)(2,1)S(1)}, bf16[512,128]{1,0:T(8,128)(2,1)S(1)}, u32[]{:S(2)}, u32[]{:S(2)}) collective-permute-start(bf16[512,128]{1,0:T(8,128)(2,1)S(1)} %added.5.rest_1_), channel_id=1, source_target_pairs={{0,1},{1,2},{2,3},{3,0},{4,5},{5,6},{6,7},{7,4},{8,9},{9,10},{10,1... | collective-permute-start | bytes 393224 | tf_op jit(solution)/shard_map/ppermute | solution.py:39
  46.7 2.6 %collective-permute-start.18 = (bf16[512,128]{1,0:T(8,128)(2,1)S(1)}, bf16[512,128]{1,0:T(8,128)(2,1)S(1)}, u32[]{:S(2)}, u32[]{:S(2)}) collective-permute-start(bf16[512,128]{1,0:T(8,128)(2,1)S(1)} %added.5.rest_1_), channel_id=1, source_target_pairs={{0,3},{1,0},{2,1},{3,2},{4,7},{5,4},{6,5},{7,6},{8,11},{9,8},{10,9... | collective-permute-start | bytes 393224 | tf_op jit(solution)/shard_map/ppermute | solution.py:39
  49.3 1.5 %collective-permute-done.7.refs_2_ = bf16[512,128]{1,0:T(8,128)(2,1)S(1)} collective-permute-done((bf16[512,128]{1,0:T(8,128)(2,1)S(1)}, bf16[512,128]{1,0:T(8,128)(2,1)S(1)}, u32[]{:S(2)}, u32[]{:S(2)}) %collective-permute-start.7) | collective-permute-done | bytes 131104 | tf_op jit(solution)/shard_map/ppermute | solution.py:39
  50.7 0.0 collective-permute-start.20
  50.8 0.7 %collective-permute-done.8.refs_3_ = bf16[512,128]{1,0:T(8,128)(2,1)S(1)} collective-permute-done((bf16[512,128]{1,0:T(8,128)(2,1)S(1)}, bf16[512,128]{1,0:T(8,128)(2,1)S(1)}, u32[]{:S(2)}, u32[]{:S(2)}) %collective-permute-start.8) | collective-permute-done | bytes 131104 | tf_op jit(solution)/shard_map/ppermute | solution.py:39
  51.5 1.3 %collective-permute-done.9.refs_4_ = bf16[512,128]{1,0:T(8,128)(2,1)S(1)} collective-permute-done((bf16[512,128]{1,0:T(8,128)(2,1)S(1)}, bf16[512,128]{1,0:T(8,128)(2,1)S(1)}, u32[]{:S(2)}, u32[]{:S(2)}) %collective-permute-start.9) | collective-permute-done | bytes 131104 | tf_op jit(solution)/shard_map/ppermute | solution.py:39
  52.7 0.1 added.4.rest_0_
  52.8 0.8 %collective-permute-start.10 = (bf16[512,128]{1,0:T(8,128)(2,1)S(1)}, bf16[512,128]{1,0:T(8,128)(2,1)S(1)}, u32[]{:S(2)}, u32[]{:S(2)}) collective-permute-start(bf16[512,128]{1,0:T(8,128)(2,1)S(1)} %added.4.rest_0_), channel_id=1, source_target_pairs={{0,1},{1,2},{2,3},{3,0},{4,5},{5,6},{6,7},{7,4},{8,9},{9,10},{10,1... | collective-permute-start | bytes 393224 | tf_op jit(solution)/shard_map/ppermute | solution.py:39
  53.6 2.5 %collective-permute-start.17 = (bf16[512,128]{1,0:T(8,128)(2,1)S(1)}, bf16[512,128]{1,0:T(8,128)(2,1)S(1)}, u32[]{:S(2)}, u32[]{:S(2)}) collective-permute-start(bf16[512,128]{1,0:T(8,128)(2,1)S(1)} %added.4.rest_0_), channel_id=1, source_target_pairs={{0,3},{1,0},{2,1},{3,2},{4,7},{5,4},{6,5},{7,6},{8,11},{9,8},{10,9... | collective-permute-start | bytes 393224 | tf_op jit(solution)/shard_map/ppermute | solution.py:39
  56.1 1.2 %collective-permute-done.16.rest_1_ = bf16[512,128]{1,0:T(8,128)(2,1)S(1)} collective-permute-done((bf16[512,128]{1,0:T(8,128)(2,1)S(1)}, bf16[512,128]{1,0:T(8,128)(2,1)S(1)}, u32[]{:S(2)}, u32[]{:S(2)}) %collective-permute-start.16) | collective-permute-done | bytes 131104 | tf_op jit(solution)/shard_map/ppermute | solution.py:39
  57.3 3.8 %project.2.rest_6_ = f32[4,512,256]{2,1,0:T(8,128)} custom-call(f32[4,512,256]{2,1,0:T(8,128)S(1)} %copy-done.2, bf16[512,128]{1,0:T(8,128)(2,1)S(1)} %added.4.rest_0_, bf16[512,128]{1,0:T(8,128)(2,1)S(1)} %added.5.rest_1_), custom_call_target="tpu_custom_call" | custom-call | flops 2000000000 | bytes 2000000 | tf_op jit(solution)/shard_map/project/pallas_call | solution.py:195
  61.2 0.0 collective-permute-done.20.rest_5_
  61.2 0.0 collective-permute-done.10.rest_0_
  61.2 2.6 %collective-permute-done.19.rest_4_ = bf16[512,128]{1,0:T(8,128)(2,1)S(1)} collective-permute-done((bf16[512,128]{1,0:T(8,128)(2,1)S(1)}, bf16[512,128]{1,0:T(8,128)(2,1)S(1)}, u32[]{:S(2)}, u32[]{:S(2)}) %collective-permute-start.19) | collective-permute-done | bytes 131104 | tf_op jit(solution)/shard_map/ppermute | solution.py:39
  63.8 4.9 %project.3 = f32[4,512,256]{2,1,0:T(8,128)} custom-call(f32[4,512,256]{2,1,0:T(8,128)S(1)} %copy-done.2, bf16[512,128]{1,0:T(8,128)(2,1)S(1)} %collective-permute-done.10.rest_0_, bf16[512,128]{1,0:T(8,128)(2,1)S(1)} %collective-permute-done.16.rest_1_, bf16[512,128]{1,0:T(8,128)(2,1)S(1)} %collective-permute-done.17.rest_2_, ...), custom_call_target="tpu_custom_call", output_to_operand_aliasing={{}: (7, {})} | custom-call | flops 6000000000 | bytes 6000000 | tf_op jit(solution)/shard_map/project/pallas_call | solution.py:195
  (11 shorter events, 0.0 us)
Async XLA Ops:
  0.0 1.6 %copy-start.1 = (f32[4,512,256]{2,1,0:T(8,128)S(1)}, f32[4,512,256]{2,1,0:T(8,128)}, u32[]{:S(2)}) copy-start(f32[4,512,256]{2,1,0:T(8,128)} %factors.3) | copy-start | bytes 6291460
  1.6 1.6 %copy-start = (bf16[4,512,512]{2,1,0:T(8,128)(2,1)S(1)}, bf16[4,512,512]{2,1,0:T(8,128)(2,1)}, u32[]{:S(2)}) copy-start(bf16[4,512,512]{2,1,0:T(8,128)(2,1)} %affinity.5) | copy-start | bytes 6291460
  1.6 1.6 %copy-start.3 = (s32[4,2]{0,1:T(2,128)S(1)}, s32[4,2]{0,1:T(2,128)}, u32[]{:S(2)}) copy-start(s32[4,2]{0,1:T(2,128)} %param.4) | copy-start | bytes 100
  5.0 25.9 %collective-permute-start.2 = (bf16[4,512,256]{2,1,0:T(8,128)(2,1)S(1)}, bf16[4,512,256]{2,1,0:T(8,128)(2,1)S(1)}, u32[]{:S(2)}, u32[]{:S(2)}) collective-permute-start(bf16[4,512,256]{2,1,0:T(8,128)(2,1)S(1)} %get-tuple-element.25), channel_id=1, source_target_pairs={{0,4},{4,0},{8,12},{12,8},{16,20},{20,16},{24,28},{28,24},{32,36},... | collective-permute-start | bytes 3145736 | tf_op jit(solution)/shard_map/ppermute | solution.py:28
  5.1 10.0 %collective-permute-start.3 = (bf16[512,256]{1,0:T(8,128)(2,1)S(1)}, bf16[512,256]{1,0:T(8,128)(2,1)S(1)}, u32[]{:S(2)}, u32[]{:S(2)}) collective-permute-start(bf16[512,256]{1,0:T(8,128)(2,1)S(1)} %get-tuple-element.28), channel_id=1, source_target_pairs={{0,1},{1,2},{2,3},{3,0},{4,5},{5,6},{6,7},{7,4},{8,9},{9,10},{10,1... | collective-permute-start | bytes 786440 | tf_op jit(solution)/shard_map/ppermute | solution.py:39
  6.8 15.1 %collective-permute-start.4 = (bf16[512,256]{1,0:T(8,128)(2,1)S(1)}, bf16[512,256]{1,0:T(8,128)(2,1)S(1)}, u32[]{:S(2)}, u32[]{:S(2)}) collective-permute-start(bf16[512,256]{1,0:T(8,128)(2,1)S(1)} %get-tuple-element.29), channel_id=1, source_target_pairs={{0,2},{1,3},{2,0},{3,1},{4,6},{5,7},{6,4},{7,5},{8,10},{9,11},{10,... | collective-permute-start | bytes 786440 | tf_op jit(solution)/shard_map/ppermute | solution.py:39
  9.7 12.2 %collective-permute-start.5 = (bf16[512,256]{1,0:T(8,128)(2,1)S(1)}, bf16[512,256]{1,0:T(8,128)(2,1)S(1)}, u32[]{:S(2)}, u32[]{:S(2)}) collective-permute-start(bf16[512,256]{1,0:T(8,128)(2,1)S(1)} %get-tuple-element.30), channel_id=1, source_target_pairs={{0,3},{1,0},{2,1},{3,2},{4,7},{5,4},{6,5},{7,6},{8,11},{9,8},{10,9... | collective-permute-start | bytes 786440 | tf_op jit(solution)/shard_map/ppermute | solution.py:39
  11.0 15.3 %collective-permute-start.11 = (bf16[4,512,128]{2,1,0:T(8,128)(2,1)S(1)}, bf16[4,512,128]{2,1,0:T(8,128)(2,1)S(1)}, u32[]{:S(2)}, u32[]{:S(2)}) collective-permute-start(bf16[4,512,128]{2,1,0:T(8,128)(2,1)S(1)} %get-tuple-element.23.right.rounded), channel_id=1, source_target_pairs={{0,4},{4,0},{8,12},{12,8},{16,20},{20,16},{24,28},{28,24},{32,36},... | collective-permute-start | bytes 1572872 | tf_op jit(solution)/shard_map/ppermute | solution.py:28
  15.1 15.8 %collective-permute-start.12 = (bf16[4,512,128]{2,1,0:T(8,128)(2,1)S(1)}, bf16[4,512,128]{2,1,0:T(8,128)(2,1)S(1)}, u32[]{:S(2)}, u32[]{:S(2)}) collective-permute-start(bf16[4,512,128]{2,1,0:T(8,128)(2,1)S(1)} %get-tuple-element.23.right.rounded), channel_id=1, source_target_pairs={{4,8},{12,16},{20,24},{28,32},{36,40},{44,48},{52,56},{60,64},{68,... | collective-permute-start | bytes 1572872 | tf_op jit(solution)/shard_map/ppermute | solution.py:34
  21.9 13.8 %collective-permute-start = (bf16[4,512,128]{2,1,0:T(8,128)(2,1)S(1)}, bf16[4,512,128]{2,1,0:T(8,128)(2,1)S(1)}, u32[]{:S(2)}, u32[]{:S(2)}) collective-permute-start(bf16[4,512,128]{2,1,0:T(8,128)(2,1)S(1)} %get-tuple-element.22.left.rounded), channel_id=1, source_target_pairs={{0,4},{4,0},{8,12},{12,8},{16,20},{20,16},{24,28},{28,24},{32,36},... | collective-permute-start | bytes 1572872 | tf_op jit(solution)/shard_map/ppermute | solution.py:28
  21.9 18.1 %collective-permute-start.1 = (bf16[4,512,128]{2,1,0:T(8,128)(2,1)S(1)}, bf16[4,512,128]{2,1,0:T(8,128)(2,1)S(1)}, u32[]{:S(2)}, u32[]{:S(2)}) collective-permute-start(bf16[4,512,128]{2,1,0:T(8,128)(2,1)S(1)} %get-tuple-element.22.left.rounded), channel_id=1, source_target_pairs={{4,8},{12,16},{20,24},{28,32},{36,40},{44,48},{52,56},{60,64},{68,... | collective-permute-start | bytes 1572872 | tf_op jit(solution)/shard_map/ppermute | solution.py:34
  26.4 15.2 %collective-permute-start.6 = (bf16[512,256]{1,0:T(8,128)(2,1)S(1)}, bf16[512,256]{1,0:T(8,128)(2,1)S(1)}, u32[]{:S(2)}, u32[]{:S(2)}) collective-permute-start(bf16[512,256]{1,0:T(8,128)(2,1)S(1)} %added.3), channel_id=1, source_target_pairs={{4,8},{12,16},{20,24},{28,32},{36,40},{44,48},{52,56},{60,64},{68,... | collective-permute-start | bytes 786440 | tf_op jit(solution)/shard_map/ppermute | solution.py:34
  32.4 12.4 %collective-permute-start.13 = (bf16[512,128]{1,0:T(8,128)(2,1)S(1)}, bf16[512,128]{1,0:T(8,128)(2,1)S(1)}, u32[]{:S(2)}, u32[]{:S(2)}) collective-permute-start(bf16[512,128]{1,0:T(8,128)(2,1)S(1)} %get-tuple-element.36), channel_id=1, source_target_pairs={{0,1},{1,2},{2,3},{3,0},{4,5},{5,6},{6,7},{7,4},{8,9},{9,10},{10,1... | collective-permute-start | bytes 393224 | tf_op jit(solution)/shard_map/ppermute | solution.py:39
  33.6 12.0 %collective-permute-start.14 = (bf16[512,128]{1,0:T(8,128)(2,1)S(1)}, bf16[512,128]{1,0:T(8,128)(2,1)S(1)}, u32[]{:S(2)}, u32[]{:S(2)}) collective-permute-start(bf16[512,128]{1,0:T(8,128)(2,1)S(1)} %get-tuple-element.37), channel_id=1, source_target_pairs={{0,3},{1,0},{2,1},{3,2},{4,7},{5,4},{6,5},{7,6},{8,11},{9,8},{10,9... | collective-permute-start | bytes 393224 | tf_op jit(solution)/shard_map/ppermute | solution.py:39
  35.8 9.9 %collective-permute-start.15 = (bf16[512,128]{1,0:T(8,128)(2,1)S(1)}, bf16[512,128]{1,0:T(8,128)(2,1)S(1)}, u32[]{:S(2)}, u32[]{:S(2)}) collective-permute-start(bf16[512,128]{1,0:T(8,128)(2,1)S(1)} %get-tuple-element.38), channel_id=1, source_target_pairs={{0,2},{1,3},{2,0},{3,1},{4,6},{5,7},{6,4},{7,5},{8,10},{9,11},{10,... | collective-permute-start | bytes 393224 | tf_op jit(solution)/shard_map/ppermute | solution.py:39
  41.5 15.8 %copy-start.2 = (f32[4,512,256]{2,1,0:T(8,128)S(1)}, f32[4,512,256]{2,1,0:T(8,128)}, u32[]{:S(2)}) copy-start(f32[4,512,256]{2,1,0:T(8,128)} %factors.3) | copy-start | bytes 6291460
  41.5 9.2 %collective-permute-start.7 = (bf16[512,128]{1,0:T(8,128)(2,1)S(1)}, bf16[512,128]{1,0:T(8,128)(2,1)S(1)}, u32[]{:S(2)}, u32[]{:S(2)}) collective-permute-start(bf16[512,128]{1,0:T(8,128)(2,1)S(1)} %get-tuple-element.31), channel_id=1, source_target_pairs={{0,1},{1,2},{2,3},{3,0},{4,5},{5,6},{6,7},{7,4},{8,9},{9,10},{10,1... | collective-permute-start | bytes 393224 | tf_op jit(solution)/shard_map/ppermute | solution.py:39
  41.6 9.8 %collective-permute-start.8 = (bf16[512,128]{1,0:T(8,128)(2,1)S(1)}, bf16[512,128]{1,0:T(8,128)(2,1)S(1)}, u32[]{:S(2)}, u32[]{:S(2)}) collective-permute-start(bf16[512,128]{1,0:T(8,128)(2,1)S(1)} %get-tuple-element.32), channel_id=1, source_target_pairs={{0,3},{1,0},{2,1},{3,2},{4,7},{5,4},{6,5},{7,6},{8,11},{9,8},{10,9... | collective-permute-start | bytes 393224 | tf_op jit(solution)/shard_map/ppermute | solution.py:39
  44.8 7.9 %collective-permute-start.9 = (bf16[512,128]{1,0:T(8,128)(2,1)S(1)}, bf16[512,128]{1,0:T(8,128)(2,1)S(1)}, u32[]{:S(2)}, u32[]{:S(2)}) collective-permute-start(bf16[512,128]{1,0:T(8,128)(2,1)S(1)} %get-tuple-element.33), channel_id=1, source_target_pairs={{0,2},{1,3},{2,0},{3,1},{4,6},{5,7},{6,4},{7,5},{8,10},{9,11},{10,... | collective-permute-start | bytes 393224 | tf_op jit(solution)/shard_map/ppermute | solution.py:39
  45.8 11.6 %collective-permute-start.16 = (bf16[512,128]{1,0:T(8,128)(2,1)S(1)}, bf16[512,128]{1,0:T(8,128)(2,1)S(1)}, u32[]{:S(2)}, u32[]{:S(2)}) collective-permute-start(bf16[512,128]{1,0:T(8,128)(2,1)S(1)} %added.5.rest_1_), channel_id=1, source_target_pairs={{0,1},{1,2},{2,3},{3,0},{4,5},{5,6},{6,7},{7,4},{8,9},{9,10},{10,1... | collective-permute-start | bytes 393224 | tf_op jit(solution)/shard_map/ppermute | solution.py:39
  46.7 14.5 %collective-permute-start.18 = (bf16[512,128]{1,0:T(8,128)(2,1)S(1)}, bf16[512,128]{1,0:T(8,128)(2,1)S(1)}, u32[]{:S(2)}, u32[]{:S(2)}) collective-permute-start(bf16[512,128]{1,0:T(8,128)(2,1)S(1)} %added.5.rest_1_), channel_id=1, source_target_pairs={{0,3},{1,0},{2,1},{3,2},{4,7},{5,4},{6,5},{7,6},{8,11},{9,8},{10,9... | collective-permute-start | bytes 393224 | tf_op jit(solution)/shard_map/ppermute | solution.py:39
  50.7 10.5 %collective-permute-start.20 = (bf16[512,128]{1,0:T(8,128)(2,1)S(1)}, bf16[512,128]{1,0:T(8,128)(2,1)S(1)}, u32[]{:S(2)}, u32[]{:S(2)}) collective-permute-start(bf16[512,128]{1,0:T(8,128)(2,1)S(1)} %added.5.rest_1_), channel_id=1, source_target_pairs={{0,2},{1,3},{2,0},{3,1},{4,6},{5,7},{6,4},{7,5},{8,10},{9,11},{10,... | collective-permute-start | bytes 393224 | tf_op jit(solution)/shard_map/ppermute | solution.py:39
  52.8 8.4 %collective-permute-start.10 = (bf16[512,128]{1,0:T(8,128)(2,1)S(1)}, bf16[512,128]{1,0:T(8,128)(2,1)S(1)}, u32[]{:S(2)}, u32[]{:S(2)}) collective-permute-start(bf16[512,128]{1,0:T(8,128)(2,1)S(1)} %added.4.rest_0_), channel_id=1, source_target_pairs={{0,1},{1,2},{2,3},{3,0},{4,5},{5,6},{6,7},{7,4},{8,9},{9,10},{10,1... | collective-permute-start | bytes 393224 | tf_op jit(solution)/shard_map/ppermute | solution.py:39
  53.6 7.6 %collective-permute-start.17 = (bf16[512,128]{1,0:T(8,128)(2,1)S(1)}, bf16[512,128]{1,0:T(8,128)(2,1)S(1)}, u32[]{:S(2)}, u32[]{:S(2)}) collective-permute-start(bf16[512,128]{1,0:T(8,128)(2,1)S(1)} %added.4.rest_0_), channel_id=1, source_target_pairs={{0,3},{1,0},{2,1},{3,2},{4,7},{5,4},{6,5},{7,6},{8,11},{9,8},{10,9... | collective-permute-start | bytes 393224 | tf_op jit(solution)/shard_map/ppermute | solution.py:39
  57.3 6.5 %collective-permute-start.19 = (bf16[512,128]{1,0:T(8,128)(2,1)S(1)}, bf16[512,128]{1,0:T(8,128)(2,1)S(1)}, u32[]{:S(2)}, u32[]{:S(2)}) collective-permute-start(bf16[512,128]{1,0:T(8,128)(2,1)S(1)} %added.4.rest_0_), channel_id=1, source_target_pairs={{0,2},{1,3},{2,0},{3,1},{4,6},{5,7},{6,4},{7,5},{8,10},{9,11},{10,... | collective-permute-start | bytes 393224 | tf_op jit(solution)/shard_map/ppermute | solution.py:39

commit v3 on v2

--- a/solution.py
+++ b/solution.py
@@ -10,8 +10,7 @@
 
 
 P_SIZE = 512
-NS_STEPS = 6
-WIDE_STEPS = 1
+KEEP = (0.0, 0.0, 0.0, 0.5, 0.5, 1.0)
 
 epsilon = 1e-06
 start_scale = 0.25
@@ -141,9 +140,8 @@
     refs[-1][...] = total.astype(refs[-1].dtype)
 
 
-def split(x):
-    high = x.astype(jnp.bfloat16)
-    return high, (x - high.astype(jnp.float32)).astype(jnp.bfloat16)
+def same_index(size):
+    return lax.broadcasted_iota(jnp.int32, (size, size), 0) == lax.broadcasted_iota(jnp.int32, (size, size), 1)
 
 
 def project_kernel(ahead, factors, *rest):
@@ -157,20 +155,14 @@
         squares = jnp.sum(jnp.sum(x * x, axis=0, keepdims=True), axis=1, keepdims=True)
         x = x * (start_scale * math.sqrt(x.shape[1]) * lax.rsqrt(squares + epsilon))
         ys.append(x.T)
-    for step in range(NS_STEPS):
-        if step < NS_STEPS - WIDE_STEPS:
-            highs = [y.astype(jnp.bfloat16) for y in ys]
-            grams = [dot(h, h, NT).astype(jnp.bfloat16) for h in highs]
-            changes = [dot(g, h) for g, h in zip(grams, highs)]
-        else:
-            halves = [split(y) for y in ys]
-            mixed = [dot(high, low, NT) for high, low in halves]
-            grams = [split(dot(high, high, NT) + (m + m.T)) for (high, low), m in zip(halves, mixed)]
-            changes = [
-                dot(gh, high) + (dot(gl, high) + dot(gh, low))
-                for (gh, gl), (high, low) in zip(grams, halves)
-            ]
-        ys = [1.5 * y - 0.5 * c for y, c in zip(ys, changes)]
+    diagonal = same_index(ys[0].shape[0])
+    for keep in KEEP:
+        highs = [y.astype(jnp.bfloat16) for y in ys]
+        grams = [dot(h, h, NT) for h in highs]
+        if keep:
+            grams = [g - jnp.where(diagonal, keep, 0.0) for g in grams]
+        changes = [dot(g.astype(jnp.bfloat16), h) for g, h in zip(grams, highs)]
+        ys = [(1.5 - 0.5 * keep) * y - 0.5 * c for y, c in zip(ys, changes)]
     copies = []
     for k, y in enumerate(ys):
         held[k] = (y * math.sqrt(P_SIZE)).T

time: 69 us -> 68.6 us (level)
  Pallas kernels: 13.9 us -> 13.1 us
    pallas_call x2, Pallas kernels: 8.7 us -> 7.97 us  [project(): pl.pallas_call(functools.partial(project_kernel, ahead), out_shape=jax.Sh...]
where the time goes in v3:
time: 68.6 us; the launch traced here: 68.4 us
  starting transfers between devices  36.9 us (54%)
  waiting for transfers between devices  15 us (22%)
  Pallas kernels  13.1 us (19%)
  local copies, waits for them, and re-layouts  3.05 us (4%)
    ppermute x15, starting transfers between devices, turned(): return lax.ppermute(x, 'rep', [(i, (i + by) % n) for i in range(n)])  24.5 us
    ppermute x15, waiting for transfers between devices, turned(): return lax.ppermute(x, 'rep', [(i, (i + by) % n) for i in range(n)])  15 us
    ppermute x3, starting transfers between devices, across(): return lax.ppermute(x, 'tiles', pairs + [(b, a) for a, b in pairs])  12.3 us
    pallas_call x2, Pallas kernels, project(): pl.pallas_call(functools.partial(project_kernel, ahead), out_shape=jax.Sh...  7.97 us
    unnamed x8, local copies, waits for them, and re-layouts  3.05 us
    pallas_call x2, Pallas kernels, forward(): pl.pallas_call(functools.partial(forward_kernel, start), out_shape=(shape...  2.92 us
    pallas_call x1, Pallas kernels, shards(): pl.pallas_call(backward_kernel, out_shape=(shape(images, keypoints, half,...  1.83 us
  transfers between devices with their start and end apart: 21, of which 7 were waited for; matrix products, arithmetic and copies ran while one was open for 0% of the time, Pallas kernels for 10%

profile of v3, /device:TPU:128, one launch (start us, length us, event | category | flops | bytes accessed | tf_op | source)
XLA Modules:
  0.0 68.4 jit_solution(13439439412145749446)
XLA Ops:
  0.0 1.6 %copy-done.1 = f32[4,512,256]{2,1,0:T(8,128)S(1)} copy-done((f32[4,512,256]{2,1,0:T(8,128)S(1)}, f32[4,512,256]{2,1,0:T(8,128)}, u32[]{:S(2)}) %copy-start.1) | copy-done | bytes 2097176
  1.6 0.1 rounded.1
  1.7 1.5 %copy-done = bf16[4,512,512]{2,1,0:T(8,128)(2,1)S(1)} copy-done((bf16[4,512,512]{2,1,0:T(8,128)(2,1)S(1)}, bf16[4,512,512]{2,1,0:T(8,128)(2,1)}, u32[]{:S(2)}) %copy-start) | copy-done | bytes 2097176
  3.2 1.8 %backward.1 = (f32[4,512,128]{2,1,0:T(8,128)S(1)}, f32[4,512,128]{2,1,0:T(8,128)S(1)}, bf16[4,512,256]{2,1,0:T(8,128)(2,1)S(1)}, f32[512,256]{1,0:T(8,128)S(1)},...) custom-call(s32[2,4]{1,0:T(2,128)S(1)} %bitcast.1, ...), custom_call_target="tpu_custom_call" | custom-call | flops 600000000 | bytes 8000000 | tf_op jit(solution)/shard_map/backward/pallas_call | solution.py:222
  5.0 0.1 collective-permute-start.2
  5.1 1.7 %collective-permute-start.3 = (bf16[512,256]{1,0:T(8,128)(2,1)S(1)}, bf16[512,256]{1,0:T(8,128)(2,1)S(1)}, u32[]{:S(2)}, u32[]{:S(2)}) collective-permute-start(bf16[512,256]{1,0:T(8,128)(2,1)S(1)} %get-tuple-element.28), channel_id=1, source_target_pairs={{0,1},{1,2},{2,3},{3,0},{4,5},{5,6},{6,7},{7,4},{8,9},{9,10},{10,1... | collective-permute-start | bytes 786440 | tf_op jit(solution)/shard_map/ppermute | solution.py:38
  6.8 2.9 %collective-permute-start.4 = (bf16[512,256]{1,0:T(8,128)(2,1)S(1)}, bf16[512,256]{1,0:T(8,128)(2,1)S(1)}, u32[]{:S(2)}, u32[]{:S(2)}) collective-permute-start(bf16[512,256]{1,0:T(8,128)(2,1)S(1)} %get-tuple-element.29), channel_id=1, source_target_pairs={{0,2},{1,3},{2,0},{3,1},{4,6},{5,7},{6,4},{7,5},{8,10},{9,11},{10,... | collective-permute-start | bytes 786440 | tf_op jit(solution)/shard_map/ppermute | solution.py:38
  9.7 1.3 %collective-permute-start.5 = (bf16[512,256]{1,0:T(8,128)(2,1)S(1)}, bf16[512,256]{1,0:T(8,128)(2,1)S(1)}, u32[]{:S(2)}, u32[]{:S(2)}) collective-permute-start(bf16[512,256]{1,0:T(8,128)(2,1)S(1)} %get-tuple-element.30), channel_id=1, source_target_pairs={{0,3},{1,0},{2,1},{3,2},{4,7},{5,4},{6,5},{7,6},{8,11},{9,8},{10,9... | collective-permute-start | bytes 786440 | tf_op jit(solution)/shard_map/ppermute | solution.py:38
  11.0 0.0 collective-permute-start.11
  11.0 4.1 %collective-permute-done.3.refs_1_ = bf16[512,256]{1,0:T(8,128)(2,1)S(1)} collective-permute-done((bf16[512,256]{1,0:T(8,128)(2,1)S(1)}, bf16[512,256]{1,0:T(8,128)(2,1)S(1)}, u32[]{:S(2)}, u32[]{:S(2)}) %collective-permute-start.3) | collective-permute-done | bytes 262176 | tf_op jit(solution)/shard_map/ppermute | solution.py:38
  15.1 3.4 %collective-permute-start.12 = (bf16[4,512,128]{2,1,0:T(8,128)(2,1)S(1)}, bf16[4,512,128]{2,1,0:T(8,128)(2,1)S(1)}, u32[]{:S(2)}, u32[]{:S(2)}) collective-permute-start(bf16[4,512,128]{2,1,0:T(8,128)(2,1)S(1)} %get-tuple-element.23.right.rounded), channel_id=1, source_target_pairs={{4,8},{12,16},{20,24},{28,32},{36,40},{44,48},{52,56},{60,64},{68,... | collective-permute-start | bytes 1572872 | tf_op jit(solution)/shard_map/ppermute | solution.py:33
  18.5 3.4 %collective-permute-done.4.refs_2_ = bf16[512,256]{1,0:T(8,128)(2,1)S(1)} collective-permute-done((bf16[512,256]{1,0:T(8,128)(2,1)S(1)}, bf16[512,256]{1,0:T(8,128)(2,1)S(1)}, u32[]{:S(2)}, u32[]{:S(2)}) %collective-permute-start.4) | collective-permute-done | bytes 262176 | tf_op jit(solution)/shard_map/ppermute | solution.py:38
  21.9 4.3 %collective-permute-start.1 = (bf16[4,512,128]{2,1,0:T(8,128)(2,1)S(1)}, bf16[4,512,128]{2,1,0:T(8,128)(2,1)S(1)}, u32[]{:S(2)}, u32[]{:S(2)}) collective-permute-start(bf16[4,512,128]{2,1,0:T(8,128)(2,1)S(1)} %get-tuple-element.22.left.rounded), channel_id=1, source_target_pairs={{4,8},{12,16},{20,24},{28,32},{36,40},{44,48},{52,56},{60,64},{68,... | collective-permute-start | bytes 1572872 | tf_op jit(solution)/shard_map/ppermute | solution.py:33
  26.2 0.1 added.3
  26.4 0.0 collective-permute-done.11.from_mate
  26.4 4.6 %collective-permute-start.6 = (bf16[512,256]{1,0:T(8,128)(2,1)S(1)}, bf16[512,256]{1,0:T(8,128)(2,1)S(1)}, u32[]{:S(2)}, u32[]{:S(2)}) collective-permute-start(bf16[512,256]{1,0:T(8,128)(2,1)S(1)} %added.3), channel_id=1, source_target_pairs={{4,8},{12,16},{20,24},{28,32},{36,40},{44,48},{52,56},{60,64},{68,... | collective-permute-start | bytes 786440 | tf_op jit(solution)/shard_map/ppermute | solution.py:33
  30.9 0.0 collective-permute-done.12.from_across
  30.9 0.0 collective-permute-done.2.terms
  31.0 1.5 %forward.3 = (f32[512,128]{1,0:T(8,128)S(1)}, bf16[512,128]{1,0:T(8,128)(2,1)S(1)}, bf16[512,128]{1,0:T(8,128)(2,1)S(1)}, bf16[512,128]{1,0:T(8,128)(2,1)S(1)}) custom-call(s32[2,4]{1,0:T(2,128)S(1)} %bitcast.2, bf16[4,512,512]{2,1,0:T(8,128)(2,1)S(1)} %copy-done, bf16[4,512,128]{2,1,0:T(8,128)(2,1)S(1)} %get-tuple-element.23.right.rounded, ...), custom_call_target="tpu_custom_call" | custom-call | flops 600000000 | bytes 4000000 | tf_op jit(solution)/shard_map/forward/pallas_call | solution.py:259
  32.4 1.2 %collective-permute-start.13 = (bf16[512,128]{1,0:T(8,128)(2,1)S(1)}, bf16[512,128]{1,0:T(8,128)(2,1)S(1)}, u32[]{:S(2)}, u32[]{:S(2)}) collective-permute-start(bf16[512,128]{1,0:T(8,128)(2,1)S(1)} %get-tuple-element.36), channel_id=1, source_target_pairs={{0,1},{1,2},{2,3},{3,0},{4,5},{5,6},{6,7},{7,4},{8,9},{9,10},{10,1... | collective-permute-start | bytes 393224 | tf_op jit(solution)/shard_map/ppermute | solution.py:38
  33.6 2.1 %collective-permute-start.14 = (bf16[512,128]{1,0:T(8,128)(2,1)S(1)}, bf16[512,128]{1,0:T(8,128)(2,1)S(1)}, u32[]{:S(2)}, u32[]{:S(2)}) collective-permute-start(bf16[512,128]{1,0:T(8,128)(2,1)S(1)} %get-tuple-element.37), channel_id=1, source_target_pairs={{0,3},{1,0},{2,1},{3,2},{4,7},{5,4},{6,5},{7,6},{8,11},{9,8},{10,9... | collective-permute-start | bytes 393224 | tf_op jit(solution)/shard_map/ppermute | solution.py:38
  35.8 4.3 %collective-permute-start.15 = (bf16[512,128]{1,0:T(8,128)(2,1)S(1)}, bf16[512,128]{1,0:T(8,128)(2,1)S(1)}, u32[]{:S(2)}, u32[]{:S(2)}) collective-permute-start(bf16[512,128]{1,0:T(8,128)(2,1)S(1)} %get-tuple-element.38), channel_id=1, source_target_pairs={{0,2},{1,3},{2,0},{3,1},{4,6},{5,7},{6,4},{7,5},{8,10},{9,11},{10,... | collective-permute-start | bytes 393224 | tf_op jit(solution)/shard_map/ppermute | solution.py:38
  40.0 0.0 collective-permute-done.1.from_across
  40.0 1.5 %forward.2 = (f32[512,128]{1,0:T(8,128)S(1)}, bf16[512,128]{1,0:T(8,128)(2,1)S(1)}, bf16[512,128]{1,0:T(8,128)(2,1)S(1)}, bf16[512,128]{1,0:T(8,128)(2,1)S(1)}) custom-call(s32[2,4]{1,0:T(2,128)S(1)} %bitcast.3, bf16[4,512,512]{2,1,0:T(8,128)(2,1)S(1)} %copy-done, bf16[4,512,128]{2,1,0:T(8,128)(2,1)S(1)} %get-tuple-element.22.left.rounded, ...), custom_call_target="tpu_custom_call" | custom-call | flops 600000000 | bytes 4000000 | tf_op jit(solution)/shard_map/forward/pallas_call | solution.py:259
  41.5 0.0 copy-start.2
  41.5 0.1 collective-permute-start.7
  41.6 0.0 collective-permute-done.6.refs_1_
  41.6 3.2 %collective-permute-start.8 = (bf16[512,128]{1,0:T(8,128)(2,1)S(1)}, bf16[512,128]{1,0:T(8,128)(2,1)S(1)}, u32[]{:S(2)}, u32[]{:S(2)}) collective-permute-start(bf16[512,128]{1,0:T(8,128)(2,1)S(1)} %get-tuple-element.32), channel_id=1, source_target_pairs={{0,3},{1,0},{2,1},{3,2},{4,7},{5,4},{6,5},{7,6},{8,11},{9,8},{10,9... | collective-permute-start | bytes 393224 | tf_op jit(solution)/shard_map/ppermute | solution.py:38
  44.8 0.8 %collective-permute-start.9 = (bf16[512,128]{1,0:T(8,128)(2,1)S(1)}, bf16[512,128]{1,0:T(8,128)(2,1)S(1)}, u32[]{:S(2)}, u32[]{:S(2)}) collective-permute-start(bf16[512,128]{1,0:T(8,128)(2,1)S(1)} %get-tuple-element.33), channel_id=1, source_target_pairs={{0,2},{1,3},{2,0},{3,1},{4,6},{5,7},{6,4},{7,5},{8,10},{9,11},{10,... | collective-permute-start | bytes 393224 | tf_op jit(solution)/shard_map/ppermute | solution.py:38
  45.7 0.0 collective-permute-done.14.refs_3_
  45.7 0.0 collective-permute-done.15.refs_4_
  45.7 0.1 added.5.rest_1_
  45.8 0.9 %collective-permute-start.16 = (bf16[512,128]{1,0:T(8,128)(2,1)S(1)}, bf16[512,128]{1,0:T(8,128)(2,1)S(1)}, u32[]{:S(2)}, u32[]{:S(2)}) collective-permute-start(bf16[512,128]{1,0:T(8,128)(2,1)S(1)} %added.5.rest_1_), channel_id=1, source_target_pairs={{0,1},{1,2},{2,3},{3,0},{4,5},{5,6},{6,7},{7,4},{8,9},{9,10},{10,1... | collective-permute-start | bytes 393224 | tf_op jit(solution)/shard_map/ppermute | solution.py:38
  46.7 2.6 %collective-permute-start.18 = (bf16[512,128]{1,0:T(8,128)(2,1)S(1)}, bf16[512,128]{1,0:T(8,128)(2,1)S(1)}, u32[]{:S(2)}, u32[]{:S(2)}) collective-permute-start(bf16[512,128]{1,0:T(8,128)(2,1)S(1)} %added.5.rest_1_), channel_id=1, source_target_pairs={{0,3},{1,0},{2,1},{3,2},{4,7},{5,4},{6,5},{7,6},{8,11},{9,8},{10,9... | collective-permute-start | bytes 393224 | tf_op jit(solution)/shard_map/ppermute | solution.py:38
  49.3 1.5 %collective-permute-done.7.refs_2_ = bf16[512,128]{1,0:T(8,128)(2,1)S(1)} collective-permute-done((bf16[512,128]{1,0:T(8,128)(2,1)S(1)}, bf16[512,128]{1,0:T(8,128)(2,1)S(1)}, u32[]{:S(2)}, u32[]{:S(2)}) %collective-permute-start.7) | collective-permute-done | bytes 131104 | tf_op jit(solution)/shard_map/ppermute | solution.py:38
  50.7 0.0 collective-permute-start.20
  50.8 0.7 %collective-permute-done.8.refs_3_ = bf16[512,128]{1,0:T(8,128)(2,1)S(1)} collective-permute-done((bf16[512,128]{1,0:T(8,128)(2,1)S(1)}, bf16[512,128]{1,0:T(8,128)(2,1)S(1)}, u32[]{:S(2)}, u32[]{:S(2)}) %collective-permute-start.8) | collective-permute-done | bytes 131104 | tf_op jit(solution)/shard_map/ppermute | solution.py:38
  51.5 1.3 %collective-permute-done.9.refs_4_ = bf16[512,128]{1,0:T(8,128)(2,1)S(1)} collective-permute-done((bf16[512,128]{1,0:T(8,128)(2,1)S(1)}, bf16[512,128]{1,0:T(8,128)(2,1)S(1)}, u32[]{:S(2)}, u32[]{:S(2)}) %collective-permute-start.9) | collective-permute-done | bytes 131104 | tf_op jit(solution)/shard_map/ppermute | solution.py:38
  52.7 0.1 added.4.rest_0_
  52.8 0.8 %collective-permute-start.10 = (bf16[512,128]{1,0:T(8,128)(2,1)S(1)}, bf16[512,128]{1,0:T(8,128)(2,1)S(1)}, u32[]{:S(2)}, u32[]{:S(2)}) collective-permute-start(bf16[512,128]{1,0:T(8,128)(2,1)S(1)} %added.4.rest_0_), channel_id=1, source_target_pairs={{0,1},{1,2},{2,3},{3,0},{4,5},{5,6},{6,7},{7,4},{8,9},{9,10},{10,1... | collective-permute-start | bytes 393224 | tf_op jit(solution)/shard_map/ppermute | solution.py:38
  53.6 2.5 %collective-permute-start.17 = (bf16[512,128]{1,0:T(8,128)(2,1)S(1)}, bf16[512,128]{1,0:T(8,128)(2,1)S(1)}, u32[]{:S(2)}, u32[]{:S(2)}) collective-permute-start(bf16[512,128]{1,0:T(8,128)(2,1)S(1)} %added.4.rest_0_), channel_id=1, source_target_pairs={{0,3},{1,0},{2,1},{3,2},{4,7},{5,4},{6,5},{7,6},{8,11},{9,8},{10,9... | collective-permute-start | bytes 393224 | tf_op jit(solution)/shard_map/ppermute | solution.py:38
  56.1 1.2 %collective-permute-done.16.rest_1_ = bf16[512,128]{1,0:T(8,128)(2,1)S(1)} collective-permute-done((bf16[512,128]{1,0:T(8,128)(2,1)S(1)}, bf16[512,128]{1,0:T(8,128)(2,1)S(1)}, u32[]{:S(2)}, u32[]{:S(2)}) %collective-permute-start.16) | collective-permute-done | bytes 131104 | tf_op jit(solution)/shard_map/ppermute | solution.py:38
  57.3 3.6 %project.2.rest_6_ = f32[4,512,256]{2,1,0:T(8,128)} custom-call(f32[4,512,256]{2,1,0:T(8,128)S(1)} %copy-done.2, bf16[512,128]{1,0:T(8,128)(2,1)S(1)} %added.4.rest_0_, bf16[512,128]{1,0:T(8,128)(2,1)S(1)} %added.5.rest_1_), custom_call_target="tpu_custom_call" | custom-call | flops 2000000000 | bytes 2000000 | tf_op jit(solution)/shard_map/project/pallas_call | solution.py:187
  60.9 0.0 collective-permute-done.18.rest_3_
  60.9 0.0 collective-permute-done.20.rest_5_
  60.9 0.0 collective-permute-done.17.rest_2_
  61.0 2.9 %collective-permute-done.19.rest_4_ = bf16[512,128]{1,0:T(8,128)(2,1)S(1)} collective-permute-done((bf16[512,128]{1,0:T(8,128)(2,1)S(1)}, bf16[512,128]{1,0:T(8,128)(2,1)S(1)}, u32[]{:S(2)}, u32[]{:S(2)}) %collective-permute-start.19) | collective-permute-done | bytes 131104 | tf_op jit(solution)/shard_map/ppermute | solution.py:38
  63.8 4.4 %project.3 = f32[4,512,256]{2,1,0:T(8,128)} custom-call(f32[4,512,256]{2,1,0:T(8,128)S(1)} %copy-done.2, bf16[512,128]{1,0:T(8,128)(2,1)S(1)} %collective-permute-done.10.rest_0_, bf16[512,128]{1,0:T(8,128)(2,1)S(1)} %collective-permute-done.16.rest_1_, bf16[512,128]{1,0:T(8,128)(2,1)S(1)} %collective-permute-done.17.rest_2_, ...), custom_call_target="tpu_custom_call", output_to_operand_aliasing={{}: (7, {})} | custom-call | flops 6000000000 | bytes 6000000 | tf_op jit(solution)/shard_map/project/pallas_call | solution.py:187
  (11 shorter events, 0.0 us)
Async XLA Ops:
  0.0 1.6 %copy-start.1 = (f32[4,512,256]{2,1,0:T(8,128)S(1)}, f32[4,512,256]{2,1,0:T(8,128)}, u32[]{:S(2)}) copy-start(f32[4,512,256]{2,1,0:T(8,128)} %factors.3) | copy-start | bytes 6291460
  1.6 1.6 %copy-start = (bf16[4,512,512]{2,1,0:T(8,128)(2,1)S(1)}, bf16[4,512,512]{2,1,0:T(8,128)(2,1)}, u32[]{:S(2)}) copy-start(bf16[4,512,512]{2,1,0:T(8,128)(2,1)} %affinity.5) | copy-start | bytes 6291460
  1.6 1.6 %copy-start.3 = (s32[4,2]{0,1:T(2,128)S(1)}, s32[4,2]{0,1:T(2,128)}, u32[]{:S(2)}) copy-start(s32[4,2]{0,1:T(2,128)} %param.4) | copy-start | bytes 100
  5.0 25.9 %collective-permute-start.2 = (bf16[4,512,256]{2,1,0:T(8,128)(2,1)S(1)}, bf16[4,512,256]{2,1,0:T(8,128)(2,1)S(1)}, u32[]{:S(2)}, u32[]{:S(2)}) collective-permute-start(bf16[4,512,256]{2,1,0:T(8,128)(2,1)S(1)} %get-tuple-element.25), channel_id=1, source_target_pairs={{0,4},{4,0},{8,12},{12,8},{16,20},{20,16},{24,28},{28,24},{32,36},... | collective-permute-start | bytes 3145736 | tf_op jit(solution)/shard_map/ppermute | solution.py:27
  5.1 10.0 %collective-permute-start.3 = (bf16[512,256]{1,0:T(8,128)(2,1)S(1)}, bf16[512,256]{1,0:T(8,128)(2,1)S(1)}, u32[]{:S(2)}, u32[]{:S(2)}) collective-permute-start(bf16[512,256]{1,0:T(8,128)(2,1)S(1)} %get-tuple-element.28), channel_id=1, source_target_pairs={{0,1},{1,2},{2,3},{3,0},{4,5},{5,6},{6,7},{7,4},{8,9},{9,10},{10,1... | collective-permute-start | bytes 786440 | tf_op jit(solution)/shard_map/ppermute | solution.py:38
  6.8 15.1 %collective-permute-start.4 = (bf16[512,256]{1,0:T(8,128)(2,1)S(1)}, bf16[512,256]{1,0:T(8,128)(2,1)S(1)}, u32[]{:S(2)}, u32[]{:S(2)}) collective-permute-start(bf16[512,256]{1,0:T(8,128)(2,1)S(1)} %get-tuple-element.29), channel_id=1, source_target_pairs={{0,2},{1,3},{2,0},{3,1},{4,6},{5,7},{6,4},{7,5},{8,10},{9,11},{10,... | collective-permute-start | bytes 786440 | tf_op jit(solution)/shard_map/ppermute | solution.py:38
  9.7 12.2 %collective-permute-start.5 = (bf16[512,256]{1,0:T(8,128)(2,1)S(1)}, bf16[512,256]{1,0:T(8,128)(2,1)S(1)}, u32[]{:S(2)}, u32[]{:S(2)}) collective-permute-start(bf16[512,256]{1,0:T(8,128)(2,1)S(1)} %get-tuple-element.30), channel_id=1, source_target_pairs={{0,3},{1,0},{2,1},{3,2},{4,7},{5,4},{6,5},{7,6},{8,11},{9,8},{10,9... | collective-permute-start | bytes 786440 | tf_op jit(solution)/shard_map/ppermute | solution.py:38
  11.0 15.3 %collective-permute-start.11 = (bf16[4,512,128]{2,1,0:T(8,128)(2,1)S(1)}, bf16[4,512,128]{2,1,0:T(8,128)(2,1)S(1)}, u32[]{:S(2)}, u32[]{:S(2)}) collective-permute-start(bf16[4,512,128]{2,1,0:T(8,128)(2,1)S(1)} %get-tuple-element.23.right.rounded), channel_id=1, source_target_pairs={{0,4},{4,0},{8,12},{12,8},{16,20},{20,16},{24,28},{28,24},{32,36},... | collective-permute-start | bytes 1572872 | tf_op jit(solution)/shard_map/ppermute | solution.py:27
  15.1 15.8 %collective-permute-start.12 = (bf16[4,512,128]{2,1,0:T(8,128)(2,1)S(1)}, bf16[4,512,128]{2,1,0:T(8,128)(2,1)S(1)}, u32[]{:S(2)}, u32[]{:S(2)}) collective-permute-start(bf16[4,512,128]{2,1,0:T(8,128)(2,1)S(1)} %get-tuple-element.23.right.rounded), channel_id=1, source_target_pairs={{4,8},{12,16},{20,24},{28,32},{36,40},{44,48},{52,56},{60,64},{68,... | collective-permute-start | bytes 1572872 | tf_op jit(solution)/shard_map/ppermute | solution.py:33
  21.9 13.8 %collective-permute-start = (bf16[4,512,128]{2,1,0:T(8,128)(2,1)S(1)}, bf16[4,512,128]{2,1,0:T(8,128)(2,1)S(1)}, u32[]{:S(2)}, u32[]{:S(2)}) collective-permute-start(bf16[4,512,128]{2,1,0:T(8,128)(2,1)S(1)} %get-tuple-element.22.left.rounded), channel_id=1, source_target_pairs={{0,4},{4,0},{8,12},{12,8},{16,20},{20,16},{24,28},{28,24},{32,36},... | collective-permute-start | bytes 1572872 | tf_op jit(solution)/shard_map/ppermute | solution.py:27
  21.9 18.1 %collective-permute-start.1 = (bf16[4,512,128]{2,1,0:T(8,128)(2,1)S(1)}, bf16[4,512,128]{2,1,0:T(8,128)(2,1)S(1)}, u32[]{:S(2)}, u32[]{:S(2)}) collective-permute-start(bf16[4,512,128]{2,1,0:T(8,128)(2,1)S(1)} %get-tuple-element.22.left.rounded), channel_id=1, source_target_pairs={{4,8},{12,16},{20,24},{28,32},{36,40},{44,48},{52,56},{60,64},{68,... | collective-permute-start | bytes 1572872 | tf_op jit(solution)/shard_map/ppermute | solution.py:33
  26.4 15.2 %collective-permute-start.6 = (bf16[512,256]{1,0:T(8,128)(2,1)S(1)}, bf16[512,256]{1,0:T(8,128)(2,1)S(1)}, u32[]{:S(2)}, u32[]{:S(2)}) collective-permute-start(bf16[512,256]{1,0:T(8,128)(2,1)S(1)} %added.3), channel_id=1, source_target_pairs={{4,8},{12,16},{20,24},{28,32},{36,40},{44,48},{52,56},{60,64},{68,... | collective-permute-start | bytes 786440 | tf_op jit(solution)/shard_map/ppermute | solution.py:33
  32.4 12.4 %collective-permute-start.13 = (bf16[512,128]{1,0:T(8,128)(2,1)S(1)}, bf16[512,128]{1,0:T(8,128)(2,1)S(1)}, u32[]{:S(2)}, u32[]{:S(2)}) collective-permute-start(bf16[512,128]{1,0:T(8,128)(2,1)S(1)} %get-tuple-element.36), channel_id=1, source_target_pairs={{0,1},{1,2},{2,3},{3,0},{4,5},{5,6},{6,7},{7,4},{8,9},{9,10},{10,1... | collective-permute-start | bytes 393224 | tf_op jit(solution)/shard_map/ppermute | solution.py:38
  33.6 12.0 %collective-permute-start.14 = (bf16[512,128]{1,0:T(8,128)(2,1)S(1)}, bf16[512,128]{1,0:T(8,128)(2,1)S(1)}, u32[]{:S(2)}, u32[]{:S(2)}) collective-permute-start(bf16[512,128]{1,0:T(8,128)(2,1)S(1)} %get-tuple-element.37), channel_id=1, source_target_pairs={{0,3},{1,0},{2,1},{3,2},{4,7},{5,4},{6,5},{7,6},{8,11},{9,8},{10,9... | collective-permute-start | bytes 393224 | tf_op jit(solution)/shard_map/ppermute | solution.py:38
  35.8 9.9 %collective-permute-start.15 = (bf16[512,128]{1,0:T(8,128)(2,1)S(1)}, bf16[512,128]{1,0:T(8,128)(2,1)S(1)}, u32[]{:S(2)}, u32[]{:S(2)}) collective-permute-start(bf16[512,128]{1,0:T(8,128)(2,1)S(1)} %get-tuple-element.38), channel_id=1, source_target_pairs={{0,2},{1,3},{2,0},{3,1},{4,6},{5,7},{6,4},{7,5},{8,10},{9,11},{10,... | collective-permute-start | bytes 393224 | tf_op jit(solution)/shard_map/ppermute | solution.py:38
  41.5 15.8 %copy-start.2 = (f32[4,512,256]{2,1,0:T(8,128)S(1)}, f32[4,512,256]{2,1,0:T(8,128)}, u32[]{:S(2)}) copy-start(f32[4,512,256]{2,1,0:T(8,128)} %factors.3) | copy-start | bytes 6291460
  41.5 9.2 %collective-permute-start.7 = (bf16[512,128]{1,0:T(8,128)(2,1)S(1)}, bf16[512,128]{1,0:T(8,128)(2,1)S(1)}, u32[]{:S(2)}, u32[]{:S(2)}) collective-permute-start(bf16[512,128]{1,0:T(8,128)(2,1)S(1)} %get-tuple-element.31), channel_id=1, source_target_pairs={{0,1},{1,2},{2,3},{3,0},{4,5},{5,6},{6,7},{7,4},{8,9},{9,10},{10,1... | collective-permute-start | bytes 393224 | tf_op jit(solution)/shard_map/ppermute | solution.py:38
  41.6 9.8 %collective-permute-start.8 = (bf16[512,128]{1,0:T(8,128)(2,1)S(1)}, bf16[512,128]{1,0:T(8,128)(2,1)S(1)}, u32[]{:S(2)}, u32[]{:S(2)}) collective-permute-start(bf16[512,128]{1,0:T(8,128)(2,1)S(1)} %get-tuple-element.32), channel_id=1, source_target_pairs={{0,3},{1,0},{2,1},{3,2},{4,7},{5,4},{6,5},{7,6},{8,11},{9,8},{10,9... | collective-permute-start | bytes 393224 | tf_op jit(solution)/shard_map/ppermute | solution.py:38
  44.8 7.9 %collective-permute-start.9 = (bf16[512,128]{1,0:T(8,128)(2,1)S(1)}, bf16[512,128]{1,0:T(8,128)(2,1)S(1)}, u32[]{:S(2)}, u32[]{:S(2)}) collective-permute-start(bf16[512,128]{1,0:T(8,128)(2,1)S(1)} %get-tuple-element.33), channel_id=1, source_target_pairs={{0,2},{1,3},{2,0},{3,1},{4,6},{5,7},{6,4},{7,5},{8,10},{9,11},{10,... | collective-permute-start | bytes 393224 | tf_op jit(solution)/shard_map/ppermute | solution.py:38
  45.8 11.6 %collective-permute-start.16 = (bf16[512,128]{1,0:T(8,128)(2,1)S(1)}, bf16[512,128]{1,0:T(8,128)(2,1)S(1)}, u32[]{:S(2)}, u32[]{:S(2)}) collective-permute-start(bf16[512,128]{1,0:T(8,128)(2,1)S(1)} %added.5.rest_1_), channel_id=1, source_target_pairs={{0,1},{1,2},{2,3},{3,0},{4,5},{5,6},{6,7},{7,4},{8,9},{9,10},{10,1... | collective-permute-start | bytes 393224 | tf_op jit(solution)/shard_map/ppermute | solution.py:38
  46.7 14.2 %collective-permute-start.18 = (bf16[512,128]{1,0:T(8,128)(2,1)S(1)}, bf16[512,128]{1,0:T(8,128)(2,1)S(1)}, u32[]{:S(2)}, u32[]{:S(2)}) collective-permute-start(bf16[512,128]{1,0:T(8,128)(2,1)S(1)} %added.5.rest_1_), channel_id=1, source_target_pairs={{0,3},{1,0},{2,1},{3,2},{4,7},{5,4},{6,5},{7,6},{8,11},{9,8},{10,9... | collective-permute-start | bytes 393224 | tf_op jit(solution)/shard_map/ppermute | solution.py:38
  50.7 10.2 %collective-permute-start.20 = (bf16[512,128]{1,0:T(8,128)(2,1)S(1)}, bf16[512,128]{1,0:T(8,128)(2,1)S(1)}, u32[]{:S(2)}, u32[]{:S(2)}) collective-permute-start(bf16[512,128]{1,0:T(8,128)(2,1)S(1)} %added.5.rest_1_), channel_id=1, source_target_pairs={{0,2},{1,3},{2,0},{3,1},{4,6},{5,7},{6,4},{7,5},{8,10},{9,11},{10,... | collective-permute-start | bytes 393224 | tf_op jit(solution)/shard_map/ppermute | solution.py:38
  52.8 8.1 %collective-permute-start.10 = (bf16[512,128]{1,0:T(8,128)(2,1)S(1)}, bf16[512,128]{1,0:T(8,128)(2,1)S(1)}, u32[]{:S(2)}, u32[]{:S(2)}) collective-permute-start(bf16[512,128]{1,0:T(8,128)(2,1)S(1)} %added.4.rest_0_), channel_id=1, source_target_pairs={{0,1},{1,2},{2,3},{3,0},{4,5},{5,6},{6,7},{7,4},{8,9},{9,10},{10,1... | collective-permute-start | bytes 393224 | tf_op jit(solution)/shard_map/ppermute | solution.py:38
  53.6 7.3 %collective-permute-start.17 = (bf16[512,128]{1,0:T(8,128)(2,1)S(1)}, bf16[512,128]{1,0:T(8,128)(2,1)S(1)}, u32[]{:S(2)}, u32[]{:S(2)}) collective-permute-start(bf16[512,128]{1,0:T(8,128)(2,1)S(1)} %added.4.rest_0_), channel_id=1, source_target_pairs={{0,3},{1,0},{2,1},{3,2},{4,7},{5,4},{6,5},{7,6},{8,11},{9,8},{10,9... | collective-permute-start | bytes 393224 | tf_op jit(solution)/shard_map/ppermute | solution.py:38
  57.3 6.5 %collective-permute-start.19 = (bf16[512,128]{1,0:T(8,128)(2,1)S(1)}, bf16[512,128]{1,0:T(8,128)(2,1)S(1)}, u32[]{:S(2)}, u32[]{:S(2)}) collective-permute-start(bf16[512,128]{1,0:T(8,128)(2,1)S(1)} %added.4.rest_0_), channel_id=1, source_target_pairs={{0,2},{1,3},{2,0},{3,1},{4,6},{5,7},{6,4},{7,5},{8,10},{9,11},{10,... | collective-permute-start | bytes 393224 | tf_op jit(solution)/shard_map/ppermute | solution.py:38

commit v4 on v3

--- a/solution.py
+++ b/solution.py
@@ -10,7 +10,7 @@
 
 
 P_SIZE = 512
-KEEP = (0.0, 0.0, 0.0, 0.5, 0.5, 1.0)
+KEEP = (0.0, 0.0, 0.5, 0.5, 1.0)
 
 epsilon = 1e-06
 start_scale = 0.25
@@ -94,9 +94,8 @@
 
 
 def forward_kernel(
-    start, pairs, affinity, rounded, from_mate, from_across, own, terms, p0, p1, p2, p3, rhs, acc, held, sem
+    start, pairs, affinity, rounded, from_mate, from_across, own, terms, p0, p1, p2, p3, acc, held, sem
 ):
-    tiles = affinity.shape[0]
     images, _, half = rounded.shape
     copy = pltpu.make_async_copy(pairs, held, sem)
     copy.start()
@@ -104,23 +103,12 @@
         acc[j] = own[j] + terms[j, :, start : start + half].astype(jnp.float32)
     copy.wait()
     firsts, slots, turns = places(held, images)
-    for t in range(tiles):
-        slot = slots[t]
-
-        @pl.when(slot < images)
-        def _():
-            rhs[t] = from_across[slot]
-
-        @pl.when(jnp.logical_and(slot >= images, slot < 2 * images))
-        def _():
-            rhs[t] = rounded[slot - images]
-
-        @pl.when(slot >= 2 * images)
-        def _():
-            rhs[t] = from_mate[slot - 2 * images]
-
-    for t in range(tiles):
-        acc[firsts[t]] = acc[firsts[t]] + dot(affinity[t], rhs[t])
+    for t, (first, slot) in enumerate(zip(firsts, slots)):
+        image = lax.rem(slot, images)
+        second = jnp.where(
+            slot < images, from_across[image], jnp.where(slot < 2 * images, rounded[image], from_mate[image])
+        )
+        acc[first] = acc[first] + dot(affinity[t], second)
     for turn, ref in zip(turns, (p0, p1, p2, p3)):
         ref[...] = acc[turn].astype(ref.dtype)
 
@@ -149,23 +137,28 @@
     turns = order(factors.shape[0])
     gradients = [jnp.concatenate([rest[2 * k][...], rest[2 * k + 1][...]], axis=1) for k in range(count)]
     out, held, sems = rest[-3:]
-    ys = []
+    ys, scales = [], []
     for k, gradient in zip(ahead, gradients):
         x = factors[turns[k]] + ascent_step * gradient.astype(jnp.float32)
+        ys.append(x.T)
         squares = jnp.sum(jnp.sum(x * x, axis=0, keepdims=True), axis=1, keepdims=True)
-        x = x * (start_scale * math.sqrt(x.shape[1]) * lax.rsqrt(squares + epsilon))
-        ys.append(x.T)
+        scales.append(start_scale * math.sqrt(x.shape[1]) * lax.rsqrt(squares + epsilon))
+    highs = [y.astype(jnp.bfloat16) for y in ys]
+    grams = [dot(h, h, NT) * (scale * scale) for h, scale in zip(highs, scales)]
+    changes = [dot(g.astype(jnp.bfloat16), h) for g, h in zip(grams, highs)]
+    ys = [(1.5 * y - 0.5 * c) * scale for y, c, scale in zip(ys, changes, scales)]
     diagonal = same_index(ys[0].shape[0])
-    for keep in KEEP:
+    for step, keep in enumerate(KEEP):
+        gain = math.sqrt(P_SIZE) if step == len(KEEP) - 1 else 1.0
         highs = [y.astype(jnp.bfloat16) for y in ys]
         grams = [dot(h, h, NT) for h in highs]
         if keep:
             grams = [g - jnp.where(diagonal, keep, 0.0) for g in grams]
         changes = [dot(g.astype(jnp.bfloat16), h) for g, h in zip(grams, highs)]
-        ys = [(1.5 - 0.5 * keep) * y - 0.5 * c for y, c in zip(ys, changes)]
+        ys = [gain * (1.5 - 0.5 * keep) * y - gain * 0.5 * c for y, c in zip(ys, changes)]
     copies = []
     for k, y in enumerate(ys):
-        held[k] = (y * math.sqrt(P_SIZE)).T
+        held[k] = y.T
         copies.append(pltpu.make_async_copy(held.at[k], out.at[turns[ahead[k]]], sems.at[k]))
         copies[-1].start()
     for copy in copies:
@@ -262,7 +255,6 @@
             in_specs=[pl.BlockSpec(memory_space=pl.ANY)] + [VMEM] * 6,
             out_specs=(VMEM,) * 4,
             scratch_shapes=[
-                pltpu.VMEM((affinity.shape[0], keypoints, half), jnp.bfloat16),
                 pltpu.VMEM((images, keypoints, half), jnp.float32),
                 pltpu.SMEM(pairs.shape, jnp.int32),
                 pltpu.SemaphoreType.DMA(()),

time: 68.6 us -> 68.3 us (level)
  starting transfers between devices: 36.9 us -> 38.4 us
  waiting for transfers between devices: 15 us -> 13.7 us
    ppermute x15, starting transfers between devices: 24.5 us -> 26 us  [turned(): return lax.ppermute(x, 'rep', [(i, (i + by) % n) for i in range(n)])]
    ppermute x15, waiting for transfers between devices: 15 us -> 13.6 us  [turned(): return lax.ppermute(x, 'rep', [(i, (i + by) % n) for i in range(n)])]
  transfers between devices with their start and end apart: 21 -> 21, of which waited for: 7 -> 6; matrix products, arithmetic and copies ran while one was open for 0% -> 0% of each run, Pallas kernels for 10% -> 9%
where the time goes in v4:
time: 68.3 us; the launch traced here: 68.1 us
  starting transfers between devices  38.4 us (56%)
  waiting for transfers between devices  13.7 us (20%)
  Pallas kernels  12.6 us (18%)
  local copies, waits for them, and re-layouts  3.05 us (4%)
    ppermute x15, starting transfers between devices, turned(): return lax.ppermute(x, 'rep', [(i, (i + by) % n) for i in range(n)])  26 us
    ppermute x15, waiting for transfers between devices, turned(): return lax.ppermute(x, 'rep', [(i, (i + by) % n) for i in range(n)])  13.6 us
    ppermute x3, starting transfers between devices, across(): return lax.ppermute(x, 'tiles', pairs + [(b, a) for a, b in pairs])  12.3 us
    pallas_call x2, Pallas kernels, project(): pl.pallas_call(functools.partial(project_kernel, ahead), out_shape=jax.Sh...  7.58 us
    unnamed x8, local copies, waits for them, and re-layouts  3.05 us
    pallas_call x2, Pallas kernels, forward(): pl.pallas_call(functools.partial(forward_kernel, start), out_shape=(shape...  2.8 us
    pallas_call x1, Pallas kernels, shards(): pl.pallas_call(backward_kernel, out_shape=(shape(images, keypoints, half,...  1.83 us
  transfers between devices with their start and end apart: 21, of which 6 were waited for; matrix products, arithmetic and copies ran while one was open for 0% of the time, Pallas kernels for 9%

profile of v4, /device:TPU:128, one launch (start us, length us, event | category | flops | bytes accessed | tf_op | source)
XLA Modules:
  0.0 68.1 jit_solution(12647178047154876231)
XLA Ops:
  0.0 1.6 %copy-done.1 = f32[4,512,256]{2,1,0:T(8,128)S(1)} copy-done((f32[4,512,256]{2,1,0:T(8,128)S(1)}, f32[4,512,256]{2,1,0:T(8,128)}, u32[]{:S(2)}) %copy-start.1) | copy-done | bytes 2097176
  1.6 0.1 rounded.1
  1.7 1.5 %copy-done = bf16[4,512,512]{2,1,0:T(8,128)(2,1)S(1)} copy-done((bf16[4,512,512]{2,1,0:T(8,128)(2,1)S(1)}, bf16[4,512,512]{2,1,0:T(8,128)(2,1)}, u32[]{:S(2)}) %copy-start) | copy-done | bytes 2097176
  3.2 1.8 %backward.1 = (f32[4,512,128]{2,1,0:T(8,128)S(1)}, f32[4,512,128]{2,1,0:T(8,128)S(1)}, bf16[4,512,256]{2,1,0:T(8,128)(2,1)S(1)}, f32[512,256]{1,0:T(8,128)S(1)},...) custom-call(s32[2,4]{1,0:T(2,128)S(1)} %bitcast.1, ...), custom_call_target="tpu_custom_call" | custom-call | flops 600000000 | bytes 8000000 | tf_op jit(solution)/shard_map/backward/pallas_call | solution.py:215
  5.0 0.1 collective-permute-start.2
  5.1 1.7 %collective-permute-start.3 = (bf16[512,256]{1,0:T(8,128)(2,1)S(1)}, bf16[512,256]{1,0:T(8,128)(2,1)S(1)}, u32[]{:S(2)}, u32[]{:S(2)}) collective-permute-start(bf16[512,256]{1,0:T(8,128)(2,1)S(1)} %get-tuple-element.28), channel_id=1, source_target_pairs={{0,1},{1,2},{2,3},{3,0},{4,5},{5,6},{6,7},{7,4},{8,9},{9,10},{10,1... | collective-permute-start | bytes 786440 | tf_op jit(solution)/shard_map/ppermute | solution.py:38
  6.8 2.9 %collective-permute-start.4 = (bf16[512,256]{1,0:T(8,128)(2,1)S(1)}, bf16[512,256]{1,0:T(8,128)(2,1)S(1)}, u32[]{:S(2)}, u32[]{:S(2)}) collective-permute-start(bf16[512,256]{1,0:T(8,128)(2,1)S(1)} %get-tuple-element.29), channel_id=1, source_target_pairs={{0,2},{1,3},{2,0},{3,1},{4,6},{5,7},{6,4},{7,5},{8,10},{9,11},{10,... | collective-permute-start | bytes 786440 | tf_op jit(solution)/shard_map/ppermute | solution.py:38
  9.7 1.3 %collective-permute-start.5 = (bf16[512,256]{1,0:T(8,128)(2,1)S(1)}, bf16[512,256]{1,0:T(8,128)(2,1)S(1)}, u32[]{:S(2)}, u32[]{:S(2)}) collective-permute-start(bf16[512,256]{1,0:T(8,128)(2,1)S(1)} %get-tuple-element.30), channel_id=1, source_target_pairs={{0,3},{1,0},{2,1},{3,2},{4,7},{5,4},{6,5},{7,6},{8,11},{9,8},{10,9... | collective-permute-start | bytes 786440 | tf_op jit(solution)/shard_map/ppermute | solution.py:38
  11.0 0.0 collective-permute-start.11
  11.0 4.1 %collective-permute-done.3.refs_1_ = bf16[512,256]{1,0:T(8,128)(2,1)S(1)} collective-permute-done((bf16[512,256]{1,0:T(8,128)(2,1)S(1)}, bf16[512,256]{1,0:T(8,128)(2,1)S(1)}, u32[]{:S(2)}, u32[]{:S(2)}) %collective-permute-start.3) | collective-permute-done | bytes 262176 | tf_op jit(solution)/shard_map/ppermute | solution.py:38
  15.1 3.4 %collective-permute-start.12 = (bf16[4,512,128]{2,1,0:T(8,128)(2,1)S(1)}, bf16[4,512,128]{2,1,0:T(8,128)(2,1)S(1)}, u32[]{:S(2)}, u32[]{:S(2)}) collective-permute-start(bf16[4,512,128]{2,1,0:T(8,128)(2,1)S(1)} %get-tuple-element.23.right.rounded), channel_id=1, source_target_pairs={{4,8},{12,16},{20,24},{28,32},{36,40},{44,48},{52,56},{60,64},{68,... | collective-permute-start | bytes 1572872 | tf_op jit(solution)/shard_map/ppermute | solution.py:33
  18.5 3.4 %collective-permute-done.4.refs_2_ = bf16[512,256]{1,0:T(8,128)(2,1)S(1)} collective-permute-done((bf16[512,256]{1,0:T(8,128)(2,1)S(1)}, bf16[512,256]{1,0:T(8,128)(2,1)S(1)}, u32[]{:S(2)}, u32[]{:S(2)}) %collective-permute-start.4) | collective-permute-done | bytes 262176 | tf_op jit(solution)/shard_map/ppermute | solution.py:38
  21.9 0.0 collective-permute-start
  21.9 4.3 %collective-permute-start.1 = (bf16[4,512,128]{2,1,0:T(8,128)(2,1)S(1)}, bf16[4,512,128]{2,1,0:T(8,128)(2,1)S(1)}, u32[]{:S(2)}, u32[]{:S(2)}) collective-permute-start(bf16[4,512,128]{2,1,0:T(8,128)(2,1)S(1)} %get-tuple-element.22.left.rounded), channel_id=1, source_target_pairs={{4,8},{12,16},{20,24},{28,32},{36,40},{44,48},{52,56},{60,64},{68,... | collective-permute-start | bytes 1572872 | tf_op jit(solution)/shard_map/ppermute | solution.py:33
  26.2 0.1 added.3
  26.4 0.0 collective-permute-done.11.from_mate
  26.4 4.6 %collective-permute-start.6 = (bf16[512,256]{1,0:T(8,128)(2,1)S(1)}, bf16[512,256]{1,0:T(8,128)(2,1)S(1)}, u32[]{:S(2)}, u32[]{:S(2)}) collective-permute-start(bf16[512,256]{1,0:T(8,128)(2,1)S(1)} %added.3), channel_id=1, source_target_pairs={{4,8},{12,16},{20,24},{28,32},{36,40},{44,48},{52,56},{60,64},{68,... | collective-permute-start | bytes 786440 | tf_op jit(solution)/shard_map/ppermute | solution.py:33
  30.9 0.0 collective-permute-done.12.from_across
  30.9 0.0 collective-permute-done.2.terms
  31.0 1.4 %forward.3 = (f32[512,128]{1,0:T(8,128)S(1)}, bf16[512,128]{1,0:T(8,128)(2,1)S(1)}, bf16[512,128]{1,0:T(8,128)(2,1)S(1)}, bf16[512,128]{1,0:T(8,128)(2,1)S(1)}) custom-call(s32[2,4]{1,0:T(2,128)S(1)} %bitcast.2, bf16[4,512,512]{2,1,0:T(8,128)(2,1)S(1)} %copy-done, bf16[4,512,128]{2,1,0:T(8,128)(2,1)S(1)} %get-tuple-element.23.right.rounded, ...), custom_call_target="tpu_custom_call" | custom-call | flops 600000000 | bytes 4000000 | tf_op jit(solution)/shard_map/forward/pallas_call | solution.py:252
  32.4 1.2 %collective-permute-start.13 = (bf16[512,128]{1,0:T(8,128)(2,1)S(1)}, bf16[512,128]{1,0:T(8,128)(2,1)S(1)}, u32[]{:S(2)}, u32[]{:S(2)}) collective-permute-start(bf16[512,128]{1,0:T(8,128)(2,1)S(1)} %get-tuple-element.36), channel_id=1, source_target_pairs={{0,1},{1,2},{2,3},{3,0},{4,5},{5,6},{6,7},{7,4},{8,9},{9,10},{10,1... | collective-permute-start | bytes 393224 | tf_op jit(solution)/shard_map/ppermute | solution.py:38
  33.6 2.1 %collective-permute-start.14 = (bf16[512,128]{1,0:T(8,128)(2,1)S(1)}, bf16[512,128]{1,0:T(8,128)(2,1)S(1)}, u32[]{:S(2)}, u32[]{:S(2)}) collective-permute-start(bf16[512,128]{1,0:T(8,128)(2,1)S(1)} %get-tuple-element.37), channel_id=1, source_target_pairs={{0,3},{1,0},{2,1},{3,2},{4,7},{5,4},{6,5},{7,6},{8,11},{9,8},{10,9... | collective-permute-start | bytes 393224 | tf_op jit(solution)/shard_map/ppermute | solution.py:38
  35.7 4.3 %collective-permute-start.15 = (bf16[512,128]{1,0:T(8,128)(2,1)S(1)}, bf16[512,128]{1,0:T(8,128)(2,1)S(1)}, u32[]{:S(2)}, u32[]{:S(2)}) collective-permute-start(bf16[512,128]{1,0:T(8,128)(2,1)S(1)} %get-tuple-element.38), channel_id=1, source_target_pairs={{0,2},{1,3},{2,0},{3,1},{4,6},{5,7},{6,4},{7,5},{8,10},{9,11},{10,... | collective-permute-start | bytes 393224 | tf_op jit(solution)/shard_map/ppermute | solution.py:38
  40.0 0.0 collective-permute-done.1.from_across
  40.0 1.4 %forward.2 = (f32[512,128]{1,0:T(8,128)S(1)}, bf16[512,128]{1,0:T(8,128)(2,1)S(1)}, bf16[512,128]{1,0:T(8,128)(2,1)S(1)}, bf16[512,128]{1,0:T(8,128)(2,1)S(1)}) custom-call(s32[2,4]{1,0:T(2,128)S(1)} %bitcast.3, bf16[4,512,512]{2,1,0:T(8,128)(2,1)S(1)} %copy-done, bf16[4,512,128]{2,1,0:T(8,128)(2,1)S(1)} %get-tuple-element.22.left.rounded, ...), custom_call_target="tpu_custom_call" | custom-call | flops 600000000 | bytes 4000000 | tf_op jit(solution)/shard_map/forward/pallas_call | solution.py:252
  41.4 0.0 copy-start.2
  41.4 0.1 collective-permute-start.7
  41.5 3.2 %collective-permute-start.8 = (bf16[512,128]{1,0:T(8,128)(2,1)S(1)}, bf16[512,128]{1,0:T(8,128)(2,1)S(1)}, u32[]{:S(2)}, u32[]{:S(2)}) collective-permute-start(bf16[512,128]{1,0:T(8,128)(2,1)S(1)} %get-tuple-element.32), channel_id=1, source_target_pairs={{0,3},{1,0},{2,1},{3,2},{4,7},{5,4},{6,5},{7,6},{8,11},{9,8},{10,9... | collective-permute-start | bytes 393224 | tf_op jit(solution)/shard_map/ppermute | solution.py:38
  44.7 0.0 collective-permute-done.13.refs_2_
  44.7 0.9 %collective-permute-start.9 = (bf16[512,128]{1,0:T(8,128)(2,1)S(1)}, bf16[512,128]{1,0:T(8,128)(2,1)S(1)}, u32[]{:S(2)}, u32[]{:S(2)}) collective-permute-start(bf16[512,128]{1,0:T(8,128)(2,1)S(1)} %get-tuple-element.33), channel_id=1, source_target_pairs={{0,2},{1,3},{2,0},{3,1},{4,6},{5,7},{6,4},{7,5},{8,10},{9,11},{10,... | collective-permute-start | bytes 393224 | tf_op jit(solution)/shard_map/ppermute | solution.py:38
  45.6 0.0 collective-permute-done.14.refs_3_
  45.6 0.0 collective-permute-done.15.refs_4_
  45.6 0.1 added.5.rest_1_
  45.7 1.0 %collective-permute-start.16 = (bf16[512,128]{1,0:T(8,128)(2,1)S(1)}, bf16[512,128]{1,0:T(8,128)(2,1)S(1)}, u32[]{:S(2)}, u32[]{:S(2)}) collective-permute-start(bf16[512,128]{1,0:T(8,128)(2,1)S(1)} %added.5.rest_1_), channel_id=1, source_target_pairs={{0,1},{1,2},{2,3},{3,0},{4,5},{5,6},{6,7},{7,4},{8,9},{9,10},{10,1... | collective-permute-start | bytes 393224 | tf_op jit(solution)/shard_map/ppermute | solution.py:38
  46.7 2.5 %collective-permute-start.18 = (bf16[512,128]{1,0:T(8,128)(2,1)S(1)}, bf16[512,128]{1,0:T(8,128)(2,1)S(1)}, u32[]{:S(2)}, u32[]{:S(2)}) collective-permute-start(bf16[512,128]{1,0:T(8,128)(2,1)S(1)} %added.5.rest_1_), channel_id=1, source_target_pairs={{0,3},{1,0},{2,1},{3,2},{4,7},{5,4},{6,5},{7,6},{8,11},{9,8},{10,9... | collective-permute-start | bytes 393224 | tf_op jit(solution)/shard_map/ppermute | solution.py:38
  49.2 1.5 %collective-permute-start.20 = (bf16[512,128]{1,0:T(8,128)(2,1)S(1)}, bf16[512,128]{1,0:T(8,128)(2,1)S(1)}, u32[]{:S(2)}, u32[]{:S(2)}) collective-permute-start(bf16[512,128]{1,0:T(8,128)(2,1)S(1)} %added.5.rest_1_), channel_id=1, source_target_pairs={{0,2},{1,3},{2,0},{3,1},{4,6},{5,7},{6,4},{7,5},{8,10},{9,11},{10,... | collective-permute-start | bytes 393224 | tf_op jit(solution)/shard_map/ppermute | solution.py:38
  50.7 0.7 %collective-permute-done.8.refs_3_ = bf16[512,128]{1,0:T(8,128)(2,1)S(1)} collective-permute-done((bf16[512,128]{1,0:T(8,128)(2,1)S(1)}, bf16[512,128]{1,0:T(8,128)(2,1)S(1)}, u32[]{:S(2)}, u32[]{:S(2)}) %collective-permute-start.8) | collective-permute-done | bytes 131104 | tf_op jit(solution)/shard_map/ppermute | solution.py:38
  51.4 1.2 %collective-permute-done.9.refs_4_ = bf16[512,128]{1,0:T(8,128)(2,1)S(1)} collective-permute-done((bf16[512,128]{1,0:T(8,128)(2,1)S(1)}, bf16[512,128]{1,0:T(8,128)(2,1)S(1)}, u32[]{:S(2)}, u32[]{:S(2)}) %collective-permute-start.9) | collective-permute-done | bytes 131104 | tf_op jit(solution)/shard_map/ppermute | solution.py:38
  52.6 0.1 added.4.rest_0_
  52.7 0.9 %collective-permute-start.10 = (bf16[512,128]{1,0:T(8,128)(2,1)S(1)}, bf16[512,128]{1,0:T(8,128)(2,1)S(1)}, u32[]{:S(2)}, u32[]{:S(2)}) collective-permute-start(bf16[512,128]{1,0:T(8,128)(2,1)S(1)} %added.4.rest_0_), channel_id=1, source_target_pairs={{0,1},{1,2},{2,3},{3,0},{4,5},{5,6},{6,7},{7,4},{8,9},{9,10},{10,1... | collective-permute-start | bytes 393224 | tf_op jit(solution)/shard_map/ppermute | solution.py:38
  53.6 2.4 %collective-permute-start.17 = (bf16[512,128]{1,0:T(8,128)(2,1)S(1)}, bf16[512,128]{1,0:T(8,128)(2,1)S(1)}, u32[]{:S(2)}, u32[]{:S(2)}) collective-permute-start(bf16[512,128]{1,0:T(8,128)(2,1)S(1)} %added.4.rest_0_), channel_id=1, source_target_pairs={{0,3},{1,0},{2,1},{3,2},{4,7},{5,4},{6,5},{7,6},{8,11},{9,8},{10,9... | collective-permute-start | bytes 393224 | tf_op jit(solution)/shard_map/ppermute | solution.py:38
  56.0 1.2 %collective-permute-done.16.rest_1_ = bf16[512,128]{1,0:T(8,128)(2,1)S(1)} collective-permute-done((bf16[512,128]{1,0:T(8,128)(2,1)S(1)}, bf16[512,128]{1,0:T(8,128)(2,1)S(1)}, u32[]{:S(2)}, u32[]{:S(2)}) %collective-permute-start.16) | collective-permute-done | bytes 131104 | tf_op jit(solution)/shard_map/ppermute | solution.py:38
  57.2 3.4 %project.2.rest_6_ = f32[4,512,256]{2,1,0:T(8,128)} custom-call(f32[4,512,256]{2,1,0:T(8,128)S(1)} %copy-done.2, bf16[512,128]{1,0:T(8,128)(2,1)S(1)} %added.4.rest_0_, bf16[512,128]{1,0:T(8,128)(2,1)S(1)} %added.5.rest_1_), custom_call_target="tpu_custom_call" | custom-call | flops 2000000000 | bytes 2000000 | tf_op jit(solution)/shard_map/project/pallas_call | solution.py:180
  60.6 0.0 collective-permute-done.18.rest_3_
  60.6 0.0 collective-permute-done.10.rest_0_
  60.7 0.0 collective-permute-done.17.rest_2_
  60.7 3.0 %collective-permute-done.19.rest_4_ = bf16[512,128]{1,0:T(8,128)(2,1)S(1)} collective-permute-done((bf16[512,128]{1,0:T(8,128)(2,1)S(1)}, bf16[512,128]{1,0:T(8,128)(2,1)S(1)}, u32[]{:S(2)}, u32[]{:S(2)}) %collective-permute-start.19) | collective-permute-done | bytes 131104 | tf_op jit(solution)/shard_map/ppermute | solution.py:38
  63.7 4.2 %project.3 = f32[4,512,256]{2,1,0:T(8,128)} custom-call(f32[4,512,256]{2,1,0:T(8,128)S(1)} %copy-done.2, bf16[512,128]{1,0:T(8,128)(2,1)S(1)} %collective-permute-done.10.rest_0_, bf16[512,128]{1,0:T(8,128)(2,1)S(1)} %collective-permute-done.16.rest_1_, bf16[512,128]{1,0:T(8,128)(2,1)S(1)} %collective-permute-done.17.rest_2_, ...), custom_call_target="tpu_custom_call", output_to_operand_aliasing={{}: (7, {})} | custom-call | flops 6000000000 | bytes 6000000 | tf_op jit(solution)/shard_map/project/pallas_call | solution.py:180
  (11 shorter events, 0.0 us)
Async XLA Ops:
  0.0 1.6 %copy-start.1 = (f32[4,512,256]{2,1,0:T(8,128)S(1)}, f32[4,512,256]{2,1,0:T(8,128)}, u32[]{:S(2)}) copy-start(f32[4,512,256]{2,1,0:T(8,128)} %factors.3) | copy-start | bytes 6291460
  1.6 1.6 %copy-start = (bf16[4,512,512]{2,1,0:T(8,128)(2,1)S(1)}, bf16[4,512,512]{2,1,0:T(8,128)(2,1)}, u32[]{:S(2)}) copy-start(bf16[4,512,512]{2,1,0:T(8,128)(2,1)} %affinity.5) | copy-start | bytes 6291460
  1.6 1.6 %copy-start.3 = (s32[4,2]{0,1:T(2,128)S(1)}, s32[4,2]{0,1:T(2,128)}, u32[]{:S(2)}) copy-start(s32[4,2]{0,1:T(2,128)} %param.4) | copy-start | bytes 100
  5.0 25.9 %collective-permute-start.2 = (bf16[4,512,256]{2,1,0:T(8,128)(2,1)S(1)}, bf16[4,512,256]{2,1,0:T(8,128)(2,1)S(1)}, u32[]{:S(2)}, u32[]{:S(2)}) collective-permute-start(bf16[4,512,256]{2,1,0:T(8,128)(2,1)S(1)} %get-tuple-element.25), channel_id=1, source_target_pairs={{0,4},{4,0},{8,12},{12,8},{16,20},{20,16},{24,28},{28,24},{32,36},... | collective-permute-start | bytes 3145736 | tf_op jit(solution)/shard_map/ppermute | solution.py:27
  5.1 10.0 %collective-permute-start.3 = (bf16[512,256]{1,0:T(8,128)(2,1)S(1)}, bf16[512,256]{1,0:T(8,128)(2,1)S(1)}, u32[]{:S(2)}, u32[]{:S(2)}) collective-permute-start(bf16[512,256]{1,0:T(8,128)(2,1)S(1)} %get-tuple-element.28), channel_id=1, source_target_pairs={{0,1},{1,2},{2,3},{3,0},{4,5},{5,6},{6,7},{7,4},{8,9},{9,10},{10,1... | collective-permute-start | bytes 786440 | tf_op jit(solution)/shard_map/ppermute | solution.py:38
  6.8 15.1 %collective-permute-start.4 = (bf16[512,256]{1,0:T(8,128)(2,1)S(1)}, bf16[512,256]{1,0:T(8,128)(2,1)S(1)}, u32[]{:S(2)}, u32[]{:S(2)}) collective-permute-start(bf16[512,256]{1,0:T(8,128)(2,1)S(1)} %get-tuple-element.29), channel_id=1, source_target_pairs={{0,2},{1,3},{2,0},{3,1},{4,6},{5,7},{6,4},{7,5},{8,10},{9,11},{10,... | collective-permute-start | bytes 786440 | tf_op jit(solution)/shard_map/ppermute | solution.py:38
  9.7 12.2 %collective-permute-start.5 = (bf16[512,256]{1,0:T(8,128)(2,1)S(1)}, bf16[512,256]{1,0:T(8,128)(2,1)S(1)}, u32[]{:S(2)}, u32[]{:S(2)}) collective-permute-start(bf16[512,256]{1,0:T(8,128)(2,1)S(1)} %get-tuple-element.30), channel_id=1, source_target_pairs={{0,3},{1,0},{2,1},{3,2},{4,7},{5,4},{6,5},{7,6},{8,11},{9,8},{10,9... | collective-permute-start | bytes 786440 | tf_op jit(solution)/shard_map/ppermute | solution.py:38
  11.0 15.3 %collective-permute-start.11 = (bf16[4,512,128]{2,1,0:T(8,128)(2,1)S(1)}, bf16[4,512,128]{2,1,0:T(8,128)(2,1)S(1)}, u32[]{:S(2)}, u32[]{:S(2)}) collective-permute-start(bf16[4,512,128]{2,1,0:T(8,128)(2,1)S(1)} %get-tuple-element.23.right.rounded), channel_id=1, source_target_pairs={{0,4},{4,0},{8,12},{12,8},{16,20},{20,16},{24,28},{28,24},{32,36},... | collective-permute-start | bytes 1572872 | tf_op jit(solution)/shard_map/ppermute | solution.py:27
  15.1 15.8 %collective-permute-start.12 = (bf16[4,512,128]{2,1,0:T(8,128)(2,1)S(1)}, bf16[4,512,128]{2,1,0:T(8,128)(2,1)S(1)}, u32[]{:S(2)}, u32[]{:S(2)}) collective-permute-start(bf16[4,512,128]{2,1,0:T(8,128)(2,1)S(1)} %get-tuple-element.23.right.rounded), channel_id=1, source_target_pairs={{4,8},{12,16},{20,24},{28,32},{36,40},{44,48},{52,56},{60,64},{68,... | collective-permute-start | bytes 1572872 | tf_op jit(solution)/shard_map/ppermute | solution.py:33
  21.9 13.8 %collective-permute-start = (bf16[4,512,128]{2,1,0:T(8,128)(2,1)S(1)}, bf16[4,512,128]{2,1,0:T(8,128)(2,1)S(1)}, u32[]{:S(2)}, u32[]{:S(2)}) collective-permute-start(bf16[4,512,128]{2,1,0:T(8,128)(2,1)S(1)} %get-tuple-element.22.left.rounded), channel_id=1, source_target_pairs={{0,4},{4,0},{8,12},{12,8},{16,20},{20,16},{24,28},{28,24},{32,36},... | collective-permute-start | bytes 1572872 | tf_op jit(solution)/shard_map/ppermute | solution.py:27
  21.9 18.1 %collective-permute-start.1 = (bf16[4,512,128]{2,1,0:T(8,128)(2,1)S(1)}, bf16[4,512,128]{2,1,0:T(8,128)(2,1)S(1)}, u32[]{:S(2)}, u32[]{:S(2)}) collective-permute-start(bf16[4,512,128]{2,1,0:T(8,128)(2,1)S(1)} %get-tuple-element.22.left.rounded), channel_id=1, source_target_pairs={{4,8},{12,16},{20,24},{28,32},{36,40},{44,48},{52,56},{60,64},{68,... | collective-permute-start | bytes 1572872 | tf_op jit(solution)/shard_map/ppermute | solution.py:33
  26.4 15.1 %collective-permute-start.6 = (bf16[512,256]{1,0:T(8,128)(2,1)S(1)}, bf16[512,256]{1,0:T(8,128)(2,1)S(1)}, u32[]{:S(2)}, u32[]{:S(2)}) collective-permute-start(bf16[512,256]{1,0:T(8,128)(2,1)S(1)} %added.3), channel_id=1, source_target_pairs={{4,8},{12,16},{20,24},{28,32},{36,40},{44,48},{52,56},{60,64},{68,... | collective-permute-start | bytes 786440 | tf_op jit(solution)/shard_map/ppermute | solution.py:33
  32.4 12.3 %collective-permute-start.13 = (bf16[512,128]{1,0:T(8,128)(2,1)S(1)}, bf16[512,128]{1,0:T(8,128)(2,1)S(1)}, u32[]{:S(2)}, u32[]{:S(2)}) collective-permute-start(bf16[512,128]{1,0:T(8,128)(2,1)S(1)} %get-tuple-element.36), channel_id=1, source_target_pairs={{0,1},{1,2},{2,3},{3,0},{4,5},{5,6},{6,7},{7,4},{8,9},{9,10},{10,1... | collective-permute-start | bytes 393224 | tf_op jit(solution)/shard_map/ppermute | solution.py:38
  33.6 12.0 %collective-permute-start.14 = (bf16[512,128]{1,0:T(8,128)(2,1)S(1)}, bf16[512,128]{1,0:T(8,128)(2,1)S(1)}, u32[]{:S(2)}, u32[]{:S(2)}) collective-permute-start(bf16[512,128]{1,0:T(8,128)(2,1)S(1)} %get-tuple-element.37), channel_id=1, source_target_pairs={{0,3},{1,0},{2,1},{3,2},{4,7},{5,4},{6,5},{7,6},{8,11},{9,8},{10,9... | collective-permute-start | bytes 393224 | tf_op jit(solution)/shard_map/ppermute | solution.py:38
  35.7 9.9 %collective-permute-start.15 = (bf16[512,128]{1,0:T(8,128)(2,1)S(1)}, bf16[512,128]{1,0:T(8,128)(2,1)S(1)}, u32[]{:S(2)}, u32[]{:S(2)}) collective-permute-start(bf16[512,128]{1,0:T(8,128)(2,1)S(1)} %get-tuple-element.38), channel_id=1, source_target_pairs={{0,2},{1,3},{2,0},{3,1},{4,6},{5,7},{6,4},{7,5},{8,10},{9,11},{10,... | collective-permute-start | bytes 393224 | tf_op jit(solution)/shard_map/ppermute | solution.py:38
  41.4 15.9 %copy-start.2 = (f32[4,512,256]{2,1,0:T(8,128)S(1)}, f32[4,512,256]{2,1,0:T(8,128)}, u32[]{:S(2)}) copy-start(f32[4,512,256]{2,1,0:T(8,128)} %factors.3) | copy-start | bytes 6291460
  41.4 7.8 %collective-permute-start.7 = (bf16[512,128]{1,0:T(8,128)(2,1)S(1)}, bf16[512,128]{1,0:T(8,128)(2,1)S(1)}, u32[]{:S(2)}, u32[]{:S(2)}) collective-permute-start(bf16[512,128]{1,0:T(8,128)(2,1)S(1)} %get-tuple-element.31), channel_id=1, source_target_pairs={{0,1},{1,2},{2,3},{3,0},{4,5},{5,6},{6,7},{7,4},{8,9},{9,10},{10,1... | collective-permute-start | bytes 393224 | tf_op jit(solution)/shard_map/ppermute | solution.py:38
  41.5 9.9 %collective-permute-start.8 = (bf16[512,128]{1,0:T(8,128)(2,1)S(1)}, bf16[512,128]{1,0:T(8,128)(2,1)S(1)}, u32[]{:S(2)}, u32[]{:S(2)}) collective-permute-start(bf16[512,128]{1,0:T(8,128)(2,1)S(1)} %get-tuple-element.32), channel_id=1, source_target_pairs={{0,3},{1,0},{2,1},{3,2},{4,7},{5,4},{6,5},{7,6},{8,11},{9,8},{10,9... | collective-permute-start | bytes 393224 | tf_op jit(solution)/shard_map/ppermute | solution.py:38
  44.7 7.9 %collective-permute-start.9 = (bf16[512,128]{1,0:T(8,128)(2,1)S(1)}, bf16[512,128]{1,0:T(8,128)(2,1)S(1)}, u32[]{:S(2)}, u32[]{:S(2)}) collective-permute-start(bf16[512,128]{1,0:T(8,128)(2,1)S(1)} %get-tuple-element.33), channel_id=1, source_target_pairs={{0,2},{1,3},{2,0},{3,1},{4,6},{5,7},{6,4},{7,5},{8,10},{9,11},{10,... | collective-permute-start | bytes 393224 | tf_op jit(solution)/shard_map/ppermute | solution.py:38
  45.7 11.5 %collective-permute-start.16 = (bf16[512,128]{1,0:T(8,128)(2,1)S(1)}, bf16[512,128]{1,0:T(8,128)(2,1)S(1)}, u32[]{:S(2)}, u32[]{:S(2)}) collective-permute-start(bf16[512,128]{1,0:T(8,128)(2,1)S(1)} %added.5.rest_1_), channel_id=1, source_target_pairs={{0,1},{1,2},{2,3},{3,0},{4,5},{5,6},{6,7},{7,4},{8,9},{9,10},{10,1... | collective-permute-start | bytes 393224 | tf_op jit(solution)/shard_map/ppermute | solution.py:38
  46.7 14.0 %collective-permute-start.18 = (bf16[512,128]{1,0:T(8,128)(2,1)S(1)}, bf16[512,128]{1,0:T(8,128)(2,1)S(1)}, u32[]{:S(2)}, u32[]{:S(2)}) collective-permute-start(bf16[512,128]{1,0:T(8,128)(2,1)S(1)} %added.5.rest_1_), channel_id=1, source_target_pairs={{0,3},{1,0},{2,1},{3,2},{4,7},{5,4},{6,5},{7,6},{8,11},{9,8},{10,9... | collective-permute-start | bytes 393224 | tf_op jit(solution)/shard_map/ppermute | solution.py:38
  49.2 11.5 %collective-permute-start.20 = (bf16[512,128]{1,0:T(8,128)(2,1)S(1)}, bf16[512,128]{1,0:T(8,128)(2,1)S(1)}, u32[]{:S(2)}, u32[]{:S(2)}) collective-permute-start(bf16[512,128]{1,0:T(8,128)(2,1)S(1)} %added.5.rest_1_), channel_id=1, source_target_pairs={{0,2},{1,3},{2,0},{3,1},{4,6},{5,7},{6,4},{7,5},{8,10},{9,11},{10,... | collective-permute-start | bytes 393224 | tf_op jit(solution)/shard_map/ppermute | solution.py:38
  52.7 8.0 %collective-permute-start.10 = (bf16[512,128]{1,0:T(8,128)(2,1)S(1)}, bf16[512,128]{1,0:T(8,128)(2,1)S(1)}, u32[]{:S(2)}, u32[]{:S(2)}) collective-permute-start(bf16[512,128]{1,0:T(8,128)(2,1)S(1)} %added.4.rest_0_), channel_id=1, source_target_pairs={{0,1},{1,2},{2,3},{3,0},{4,5},{5,6},{6,7},{7,4},{8,9},{9,10},{10,1... | collective-permute-start | bytes 393224 | tf_op jit(solution)/shard_map/ppermute | solution.py:38
  53.6 7.0 %collective-permute-start.17 = (bf16[512,128]{1,0:T(8,128)(2,1)S(1)}, bf16[512,128]{1,0:T(8,128)(2,1)S(1)}, u32[]{:S(2)}, u32[]{:S(2)}) collective-permute-start(bf16[512,128]{1,0:T(8,128)(2,1)S(1)} %added.4.rest_0_), channel_id=1, source_target_pairs={{0,3},{1,0},{2,1},{3,2},{4,7},{5,4},{6,5},{7,6},{8,11},{9,8},{10,9... | collective-permute-start | bytes 393224 | tf_op jit(solution)/shard_map/ppermute | solution.py:38
  57.2 6.5 %collective-permute-start.19 = (bf16[512,128]{1,0:T(8,128)(2,1)S(1)}, bf16[512,128]{1,0:T(8,128)(2,1)S(1)}, u32[]{:S(2)}, u32[]{:S(2)}) collective-permute-start(bf16[512,128]{1,0:T(8,128)(2,1)S(1)} %added.4.rest_0_), channel_id=1, source_target_pairs={{0,2},{1,3},{2,0},{3,1},{4,6},{5,7},{6,4},{7,5},{8,10},{9,11},{10,... | collective-permute-start | bytes 393224 | tf_op jit(solution)/shard_map/ppermute | solution.py:38

commit v5 on v4

--- a/solution.py
+++ b/solution.py
@@ -64,33 +64,24 @@
 NT = ((1,), (1,))
 
 
-def backward_kernel(pairs, affinity, left, right, own_left, own_right, to_mate, c0, c1, c2, c3, acc):
+def backward_kernel(pairs, affinity, left, right, sums, c0, c1, c2, c3, held, sem):
     tiles = affinity.shape[0]
-    images, _, half = left.shape
-    firsts, slots, turns = places(pairs, images)
+    images = left.shape[0]
+    copy = pltpu.make_async_copy(pairs, held, sem)
+    copy.start()
+    sums[...] = jnp.zeros_like(sums)
+    copy.wait()
+    firsts, slots, turns = places(held, images)
     for t in range(tiles):
-        fresh = slots[t] >= 0
-        for u in range(t):
-            fresh = jnp.logical_and(fresh, slots[u] != slots[t])
         first = jnp.concatenate([left[firsts[t]], right[firsts[t]]], axis=1)
-        term = dot(affinity[t], first, TN)
-        acc[slots[t]] = jnp.where(fresh, jnp.zeros_like(term), acc[slots[t]]) + term
-
-    def total(slot):
-        hit = slots[0] == slot
-        for t in range(1, tiles):
-            hit = jnp.logical_or(hit, slots[t] == slot)
-        value = acc[slot]
-        return jnp.where(hit, value, jnp.zeros_like(value))
-
+        sums[slots[t]] = sums[slots[t]] + dot(affinity[t], first, TN)
     for turn, ref in zip(turns, (c0, c1, c2, c3)):
-        ref[...] = total(turn).astype(ref.dtype)
-    for j in range(images):
-        to_mate[j] = total(2 * images + j).astype(to_mate.dtype)
-    for j in range(images):
-        value = total(images + j)
-        own_left[j] = value[:, :half]
-        own_right[j] = value[:, half:]
+        ref[...] = sums[turn].astype(ref.dtype)
+
+
+def narrow_kernel(first, sums, out):
+    for j in range(out.shape[0]):
+        out[j] = sums[first + j].astype(out.dtype)
 
 
 def forward_kernel(
@@ -100,7 +91,7 @@
     copy = pltpu.make_async_copy(pairs, held, sem)
     copy.start()
     for j in range(images):
-        acc[j] = own[j] + terms[j, :, start : start + half].astype(jnp.float32)
+        acc[j] = own[images + j, :, start : start + half] + terms[j, :, start : start + half].astype(jnp.float32)
     copy.wait()
     firsts, slots, turns = places(held, images)
     for t, (first, slot) in enumerate(zip(firsts, slots)):
@@ -212,22 +203,29 @@
     def shape(*dims, dtype=jnp.bfloat16):
         return jax.ShapeDtypeStruct(dims, dtype)
 
-    own_left, own_right, to_mate, c0, c1, c2, c3 = pl.pallas_call(
+    sums, c0, c1, c2, c3 = pl.pallas_call(
         backward_kernel,
         out_shape=(
-            shape(images, keypoints, half, dtype=jnp.float32),
-            shape(images, keypoints, half, dtype=jnp.float32),
-            shape(images, keypoints, universe),
+            shape(3 * images, keypoints, universe, dtype=jnp.float32),
             shape(keypoints, universe, dtype=jnp.float32),
         )
         + (shape(keypoints, universe),) * 3,
-        in_specs=[SMEM, VMEM, VMEM, VMEM],
-        out_specs=(VMEM,) * 7,
-        scratch_shapes=[pltpu.VMEM((3 * images, keypoints, universe), jnp.float32)],
-        compiler_params=pltpu.CompilerParams(vmem_limit_bytes=12 * MIB),
+        in_specs=[pl.BlockSpec(memory_space=pl.ANY), VMEM, VMEM, VMEM],
+        out_specs=(VMEM,) * 5,
+        scratch_shapes=[pltpu.SMEM(pairs.shape, jnp.int32), pltpu.SemaphoreType.DMA(())],
+        compiler_params=pltpu.CompilerParams(vmem_limit_bytes=8 * MIB),
         cost_estimate=pl.CostEstimate(flops=600000000, bytes_accessed=8000000, transcendentals=0),
         name="backward",
     )(pairs, affinity, left, right)
+    to_mate = pl.pallas_call(
+        functools.partial(narrow_kernel, 2 * images),
+        out_shape=shape(images, keypoints, universe),
+        in_specs=[VMEM],
+        out_specs=VMEM,
+        compiler_params=pltpu.CompilerParams(vmem_limit_bytes=4 * MIB),
+        cost_estimate=pl.CostEstimate(flops=1000000, bytes_accessed=3000000, transcendentals=0),
+        name="narrow",
+    )(sums)
     x1 = turned(c1, 1)
     x3 = turned(c3, -1)
     x2 = turned(c2, 2)
@@ -270,9 +268,9 @@
     def gathered(gradient):
         return [turned(gradient, 1), turned(gradient, -1), turned(gradient, 2)]
 
-    left_parts = forward(0, left, mate_left, across_left, own_left)
+    left_parts = forward(0, left, mate_left, across_left, sums)
     left_parts = scattered(left_parts)
-    right_parts = forward(half, right, mate_right, across_right, own_right)
+    right_parts = forward(half, right, mate_right, across_right, sums)
     right_parts = scattered(right_parts)
     left_sum = added(0, *left_parts[:1], crossed, *left_parts[1:])
     right_sum = added(half, *right_parts[:1], crossed, *right_parts[1:])

time: 68.3 us -> 68 us (level)
    pallas_call x1 -> x2, Pallas kernels: 1.83 us -> 1.61 us  [the longest x1 1.51 us: shards(): pl.pallas_call(backward_kernel, out_shape=(shape(3 * images, keypoints, u...]
where the time goes in v5:
time: 68 us; the launch traced here: 67.8 us
  starting transfers between devices  38.4 us (56%)
  waiting for transfers between devices  13.6 us (20%)
  Pallas kernels  12.3 us (18%)
  local copies, waits for them, and re-layouts  3.05 us (4%)
    ppermute x15, starting transfers between devices, turned(): return lax.ppermute(x, 'rep', [(i, (i + by) % n) for i in range(n)])  26 us
    ppermute x15, waiting for transfers between devices, turned(): return lax.ppermute(x, 'rep', [(i, (i + by) % n) for i in range(n)])  13.6 us
    ppermute x3, starting transfers between devices, across(): return lax.ppermute(x, 'tiles', pairs + [(b, a) for a, b in pairs])  12.3 us
    pallas_call x2, Pallas kernels, project(): pl.pallas_call(functools.partial(project_kernel, ahead), out_shape=jax.Sh...  7.58 us
    unnamed x8, local copies, waits for them, and re-layouts  3.05 us
    pallas_call x2, Pallas kernels, forward(): pl.pallas_call(functools.partial(forward_kernel, start), out_shape=(shape...  2.7 us
    pallas_call x1, Pallas kernels, shards(): pl.pallas_call(backward_kernel, out_shape=(shape(3 * images, keypoints, u...  1.51 us
  transfers between devices with their start and end apart: 21, of which 6 were waited for; matrix products, arithmetic and copies ran while one was open for 0% of the time, Pallas kernels for 9%

profile of v5, /device:TPU:128, one launch (start us, length us, event | category | flops | bytes accessed | tf_op | source)
XLA Modules:
  0.0 67.8 jit_solution(12334161890182932136)
XLA Ops:
  0.0 1.6 %copy-done.1 = f32[4,512,256]{2,1,0:T(8,128)S(1)} copy-done((f32[4,512,256]{2,1,0:T(8,128)S(1)}, f32[4,512,256]{2,1,0:T(8,128)}, u32[]{:S(2)}) %copy-start.1) | copy-done | bytes 2097176
  1.6 0.1 rounded.1
  1.7 1.5 %copy-done = bf16[4,512,512]{2,1,0:T(8,128)(2,1)S(1)} copy-done((bf16[4,512,512]{2,1,0:T(8,128)(2,1)S(1)}, bf16[4,512,512]{2,1,0:T(8,128)(2,1)}, u32[]{:S(2)}) %copy-start) | copy-done | bytes 2097176
  3.2 1.5 %backward.1 = (f32[12,512,256]{2,1,0:T(8,128)S(1)}, f32[512,256]{1,0:T(8,128)S(1)}, bf16[512,256]{1,0:T(8,128)(2,1)S(1)}, bf16[512,256]{1,0:T(8,128)(2,1)S(1)}, bf16[512,256]{1,0:T(8,128)(2,1)S(1)}) custom-call(s32[2,4]{1,0:T(2,128)S(1)} %bitcast.1, bf16[4,512,512]{2,1,0:T(8,128)(2,1)S(1)} %copy-done, ...), custom_call_target="tpu_custom_call" | custom-call | flops 600000000 | bytes 8000000 | tf_op jit(solution)/shard_map/backward/pallas_call | solution.py:206
  4.7 0.1 narrow.1
  4.8 0.1 collective-permute-start.2
  4.9 1.7 %collective-permute-start.3 = (bf16[512,256]{1,0:T(8,128)(2,1)S(1)}, bf16[512,256]{1,0:T(8,128)(2,1)S(1)}, u32[]{:S(2)}, u32[]{:S(2)}) collective-permute-start(bf16[512,256]{1,0:T(8,128)(2,1)S(1)} %get-tuple-element.25), channel_id=1, source_target_pairs={{0,1},{1,2},{2,3},{3,0},{4,5},{5,6},{6,7},{7,4},{8,9},{9,10},{10,1... | collective-permute-start | bytes 786440 | tf_op jit(solution)/shard_map/ppermute | solution.py:38
  6.6 2.9 %collective-permute-start.4 = (bf16[512,256]{1,0:T(8,128)(2,1)S(1)}, bf16[512,256]{1,0:T(8,128)(2,1)S(1)}, u32[]{:S(2)}, u32[]{:S(2)}) collective-permute-start(bf16[512,256]{1,0:T(8,128)(2,1)S(1)} %get-tuple-element.26), channel_id=1, source_target_pairs={{0,2},{1,3},{2,0},{3,1},{4,6},{5,7},{6,4},{7,5},{8,10},{9,11},{10,... | collective-permute-start | bytes 786440 | tf_op jit(solution)/shard_map/ppermute | solution.py:38
  9.5 1.3 %collective-permute-start.5 = (bf16[512,256]{1,0:T(8,128)(2,1)S(1)}, bf16[512,256]{1,0:T(8,128)(2,1)S(1)}, u32[]{:S(2)}, u32[]{:S(2)}) collective-permute-start(bf16[512,256]{1,0:T(8,128)(2,1)S(1)} %get-tuple-element.27), channel_id=1, source_target_pairs={{0,3},{1,0},{2,1},{3,2},{4,7},{5,4},{6,5},{7,6},{8,11},{9,8},{10,9... | collective-permute-start | bytes 786440 | tf_op jit(solution)/shard_map/ppermute | solution.py:38
  10.8 0.0 collective-permute-start.11
  10.8 4.1 %collective-permute-done.3.refs_1_ = bf16[512,256]{1,0:T(8,128)(2,1)S(1)} collective-permute-done((bf16[512,256]{1,0:T(8,128)(2,1)S(1)}, bf16[512,256]{1,0:T(8,128)(2,1)S(1)}, u32[]{:S(2)}, u32[]{:S(2)}) %collective-permute-start.3) | collective-permute-done | bytes 262176 | tf_op jit(solution)/shard_map/ppermute | solution.py:38
  14.9 3.4 %collective-permute-start.12 = (bf16[4,512,128]{2,1,0:T(8,128)(2,1)S(1)}, bf16[4,512,128]{2,1,0:T(8,128)(2,1)S(1)}, u32[]{:S(2)}, u32[]{:S(2)}) collective-permute-start(bf16[4,512,128]{2,1,0:T(8,128)(2,1)S(1)} %get-tuple-element.21.right.rounded), channel_id=1, source_target_pairs={{4,8},{12,16},{20,24},{28,32},{36,40},{44,48},{52,56},{60,64},{68,... | collective-permute-start | bytes 1572872 | tf_op jit(solution)/shard_map/ppermute | solution.py:33
  18.3 3.4 %collective-permute-done.4.refs_2_ = bf16[512,256]{1,0:T(8,128)(2,1)S(1)} collective-permute-done((bf16[512,256]{1,0:T(8,128)(2,1)S(1)}, bf16[512,256]{1,0:T(8,128)(2,1)S(1)}, u32[]{:S(2)}, u32[]{:S(2)}) %collective-permute-start.4) | collective-permute-done | bytes 262176 | tf_op jit(solution)/shard_map/ppermute | solution.py:38
  21.7 0.0 collective-permute-start
  21.7 0.0 collective-permute-done.5.refs_3_
  21.7 4.3 %collective-permute-start.1 = (bf16[4,512,128]{2,1,0:T(8,128)(2,1)S(1)}, bf16[4,512,128]{2,1,0:T(8,128)(2,1)S(1)}, u32[]{:S(2)}, u32[]{:S(2)}) collective-permute-start(bf16[4,512,128]{2,1,0:T(8,128)(2,1)S(1)} %get-tuple-element.20.left.rounded), channel_id=1, source_target_pairs={{4,8},{12,16},{20,24},{28,32},{36,40},{44,48},{52,56},{60,64},{68,... | collective-permute-start | bytes 1572872 | tf_op jit(solution)/shard_map/ppermute | solution.py:33
  26.0 0.1 added.3
  26.1 0.0 collective-permute-done.11.from_mate
  26.2 4.6 %collective-permute-start.6 = (bf16[512,256]{1,0:T(8,128)(2,1)S(1)}, bf16[512,256]{1,0:T(8,128)(2,1)S(1)}, u32[]{:S(2)}, u32[]{:S(2)}) collective-permute-start(bf16[512,256]{1,0:T(8,128)(2,1)S(1)} %added.3), channel_id=1, source_target_pairs={{4,8},{12,16},{20,24},{28,32},{36,40},{44,48},{52,56},{60,64},{68,... | collective-permute-start | bytes 786440 | tf_op jit(solution)/shard_map/ppermute | solution.py:33
  30.7 0.0 collective-permute-done.12.from_across
  30.7 1.4 %forward.3 = (f32[512,128]{1,0:T(8,128)S(1)}, bf16[512,128]{1,0:T(8,128)(2,1)S(1)}, bf16[512,128]{1,0:T(8,128)(2,1)S(1)}, bf16[512,128]{1,0:T(8,128)(2,1)S(1)}) custom-call(s32[2,4]{1,0:T(2,128)S(1)} %bitcast.2, bf16[4,512,512]{2,1,0:T(8,128)(2,1)S(1)} %copy-done, bf16[4,512,128]{2,1,0:T(8,128)(2,1)S(1)} %get-tuple-element.21.right.rounded, ...), custom_call_target="tpu_custom_call" | custom-call | flops 600000000 | bytes 4000000 | tf_op jit(solution)/shard_map/forward/pallas_call | solution.py:250
  32.1 1.2 %collective-permute-start.13 = (bf16[512,128]{1,0:T(8,128)(2,1)S(1)}, bf16[512,128]{1,0:T(8,128)(2,1)S(1)}, u32[]{:S(2)}, u32[]{:S(2)}) collective-permute-start(bf16[512,128]{1,0:T(8,128)(2,1)S(1)} %get-tuple-element.32), channel_id=1, source_target_pairs={{0,1},{1,2},{2,3},{3,0},{4,5},{5,6},{6,7},{7,4},{8,9},{9,10},{10,1... | collective-permute-start | bytes 393224 | tf_op jit(solution)/shard_map/ppermute | solution.py:38
  33.3 2.1 %collective-permute-start.14 = (bf16[512,128]{1,0:T(8,128)(2,1)S(1)}, bf16[512,128]{1,0:T(8,128)(2,1)S(1)}, u32[]{:S(2)}, u32[]{:S(2)}) collective-permute-start(bf16[512,128]{1,0:T(8,128)(2,1)S(1)} %get-tuple-element.33), channel_id=1, source_target_pairs={{0,3},{1,0},{2,1},{3,2},{4,7},{5,4},{6,5},{7,6},{8,11},{9,8},{10,9... | collective-permute-start | bytes 393224 | tf_op jit(solution)/shard_map/ppermute | solution.py:38
  35.4 0.0 collective-permute-done.from_mate
  35.4 4.3 %collective-permute-start.15 = (bf16[512,128]{1,0:T(8,128)(2,1)S(1)}, bf16[512,128]{1,0:T(8,128)(2,1)S(1)}, u32[]{:S(2)}, u32[]{:S(2)}) collective-permute-start(bf16[512,128]{1,0:T(8,128)(2,1)S(1)} %get-tuple-element.34), channel_id=1, source_target_pairs={{0,2},{1,3},{2,0},{3,1},{4,6},{5,7},{6,4},{7,5},{8,10},{9,11},{10,... | collective-permute-start | bytes 393224 | tf_op jit(solution)/shard_map/ppermute | solution.py:38
  39.7 0.0 collective-permute-done.1.from_across
  39.7 1.4 %forward.2 = (f32[512,128]{1,0:T(8,128)S(1)}, bf16[512,128]{1,0:T(8,128)(2,1)S(1)}, bf16[512,128]{1,0:T(8,128)(2,1)S(1)}, bf16[512,128]{1,0:T(8,128)(2,1)S(1)}) custom-call(s32[2,4]{1,0:T(2,128)S(1)} %bitcast.3, bf16[4,512,512]{2,1,0:T(8,128)(2,1)S(1)} %copy-done, bf16[4,512,128]{2,1,0:T(8,128)(2,1)S(1)} %get-tuple-element.20.left.rounded, ...), custom_call_target="tpu_custom_call" | custom-call | flops 600000000 | bytes 4000000 | tf_op jit(solution)/shard_map/forward/pallas_call | solution.py:250
  41.1 0.0 copy-start.2
  41.1 0.1 collective-permute-start.7
  41.2 0.0 collective-permute-done.6.refs_1_
  41.2 3.2 %collective-permute-start.8 = (bf16[512,128]{1,0:T(8,128)(2,1)S(1)}, bf16[512,128]{1,0:T(8,128)(2,1)S(1)}, u32[]{:S(2)}, u32[]{:S(2)}) collective-permute-start(bf16[512,128]{1,0:T(8,128)(2,1)S(1)} %get-tuple-element.29), channel_id=1, source_target_pairs={{0,3},{1,0},{2,1},{3,2},{4,7},{5,4},{6,5},{7,6},{8,11},{9,8},{10,9... | collective-permute-start | bytes 393224 | tf_op jit(solution)/shard_map/ppermute | solution.py:38
  44.4 0.9 %collective-permute-start.9 = (bf16[512,128]{1,0:T(8,128)(2,1)S(1)}, bf16[512,128]{1,0:T(8,128)(2,1)S(1)}, u32[]{:S(2)}, u32[]{:S(2)}) collective-permute-start(bf16[512,128]{1,0:T(8,128)(2,1)S(1)} %get-tuple-element.30), channel_id=1, source_target_pairs={{0,2},{1,3},{2,0},{3,1},{4,6},{5,7},{6,4},{7,5},{8,10},{9,11},{10,... | collective-permute-start | bytes 393224 | tf_op jit(solution)/shard_map/ppermute | solution.py:38
  45.3 0.0 collective-permute-done.14.refs_3_
  45.3 0.1 added.5.rest_1_
  45.4 1.0 %collective-permute-start.16 = (bf16[512,128]{1,0:T(8,128)(2,1)S(1)}, bf16[512,128]{1,0:T(8,128)(2,1)S(1)}, u32[]{:S(2)}, u32[]{:S(2)}) collective-permute-start(bf16[512,128]{1,0:T(8,128)(2,1)S(1)} %added.5.rest_1_), channel_id=1, source_target_pairs={{0,1},{1,2},{2,3},{3,0},{4,5},{5,6},{6,7},{7,4},{8,9},{9,10},{10,1... | collective-permute-start | bytes 393224 | tf_op jit(solution)/shard_map/ppermute | solution.py:38
  46.4 2.5 %collective-permute-start.18 = (bf16[512,128]{1,0:T(8,128)(2,1)S(1)}, bf16[512,128]{1,0:T(8,128)(2,1)S(1)}, u32[]{:S(2)}, u32[]{:S(2)}) collective-permute-start(bf16[512,128]{1,0:T(8,128)(2,1)S(1)} %added.5.rest_1_), channel_id=1, source_target_pairs={{0,3},{1,0},{2,1},{3,2},{4,7},{5,4},{6,5},{7,6},{8,11},{9,8},{10,9... | collective-permute-start | bytes 393224 | tf_op jit(solution)/shard_map/ppermute | solution.py:38
  48.9 1.5 %collective-permute-start.20 = (bf16[512,128]{1,0:T(8,128)(2,1)S(1)}, bf16[512,128]{1,0:T(8,128)(2,1)S(1)}, u32[]{:S(2)}, u32[]{:S(2)}) collective-permute-start(bf16[512,128]{1,0:T(8,128)(2,1)S(1)} %added.5.rest_1_), channel_id=1, source_target_pairs={{0,2},{1,3},{2,0},{3,1},{4,6},{5,7},{6,4},{7,5},{8,10},{9,11},{10,... | collective-permute-start | bytes 393224 | tf_op jit(solution)/shard_map/ppermute | solution.py:38
  50.4 0.6 collective-permute-done.8.refs_3_
  51.0 1.3 %collective-permute-done.9.refs_4_ = bf16[512,128]{1,0:T(8,128)(2,1)S(1)} collective-permute-done((bf16[512,128]{1,0:T(8,128)(2,1)S(1)}, bf16[512,128]{1,0:T(8,128)(2,1)S(1)}, u32[]{:S(2)}, u32[]{:S(2)}) %collective-permute-start.9) | collective-permute-done | bytes 131104 | tf_op jit(solution)/shard_map/ppermute | solution.py:38
  52.3 0.1 added.4.rest_0_
  52.4 1.0 %collective-permute-start.10 = (bf16[512,128]{1,0:T(8,128)(2,1)S(1)}, bf16[512,128]{1,0:T(8,128)(2,1)S(1)}, u32[]{:S(2)}, u32[]{:S(2)}) collective-permute-start(bf16[512,128]{1,0:T(8,128)(2,1)S(1)} %added.4.rest_0_), channel_id=1, source_target_pairs={{0,1},{1,2},{2,3},{3,0},{4,5},{5,6},{6,7},{7,4},{8,9},{9,10},{10,1... | collective-permute-start | bytes 393224 | tf_op jit(solution)/shard_map/ppermute | solution.py:38
  53.4 2.3 %collective-permute-start.17 = (bf16[512,128]{1,0:T(8,128)(2,1)S(1)}, bf16[512,128]{1,0:T(8,128)(2,1)S(1)}, u32[]{:S(2)}, u32[]{:S(2)}) collective-permute-start(bf16[512,128]{1,0:T(8,128)(2,1)S(1)} %added.4.rest_0_), channel_id=1, source_target_pairs={{0,3},{1,0},{2,1},{3,2},{4,7},{5,4},{6,5},{7,6},{8,11},{9,8},{10,9... | collective-permute-start | bytes 393224 | tf_op jit(solution)/shard_map/ppermute | solution.py:38
  55.7 1.2 %collective-permute-done.16.rest_1_ = bf16[512,128]{1,0:T(8,128)(2,1)S(1)} collective-permute-done((bf16[512,128]{1,0:T(8,128)(2,1)S(1)}, bf16[512,128]{1,0:T(8,128)(2,1)S(1)}, u32[]{:S(2)}, u32[]{:S(2)}) %collective-permute-start.16) | collective-permute-done | bytes 131104 | tf_op jit(solution)/shard_map/ppermute | solution.py:38
  56.9 3.4 %project.2.rest_6_ = f32[4,512,256]{2,1,0:T(8,128)} custom-call(f32[4,512,256]{2,1,0:T(8,128)S(1)} %copy-done.2, bf16[512,128]{1,0:T(8,128)(2,1)S(1)} %added.4.rest_0_, bf16[512,128]{1,0:T(8,128)(2,1)S(1)} %added.5.rest_1_), custom_call_target="tpu_custom_call" | custom-call | flops 2000000000 | bytes 2000000 | tf_op jit(solution)/shard_map/project/pallas_call | solution.py:171
  60.3 0.0 collective-permute-done.18.rest_3_
  60.3 0.0 collective-permute-done.10.rest_0_
  60.4 3.0 %collective-permute-done.19.rest_4_ = bf16[512,128]{1,0:T(8,128)(2,1)S(1)} collective-permute-done((bf16[512,128]{1,0:T(8,128)(2,1)S(1)}, bf16[512,128]{1,0:T(8,128)(2,1)S(1)}, u32[]{:S(2)}, u32[]{:S(2)}) %collective-permute-start.19) | collective-permute-done | bytes 131104 | tf_op jit(solution)/shard_map/ppermute | solution.py:38
  63.4 4.2 %project.3 = f32[4,512,256]{2,1,0:T(8,128)} custom-call(f32[4,512,256]{2,1,0:T(8,128)S(1)} %copy-done.2, bf16[512,128]{1,0:T(8,128)(2,1)S(1)} %collective-permute-done.10.rest_0_, bf16[512,128]{1,0:T(8,128)(2,1)S(1)} %collective-permute-done.16.rest_1_, bf16[512,128]{1,0:T(8,128)(2,1)S(1)} %collective-permute-done.17.rest_2_, ...), custom_call_target="tpu_custom_call", output_to_operand_aliasing={{}: (7, {})} | custom-call | flops 6000000000 | bytes 6000000 | tf_op jit(solution)/shard_map/project/pallas_call | solution.py:171
  (12 shorter events, 0.0 us)
Async XLA Ops:
  0.0 1.6 %copy-start.1 = (f32[4,512,256]{2,1,0:T(8,128)S(1)}, f32[4,512,256]{2,1,0:T(8,128)}, u32[]{:S(2)}) copy-start(f32[4,512,256]{2,1,0:T(8,128)} %factors.3) | copy-start | bytes 6291460
  1.6 1.6 %copy-start = (bf16[4,512,512]{2,1,0:T(8,128)(2,1)S(1)}, bf16[4,512,512]{2,1,0:T(8,128)(2,1)}, u32[]{:S(2)}) copy-start(bf16[4,512,512]{2,1,0:T(8,128)(2,1)} %affinity.5) | copy-start | bytes 6291460
  1.6 1.6 %copy-start.3 = (s32[4,2]{0,1:T(2,128)S(1)}, s32[4,2]{0,1:T(2,128)}, u32[]{:S(2)}) copy-start(s32[4,2]{0,1:T(2,128)} %param.4) | copy-start | bytes 100
  4.8 25.9 %collective-permute-start.2 = (bf16[4,512,256]{2,1,0:T(8,128)(2,1)S(1)}, bf16[4,512,256]{2,1,0:T(8,128)(2,1)S(1)}, u32[]{:S(2)}, u32[]{:S(2)}) collective-permute-start(bf16[4,512,256]{2,1,0:T(8,128)(2,1)S(1)} %narrow.1), channel_id=1, source_target_pairs={{0,4},{4,0},{8,12},{12,8},{16,20},{20,16},{24,28},{28,24},{32,36},... | collective-permute-start | bytes 3145736 | tf_op jit(solution)/shard_map/ppermute | solution.py:27
  4.9 10.0 %collective-permute-start.3 = (bf16[512,256]{1,0:T(8,128)(2,1)S(1)}, bf16[512,256]{1,0:T(8,128)(2,1)S(1)}, u32[]{:S(2)}, u32[]{:S(2)}) collective-permute-start(bf16[512,256]{1,0:T(8,128)(2,1)S(1)} %get-tuple-element.25), channel_id=1, source_target_pairs={{0,1},{1,2},{2,3},{3,0},{4,5},{5,6},{6,7},{7,4},{8,9},{9,10},{10,1... | collective-permute-start | bytes 786440 | tf_op jit(solution)/shard_map/ppermute | solution.py:38
  6.6 15.1 %collective-permute-start.4 = (bf16[512,256]{1,0:T(8,128)(2,1)S(1)}, bf16[512,256]{1,0:T(8,128)(2,1)S(1)}, u32[]{:S(2)}, u32[]{:S(2)}) collective-permute-start(bf16[512,256]{1,0:T(8,128)(2,1)S(1)} %get-tuple-element.26), channel_id=1, source_target_pairs={{0,2},{1,3},{2,0},{3,1},{4,6},{5,7},{6,4},{7,5},{8,10},{9,11},{10,... | collective-permute-start | bytes 786440 | tf_op jit(solution)/shard_map/ppermute | solution.py:38
  9.5 12.2 %collective-permute-start.5 = (bf16[512,256]{1,0:T(8,128)(2,1)S(1)}, bf16[512,256]{1,0:T(8,128)(2,1)S(1)}, u32[]{:S(2)}, u32[]{:S(2)}) collective-permute-start(bf16[512,256]{1,0:T(8,128)(2,1)S(1)} %get-tuple-element.27), channel_id=1, source_target_pairs={{0,3},{1,0},{2,1},{3,2},{4,7},{5,4},{6,5},{7,6},{8,11},{9,8},{10,9... | collective-permute-start | bytes 786440 | tf_op jit(solution)/shard_map/ppermute | solution.py:38
  10.8 15.3 %collective-permute-start.11 = (bf16[4,512,128]{2,1,0:T(8,128)(2,1)S(1)}, bf16[4,512,128]{2,1,0:T(8,128)(2,1)S(1)}, u32[]{:S(2)}, u32[]{:S(2)}) collective-permute-start(bf16[4,512,128]{2,1,0:T(8,128)(2,1)S(1)} %get-tuple-element.21.right.rounded), channel_id=1, source_target_pairs={{0,4},{4,0},{8,12},{12,8},{16,20},{20,16},{24,28},{28,24},{32,36},... | collective-permute-start | bytes 1572872 | tf_op jit(solution)/shard_map/ppermute | solution.py:27
  14.9 15.8 %collective-permute-start.12 = (bf16[4,512,128]{2,1,0:T(8,128)(2,1)S(1)}, bf16[4,512,128]{2,1,0:T(8,128)(2,1)S(1)}, u32[]{:S(2)}, u32[]{:S(2)}) collective-permute-start(bf16[4,512,128]{2,1,0:T(8,128)(2,1)S(1)} %get-tuple-element.21.right.rounded), channel_id=1, source_target_pairs={{4,8},{12,16},{20,24},{28,32},{36,40},{44,48},{52,56},{60,64},{68,... | collective-permute-start | bytes 1572872 | tf_op jit(solution)/shard_map/ppermute | solution.py:33
  21.7 13.7 %collective-permute-start = (bf16[4,512,128]{2,1,0:T(8,128)(2,1)S(1)}, bf16[4,512,128]{2,1,0:T(8,128)(2,1)S(1)}, u32[]{:S(2)}, u32[]{:S(2)}) collective-permute-start(bf16[4,512,128]{2,1,0:T(8,128)(2,1)S(1)} %get-tuple-element.20.left.rounded), channel_id=1, source_target_pairs={{0,4},{4,0},{8,12},{12,8},{16,20},{20,16},{24,28},{28,24},{32,36},... | collective-permute-start | bytes 1572872 | tf_op jit(solution)/shard_map/ppermute | solution.py:27
  21.7 18.0 %collective-permute-start.1 = (bf16[4,512,128]{2,1,0:T(8,128)(2,1)S(1)}, bf16[4,512,128]{2,1,0:T(8,128)(2,1)S(1)}, u32[]{:S(2)}, u32[]{:S(2)}) collective-permute-start(bf16[4,512,128]{2,1,0:T(8,128)(2,1)S(1)} %get-tuple-element.20.left.rounded), channel_id=1, source_target_pairs={{4,8},{12,16},{20,24},{28,32},{36,40},{44,48},{52,56},{60,64},{68,... | collective-permute-start | bytes 1572872 | tf_op jit(solution)/shard_map/ppermute | solution.py:33
  26.2 15.0 %collective-permute-start.6 = (bf16[512,256]{1,0:T(8,128)(2,1)S(1)}, bf16[512,256]{1,0:T(8,128)(2,1)S(1)}, u32[]{:S(2)}, u32[]{:S(2)}) collective-permute-start(bf16[512,256]{1,0:T(8,128)(2,1)S(1)} %added.3), channel_id=1, source_target_pairs={{4,8},{12,16},{20,24},{28,32},{36,40},{44,48},{52,56},{60,64},{68,... | collective-permute-start | bytes 786440 | tf_op jit(solution)/shard_map/ppermute | solution.py:33
  32.1 12.3 %collective-permute-start.13 = (bf16[512,128]{1,0:T(8,128)(2,1)S(1)}, bf16[512,128]{1,0:T(8,128)(2,1)S(1)}, u32[]{:S(2)}, u32[]{:S(2)}) collective-permute-start(bf16[512,128]{1,0:T(8,128)(2,1)S(1)} %get-tuple-element.32), channel_id=1, source_target_pairs={{0,1},{1,2},{2,3},{3,0},{4,5},{5,6},{6,7},{7,4},{8,9},{9,10},{10,1... | collective-permute-start | bytes 393224 | tf_op jit(solution)/shard_map/ppermute | solution.py:38
  33.3 12.0 %collective-permute-start.14 = (bf16[512,128]{1,0:T(8,128)(2,1)S(1)}, bf16[512,128]{1,0:T(8,128)(2,1)S(1)}, u32[]{:S(2)}, u32[]{:S(2)}) collective-permute-start(bf16[512,128]{1,0:T(8,128)(2,1)S(1)} %get-tuple-element.33), channel_id=1, source_target_pairs={{0,3},{1,0},{2,1},{3,2},{4,7},{5,4},{6,5},{7,6},{8,11},{9,8},{10,9... | collective-permute-start | bytes 393224 | tf_op jit(solution)/shard_map/ppermute | solution.py:38
  35.4 9.9 %collective-permute-start.15 = (bf16[512,128]{1,0:T(8,128)(2,1)S(1)}, bf16[512,128]{1,0:T(8,128)(2,1)S(1)}, u32[]{:S(2)}, u32[]{:S(2)}) collective-permute-start(bf16[512,128]{1,0:T(8,128)(2,1)S(1)} %get-tuple-element.34), channel_id=1, source_target_pairs={{0,2},{1,3},{2,0},{3,1},{4,6},{5,7},{6,4},{7,5},{8,10},{9,11},{10,... | collective-permute-start | bytes 393224 | tf_op jit(solution)/shard_map/ppermute | solution.py:38
  41.1 15.9 %copy-start.2 = (f32[4,512,256]{2,1,0:T(8,128)S(1)}, f32[4,512,256]{2,1,0:T(8,128)}, u32[]{:S(2)}) copy-start(f32[4,512,256]{2,1,0:T(8,128)} %factors.3) | copy-start | bytes 6291460
  41.1 7.8 %collective-permute-start.7 = (bf16[512,128]{1,0:T(8,128)(2,1)S(1)}, bf16[512,128]{1,0:T(8,128)(2,1)S(1)}, u32[]{:S(2)}, u32[]{:S(2)}) collective-permute-start(bf16[512,128]{1,0:T(8,128)(2,1)S(1)} %get-tuple-element.28), channel_id=1, source_target_pairs={{0,1},{1,2},{2,3},{3,0},{4,5},{5,6},{6,7},{7,4},{8,9},{9,10},{10,1... | collective-permute-start | bytes 393224 | tf_op jit(solution)/shard_map/ppermute | solution.py:38
  41.2 9.8 %collective-permute-start.8 = (bf16[512,128]{1,0:T(8,128)(2,1)S(1)}, bf16[512,128]{1,0:T(8,128)(2,1)S(1)}, u32[]{:S(2)}, u32[]{:S(2)}) collective-permute-start(bf16[512,128]{1,0:T(8,128)(2,1)S(1)} %get-tuple-element.29), channel_id=1, source_target_pairs={{0,3},{1,0},{2,1},{3,2},{4,7},{5,4},{6,5},{7,6},{8,11},{9,8},{10,9... | collective-permute-start | bytes 393224 | tf_op jit(solution)/shard_map/ppermute | solution.py:38
  44.4 7.9 %collective-permute-start.9 = (bf16[512,128]{1,0:T(8,128)(2,1)S(1)}, bf16[512,128]{1,0:T(8,128)(2,1)S(1)}, u32[]{:S(2)}, u32[]{:S(2)}) collective-permute-start(bf16[512,128]{1,0:T(8,128)(2,1)S(1)} %get-tuple-element.30), channel_id=1, source_target_pairs={{0,2},{1,3},{2,0},{3,1},{4,6},{5,7},{6,4},{7,5},{8,10},{9,11},{10,... | collective-permute-start | bytes 393224 | tf_op jit(solution)/shard_map/ppermute | solution.py:38
  45.4 11.5 %collective-permute-start.16 = (bf16[512,128]{1,0:T(8,128)(2,1)S(1)}, bf16[512,128]{1,0:T(8,128)(2,1)S(1)}, u32[]{:S(2)}, u32[]{:S(2)}) collective-permute-start(bf16[512,128]{1,0:T(8,128)(2,1)S(1)} %added.5.rest_1_), channel_id=1, source_target_pairs={{0,1},{1,2},{2,3},{3,0},{4,5},{5,6},{6,7},{7,4},{8,9},{9,10},{10,1... | collective-permute-start | bytes 393224 | tf_op jit(solution)/shard_map/ppermute | solution.py:38
  46.4 13.9 %collective-permute-start.18 = (bf16[512,128]{1,0:T(8,128)(2,1)S(1)}, bf16[512,128]{1,0:T(8,128)(2,1)S(1)}, u32[]{:S(2)}, u32[]{:S(2)}) collective-permute-start(bf16[512,128]{1,0:T(8,128)(2,1)S(1)} %added.5.rest_1_), channel_id=1, source_target_pairs={{0,3},{1,0},{2,1},{3,2},{4,7},{5,4},{6,5},{7,6},{8,11},{9,8},{10,9... | collective-permute-start | bytes 393224 | tf_op jit(solution)/shard_map/ppermute | solution.py:38
  48.9 11.4 %collective-permute-start.20 = (bf16[512,128]{1,0:T(8,128)(2,1)S(1)}, bf16[512,128]{1,0:T(8,128)(2,1)S(1)}, u32[]{:S(2)}, u32[]{:S(2)}) collective-permute-start(bf16[512,128]{1,0:T(8,128)(2,1)S(1)} %added.5.rest_1_), channel_id=1, source_target_pairs={{0,2},{1,3},{2,0},{3,1},{4,6},{5,7},{6,4},{7,5},{8,10},{9,11},{10,... | collective-permute-start | bytes 393224 | tf_op jit(solution)/shard_map/ppermute | solution.py:38
  52.4 8.0 %collective-permute-start.10 = (bf16[512,128]{1,0:T(8,128)(2,1)S(1)}, bf16[512,128]{1,0:T(8,128)(2,1)S(1)}, u32[]{:S(2)}, u32[]{:S(2)}) collective-permute-start(bf16[512,128]{1,0:T(8,128)(2,1)S(1)} %added.4.rest_0_), channel_id=1, source_target_pairs={{0,1},{1,2},{2,3},{3,0},{4,5},{5,6},{6,7},{7,4},{8,9},{9,10},{10,1... | collective-permute-start | bytes 393224 | tf_op jit(solution)/shard_map/ppermute | solution.py:38
  53.4 7.0 %collective-permute-start.17 = (bf16[512,128]{1,0:T(8,128)(2,1)S(1)}, bf16[512,128]{1,0:T(8,128)(2,1)S(1)}, u32[]{:S(2)}, u32[]{:S(2)}) collective-permute-start(bf16[512,128]{1,0:T(8,128)(2,1)S(1)} %added.4.rest_0_), channel_id=1, source_target_pairs={{0,3},{1,0},{2,1},{3,2},{4,7},{5,4},{6,5},{7,6},{8,11},{9,8},{10,9... | collective-permute-start | bytes 393224 | tf_op jit(solution)/shard_map/ppermute | solution.py:38
  56.9 6.5 %collective-permute-start.19 = (bf16[512,128]{1,0:T(8,128)(2,1)S(1)}, bf16[512,128]{1,0:T(8,128)(2,1)S(1)}, u32[]{:S(2)}, u32[]{:S(2)}) collective-permute-start(bf16[512,128]{1,0:T(8,128)(2,1)S(1)} %added.4.rest_0_), channel_id=1, source_target_pairs={{0,2},{1,3},{2,0},{3,1},{4,6},{5,7},{6,4},{7,5},{8,10},{9,11},{10,... | collective-permute-start | bytes 393224 | tf_op jit(solution)/shard_map/ppermute | solution.py:38
